TPU v7x, 256 devices: a whole 4x4x8 slice. The times are simulated.
256 devices in a mesh: sa: 32 (over y, z), sb: 8 (over x, core).
Axes of the slice: x: 4, y: 4, z: 8, core: 2. Of those that a mesh axis runs over, the one named last changes fastest.
Arguments:
- queries: bfloat16 [131072, 4096], P(('sa', 'sb')), may hold values from -6 to 6
- keys: bfloat16 [131072, 4096], P(('sa', 'sb')), may hold values from -0.5390625 to 0.5390625
- values: bfloat16 [131072, 2048], P(('sa', 'sb')), may hold values from -6 to 6
- level_weights: bfloat16 [131072, 18, 32], P(('sa', 'sb')), may hold values from 0.25 to 4
- out_gain: bfloat16 [2048], replicated, may hold values from 0.25 to 1.75
Outputs:
- mixed: bfloat16 [131072, 2048], P(('sa', 'sb'))
All inputs are finite; a program needn't handle non-finite values.
Results may differ from a plain program's by a relative error of at most 0.008.
Values sent between devices are 32-bit elements; how exact they have to be, the bound alone decides.
No kernel may reach another device: no remote copies, remote signals or barrier semaphores. Data moves between devices by JAX's collectives and lax.ppermute only.
A program may use at most 192 MiB of HBM per device.

v0:
```python
import jax
import jax.numpy as jnp
from jax import lax
from jax.sharding import PartitionSpec as P

DK = 128
DV = 64
TOK_BITS = 9


epsilon = 1e-06


def swapped(value, axis, distance):
    mask = 2**distance
    pairs = [(source, source ^ mask) for source in range(lax.axis_size(axis))]
    return lax.ppermute(value, axis, pairs)


def from_behind(block, axis, distance):
    devices = range(lax.axis_size(axis))
    route = [(i - distance, i) for i in devices if i - distance in devices]
    return lax.ppermute(block, axis, route)


def block_levels(length):
    position = jnp.arange(length, dtype=jnp.int32)
    xored = jnp.bitwise_xor(position[:, None], position[None, :])
    level_index = jnp.zeros((length, length), jnp.int32)
    for level_bit in range(TOK_BITS):
        level_index = level_index + (xored >= 1 << level_bit).astype(jnp.int32)
    causal = position[:, None] >= position[None, :]
    return (level_index, causal)


def pair_weights(level_index, causal, weight_rows):
    table = jnp.transpose(weight_rows[:, : TOK_BITS + 1, :].astype(jnp.float32), (2, 0, 1))
    weight = jnp.zeros((table.shape[0], level_index.shape[0], level_index.shape[1]), jnp.float32)
    for level_number in range(TOK_BITS + 1):
        weight = jnp.where(
            level_index[None] == level_number, table[:, :, level_number][:, :, None], weight
        )
    return jnp.where(causal[None], weight, 0.0)


def on_device(queries, keys, values, level_weights, out_gain):
    length = queries.shape[0]
    head_count = out_gain.shape[0] // DV
    query_matrix_rows = queries.reshape(length, head_count, DK)
    key_matrix_rows = keys.reshape(length, head_count, DK)
    value_matrix_rows = values.reshape(length, head_count, DV)
    level_index, causal = block_levels(length)
    weight = pair_weights(level_index, causal, level_weights)
    scores = jnp.einsum(
        "thk,shk->hts", query_matrix_rows, key_matrix_rows, preferred_element_type=jnp.float32
    )
    weighted = (scores * weight).astype(jnp.bfloat16)
    summed = jnp.einsum(
        "hts,shv->thv", weighted, value_matrix_rows, preferred_element_type=jnp.float32
    )
    segment_block_state = jnp.einsum(
        "tdw,tdr->dwr", key_matrix_rows, value_matrix_rows, preferred_element_type=jnp.float32
    )
    inner_size = lax.axis_size("sb")
    inner_bits = inner_size.bit_length() - 1
    outer_bits = lax.axis_size("sa").bit_length() - 1
    inner_index = lax.axis_index("sb")
    outer_index = lax.axis_index("sa")
    block_index = outer_index * inner_size + inner_index
    level_states = []
    carried = segment_block_state
    for rank_bit in range(inner_bits):
        partner = swapped(carried, "sb", rank_bit)
        level_states.append(partner)
        carried = carried + partner
    for rank_bit in range(outer_bits - 1):
        partner = swapped(carried, "sa", rank_bit)
        level_states.append(partner)
        carried = carried + partner
    top_bit = outer_bits - 1
    level_states.append(from_behind(carried, "sa", 1 << top_bit))
    for rank_bit, fenwick_level_state in enumerate(level_states):
        active_flag = (block_index >> rank_bit & 1).astype(jnp.float32)
        upper_half_state = fenwick_level_state.astype(jnp.bfloat16)
        lower_half_state = (fenwick_level_state - upper_half_state.astype(jnp.float32)).astype(
            jnp.bfloat16
        )
        state_readout_output = jnp.einsum(
            "jeu,eud->jed", query_matrix_rows, upper_half_state, preferred_element_type=jnp.float32
        )
        state_readout_output = state_readout_output + jnp.einsum(
            "jeu,eud->jed", query_matrix_rows, lower_half_state, preferred_element_type=jnp.float32
        )
        factor = level_weights[:, TOK_BITS + 1 + rank_bit, :].astype(jnp.float32) * active_flag
        summed = summed + factor[:, :, None] * state_readout_output
    inverse_rms = lax.rsqrt(jnp.mean(summed * summed, axis=-1, keepdims=True) + epsilon)
    gain_rows = out_gain.reshape(head_count, DV).astype(jnp.float32)
    return (summed * inverse_rms * gain_rows).reshape(length, head_count * DV).astype(jnp.bfloat16)


def solution(mesh):
    return jax.shard_map(
        on_device,
        mesh=mesh,
        in_specs=(
            P(("sa", "sb"), None),
            P(("sa", "sb"), None),
            P(("sa", "sb"), None),
            P(("sa", "sb"), None, None),
            P(),
        ),
        out_specs=P(("sa", "sb"), None),
        check_vma=False,
    )
```

profile of v0, /device:TPU:1, one launch (start us, length us, event | category | flops | bytes accessed | tf_op | source)
XLA Modules:
  0.0 282.2 jit_solution(15097330018270014368)
XLA Ops:
  0.0 2.9 %copy.26 = bf16[512,2048]{0,1:T(8,128)(2,1)S(1)} copy(bf16[512,2048]{1,0:T(8,128)(2,1)} %param.7) | data formatting | bytes 4194304 | tf_op args[2]
  2.9 3.2 %fusion.5 = f32[32,128,64]{1,2,0:T(8,128)S(1)} fusion(bf16[512,32,64]{0,2,1:T(8,128)(2,1)S(1)} %bitcast.211, bf16[512,4096]{1,0:T(8,128)(2,1)} %param.6), kind=kOutput, calls=%fused_computation.4 | convolution fusion | flops 268435456 | bytes 7340032 | tf_op jit(solution)/shard_map/tdw,tdr->dwr/dot_general | solution.py:61
  6.1 3.3 %collective-permute-start = (f32[32,128,64]{1,2,0:T(8,128)S(1)}, f32[32,128,64]{1,2,0:T(8,128)S(1)}, u32[]{:S(2)}, u32[]{:S(2)}) collective-permute-start(f32[32,128,64]{1,2,0:T(8,128)S(1)} %fusion.5), channel_id=1, source_target_pairs={{0,1},{1,0},{2,3},{3,2},{4,5},{5,4},{6,7},{7,6},{8,9},{9,8},{10,11... | collective-permute-start | bytes 3145736 | tf_op jit(solution)/shard_map/ppermute | solution.py:17
  13.0 36.4 %multiply_convert_fusion.5 = bf16[32,512,512]{2,1,0:T(8,128)(2,1)} fusion(f32[32,512]{1,0:T(8,128)S(1)} %get-tuple-element.6, f32[32,512]{1,0:T(8,128)S(1)} %get-tuple-element.7, f32[32,512]{1,0:T(8,128)S(1)} %get-tuple-element.8, f32[32,512]{1,0:T(8,128)S(1)} %get-tuple-element.9, f32[32,512]{1,0:T(8,128)S(1)} %get-tuple-element.10, ...), kind=kOutput, calls=%fused_computation.clone.clone.1 | convolution fusion | flops 2256535552 | bytes 28704768 | tf_op jit(solution)/shard_map/thk,shk->hts/dot_general | solution.py:54
  51.2 2.0 collective-permute-start.2
  53.2 8.8 %fusion = f32[32,512,64]{1,2,0:T(8,128)S(1)} fusion(bf16[512,32,64]{0,2,1:T(8,128)(2,1)S(1)} %bitcast.212, bf16[32,512,512]{2,1,0:T(8,128)(2,1)} %multiply_convert_fusion.5), kind=kOutput, calls=%fused_computation.1 | convolution fusion | flops 1073741824 | bytes 23068672 | tf_op jit(solution)/shard_map/hts,shv->thv/dot_general | solution.py:58
  62.0 15.2 %collective-permute-done.2 = f32[32,128,64]{1,2,0:T(8,128)S(1)} collective-permute-done((f32[32,128,64]{1,2,0:T(8,128)S(1)}, f32[32,128,64]{1,2,0:T(8,128)S(1)}, u32[]{:S(2)}, u32[]{:S(2)}) %collective-permute-start.2) | collective-permute-done | bytes 1048608 | tf_op jit(solution)/shard_map/ppermute | solution.py:17
  81.6 3.5 %fusion.39 = f32[32,64,512]{2,1,0:T(8,128)} fusion(f32[32,128,64]{1,2,0:T(8,128)S(1)} %copy-done.3, bf16[512,4096]{1,0:T(8,128)(2,1)S(1)} %copy-done.1), kind=kOutput, calls=%fused_computation.37 | convolution fusion | flops 268697600 | bytes 9437184 | tf_op jit(solution)/shard_map/jeu,eud->jed/dot_general | solution.py:88
  85.1 16.0 %collective-permute-done.3 = f32[32,128,64]{1,2,0:T(8,128)S(1)} collective-permute-done((f32[32,128,64]{1,2,0:T(8,128)S(1)}, f32[32,128,64]{1,2,0:T(8,128)S(1)}, u32[]{:S(2)}, u32[]{:S(2)}) %collective-permute-start.3) | collective-permute-done | bytes 1048608 | tf_op jit(solution)/shard_map/ppermute | solution.py:17
  101.2 2.2 collective-permute-start.4
  103.5 3.7 %fusion.31 = f32[32,64,512]{2,1,0:T(8,128)} fusion(f32[32,128,64]{1,2,0:T(8,128)S(1)} %copy-done.5, bf16[512,4096]{1,0:T(8,128)(2,1)S(1)} %copy-done.1), kind=kOutput, calls=%fused_computation.30 | convolution fusion | flops 269484032 | bytes 9437184 | tf_op jit(solution)/shard_map/jeu,eud->jed/dot_general | solution.py:91
  107.1 3.5 %fusion.33 = f32[32,64,512]{2,1,0:T(8,128)} fusion(f32[32,128,64]{1,2,0:T(8,128)S(1)} %copy-done.5, bf16[512,4096]{1,0:T(8,128)(2,1)S(1)} %copy-done.1), kind=kOutput, calls=%fused_computation.32 | convolution fusion | flops 268697600 | bytes 9437184 | tf_op jit(solution)/shard_map/jeu,eud->jed/dot_general | solution.py:88
  110.7 3.5 %fusion.27 = f32[32,64,512]{2,1,0:T(8,128)} fusion(f32[32,128,64]{1,2,0:T(8,128)S(1)} %collective-permute-done.2, bf16[512,4096]{1,0:T(8,128)(2,1)S(1)} %copy-done.1), kind=kOutput, calls=%fused_computation.26 | convolution fusion | flops 269484032 | bytes 9437184 | tf_op jit(solution)/shard_map/jeu,eud->jed/dot_general | solution.py:91
  114.2 34.7 %collective-permute-done.4 = f32[32,128,64]{1,2,0:T(8,128)S(1)} collective-permute-done((f32[32,128,64]{1,2,0:T(8,128)S(1)}, f32[32,128,64]{1,2,0:T(8,128)S(1)}, u32[]{:S(2)}, u32[]{:S(2)}) %collective-permute-start.4) | collective-permute-done | bytes 1048608 | tf_op jit(solution)/shard_map/ppermute | solution.py:17
  149.1 6.1 %collective-permute-start.5 = (f32[32,128,64]{1,2,0:T(8,128)S(1)}, f32[32,128,64]{1,2,0:T(8,128)S(1)}, u32[]{:S(2)}, u32[]{:S(2)}) collective-permute-start(f32[32,128,64]{1,2,0:T(8,128)S(1)} %add.551), channel_id=1, source_target_pairs={{0,32},{8,40},{16,48},{24,56},{32,0},{40,8},{48,16},{56,24},{64,96... | collective-permute-start | bytes 3145736 | tf_op jit(solution)/shard_map/ppermute | solution.py:17
  155.2 3.6 %fusion.29 = f32[32,64,512]{2,1,0:T(8,128)} fusion(f32[32,128,64]{1,2,0:T(8,128)S(1)} %collective-permute-done.2, bf16[512,4096]{1,0:T(8,128)(2,1)S(1)} %copy-done.1), kind=kOutput, calls=%fused_computation.28 | convolution fusion | flops 268697600 | bytes 9437184 | tf_op jit(solution)/shard_map/jeu,eud->jed/dot_general | solution.py:88
  158.8 3.7 %fusion.23 = f32[32,64,512]{2,1,0:T(8,128)} fusion(f32[32,128,64]{1,2,0:T(8,128)S(1)} %collective-permute-done.3, bf16[512,4096]{1,0:T(8,128)(2,1)S(1)} %copy-done.1), kind=kOutput, calls=%fused_computation.22 | convolution fusion | flops 269484032 | bytes 9437184 | tf_op jit(solution)/shard_map/jeu,eud->jed/dot_general | solution.py:91
  162.5 3.5 %fusion.25 = f32[32,64,512]{2,1,0:T(8,128)} fusion(f32[32,128,64]{1,2,0:T(8,128)S(1)} %collective-permute-done.3, bf16[512,4096]{1,0:T(8,128)(2,1)S(1)} %copy-done.1), kind=kOutput, calls=%fused_computation.24 | convolution fusion | flops 268697600 | bytes 9437184 | tf_op jit(solution)/shard_map/jeu,eud->jed/dot_general | solution.py:88
  166.0 34.6 %collective-permute-done.5 = f32[32,128,64]{1,2,0:T(8,128)S(1)} collective-permute-done((f32[32,128,64]{1,2,0:T(8,128)S(1)}, f32[32,128,64]{1,2,0:T(8,128)S(1)}, u32[]{:S(2)}, u32[]{:S(2)}) %collective-permute-start.5) | collective-permute-done | bytes 1048608 | tf_op jit(solution)/shard_map/ppermute | solution.py:17
  202.4 3.6 %fusion.19 = f32[32,64,512]{2,1,0:T(8,128)} fusion(f32[32,128,64]{1,2,0:T(8,128)S(1)} %collective-permute-done.4, bf16[512,4096]{1,0:T(8,128)(2,1)S(1)} %copy-done.1), kind=kOutput, calls=%fused_computation.18 | convolution fusion | flops 269484032 | bytes 9437184 | tf_op jit(solution)/shard_map/jeu,eud->jed/dot_general | solution.py:91
  206.0 3.6 %fusion.21 = f32[32,64,512]{2,1,0:T(8,128)} fusion(f32[32,128,64]{1,2,0:T(8,128)S(1)} %collective-permute-done.4, bf16[512,4096]{1,0:T(8,128)(2,1)S(1)} %copy-done.1), kind=kOutput, calls=%fused_computation.20 | convolution fusion | flops 268697600 | bytes 9437184 | tf_op jit(solution)/shard_map/jeu,eud->jed/dot_general | solution.py:88
  209.6 3.5 %fusion.15 = f32[32,64,512]{2,1,0:T(8,128)} fusion(f32[32,128,64]{1,2,0:T(8,128)S(1)} %collective-permute-done.5, bf16[512,4096]{1,0:T(8,128)(2,1)S(1)} %copy-done.1), kind=kOutput, calls=%fused_computation.14 | convolution fusion | flops 269484032 | bytes 9437184 | tf_op jit(solution)/shard_map/jeu,eud->jed/dot_general | solution.py:91
  213.1 10.9 %collective-permute-done.6 = f32[32,128,64]{1,2,0:T(8,128)S(1)} collective-permute-done((f32[32,128,64]{1,2,0:T(8,128)S(1)}, f32[32,128,64]{1,2,0:T(8,128)S(1)}, u32[]{:S(2)}, u32[]{:S(2)}) %collective-permute-start.6) | collective-permute-done | bytes 1048608 | tf_op jit(solution)/shard_map/ppermute | solution.py:17
  224.2 5.0 %collective-permute-start.7 = (f32[32,128,64]{1,2,0:T(8,128)S(1)}, f32[32,128,64]{1,2,0:T(8,128)S(1)}, u32[]{:S(2)}, u32[]{:S(2)}) collective-permute-start(f32[32,128,64]{1,2,0:T(8,128)S(1)} %add.559), channel_id=1, source_target_pairs={{0,128},{8,136},{16,144},{24,152},{32,160},{40,168},{48,176},{56,1... | collective-permute-start | bytes 3145736 | tf_op jit(solution)/shard_map/ppermute | solution.py:23
  229.2 3.5 %fusion.17 = f32[32,64,512]{2,1,0:T(8,128)} fusion(f32[32,128,64]{1,2,0:T(8,128)S(1)} %collective-permute-done.5, bf16[512,4096]{1,0:T(8,128)(2,1)S(1)} %copy-done.1), kind=kOutput, calls=%fused_computation.16 | convolution fusion | flops 268697600 | bytes 9437184 | tf_op jit(solution)/shard_map/jeu,eud->jed/dot_general | solution.py:88
  232.7 3.6 %fusion.11 = f32[32,64,512]{2,1,0:T(8,128)} fusion(f32[32,128,64]{1,2,0:T(8,128)S(1)} %collective-permute-done.6, bf16[512,4096]{1,0:T(8,128)(2,1)S(1)} %copy-done.1), kind=kOutput, calls=%fused_computation.10 | convolution fusion | flops 269484032 | bytes 9437184 | tf_op jit(solution)/shard_map/jeu,eud->jed/dot_general | solution.py:91
  236.3 3.6 %fusion.13 = f32[32,64,512]{2,1,0:T(8,128)} fusion(f32[32,128,64]{1,2,0:T(8,128)S(1)} %collective-permute-done.6, bf16[512,4096]{1,0:T(8,128)(2,1)S(1)} %copy-done.1), kind=kOutput, calls=%fused_computation.12 | convolution fusion | flops 268697600 | bytes 9437184 | tf_op jit(solution)/shard_map/jeu,eud->jed/dot_general | solution.py:88
  239.9 9.1 %collective-permute-done.7 = f32[32,128,64]{1,2,0:T(8,128)S(1)} collective-permute-done((f32[32,128,64]{1,2,0:T(8,128)S(1)}, f32[32,128,64]{1,2,0:T(8,128)S(1)}, u32[]{:S(2)}, u32[]{:S(2)}) %collective-permute-start.7) | collective-permute-done | bytes 1048608 | tf_op jit(solution)/shard_map/ppermute | solution.py:23
  249.0 3.6 %fusion.7 = f32[32,64,512]{2,1,0:T(8,128)} fusion(f32[32,128,64]{1,2,0:T(8,128)S(1)} %collective-permute-done.7, bf16[512,4096]{1,0:T(8,128)(2,1)S(1)} %copy-done.1), kind=kOutput, calls=%fused_computation.6 | convolution fusion | flops 269484032 | bytes 9437184 | tf_op jit(solution)/shard_map/jeu,eud->jed/dot_general | solution.py:91
  252.6 23.7 %multiply_reduce_fusion = (f32[512,32]{0,1:T(8,128)}, f32[512,32,64]{0,2,1:T(8,128)}) fusion(f32[32,64,512]{2,1,0:T(8,128)} %fusion.7, f32[32,128,64]{1,2,0:T(8,128)} %copy-done.6, f32[512,32]{0,1:T(8,128)S(1)} %get-tuple-element.21, f32[32,64,512]{2,1,0:T(8,128)} %fusion.13, f32[32,64,512]{2,1,0:T(8,128)} %fusion.11, f32[512,32]{0,1:T(8,128)} %get-tuple-element.22, ...), kind=kOutput, calls=%fused_computation.56 | convolution fusion | flops 295944192 | bytes 77135872 | tf_op jit(solution)/shard_map/jeu,eud->jed/dot_general | solution.py:88
  277.1 2.7 multiply_convert_fusion.2
  279.8 2.4 copy.44
  (44 shorter events, 12.9 us)
Async XLA Ops:
  2.9 8.5 %copy-start.8 = (bf16[512,18,32]{0,2,1:T(8,128)(2,1)S(1)}, bf16[512,18,32]{0,2,1:T(8,128)(2,1)}, u32[]{:S(2)}) copy-start(bf16[512,18,32]{0,2,1:T(8,128)(2,1)} %param.8) | copy-start | bytes 1769476
  2.9 10.1 %copy-start.7 = (bf16[512,4096]{1,0:T(8,128)(2,1)S(1)}, bf16[512,4096]{1,0:T(8,128)(2,1)}, u32[]{:S(2)}) copy-start(bf16[512,4096]{1,0:T(8,128)(2,1)} %param.6) | copy-start | bytes 12582916
  6.1 6.9 %copy-start = (bf16[512,4096]{1,0:T(8,128)(2,1)S(1)}, bf16[512,4096]{1,0:T(8,128)(2,1)}, u32[]{:S(2)}) copy-start(bf16[512,4096]{1,0:T(8,128)(2,1)} %param.5) | copy-start | bytes 12582916
  6.1 5.6 %collective-permute-start = (f32[32,128,64]{1,2,0:T(8,128)S(1)}, f32[32,128,64]{1,2,0:T(8,128)S(1)}, u32[]{:S(2)}, u32[]{:S(2)}) collective-permute-start(f32[32,128,64]{1,2,0:T(8,128)S(1)} %fusion.5), channel_id=1, source_target_pairs={{0,1},{1,0},{2,3},{3,2},{4,5},{5,4},{6,7},{7,6},{8,9},{9,8},{10,11... | collective-permute-start | bytes 3145736 | tf_op jit(solution)/shard_map/ppermute | solution.py:17
  11.7 37.7 %copy-start.2 = (f32[32,128,64]{1,2,0:T(8,128)}, f32[32,128,64]{1,2,0:T(8,128)S(1)}, u32[]{:S(2)}) copy-start(f32[32,128,64]{1,2,0:T(8,128)S(1)} %collective-permute-done) | copy-start | bytes 3145732
  13.0 36.5 %collective-permute-start.1 = (f32[32,128,64]{1,2,0:T(8,128)}, f32[32,128,64]{1,2,0:T(8,128)S(1)}, u32[]{:S(2)}, u32[]{:S(2)}) collective-permute-start(f32[32,128,64]{1,2,0:T(8,128)} %add.535), channel_id=1, source_target_pairs={{0,2},{1,3},{2,0},{3,1},{4,6},{5,7},{6,4},{7,5},{8,10},{9,11},{10,... | collective-permute-start | bytes 3145736 | tf_op jit(solution)/shard_map/ppermute | solution.py:17
  13.0 36.4 %copy-start.9 = (bf16[2048]{0:T(1024)(128)(2,1)S(1)}, bf16[2048]{0:T(1024)(128)(2,1)}, u32[]{:S(2)}) copy-start(bf16[2048]{0:T(1024)(128)(2,1)} %param.9) | copy-start | bytes 12292
  49.5 12.5 %copy-start.4 = (f32[32,128,64]{1,2,0:T(8,128)}, f32[32,128,64]{1,2,0:T(8,128)S(1)}, u32[]{:S(2)}) copy-start(f32[32,128,64]{1,2,0:T(8,128)S(1)} %collective-permute-done.1) | copy-start | bytes 3145732
  51.2 26.0 %collective-permute-start.2 = (f32[32,128,64]{1,2,0:T(8,128)S(1)}, f32[32,128,64]{1,2,0:T(8,128)S(1)}, u32[]{:S(2)}, u32[]{:S(2)}) collective-permute-start(f32[32,128,64]{1,2,0:T(8,128)S(1)} %add.539), channel_id=1, source_target_pairs={{0,4},{1,5},{2,6},{3,7},{4,0},{5,1},{6,2},{7,3},{8,12},{9,13},{10,... | collective-permute-start | bytes 3145736 | tf_op jit(solution)/shard_map/ppermute | solution.py:17
  53.2 26.8 %copy-start.1 = (bf16[512,4096]{1,0:T(8,128)(2,1)S(1)}, bf16[512,4096]{1,0:T(8,128)(2,1)}, u32[]{:S(2)}) copy-start(bf16[512,4096]{1,0:T(8,128)(2,1)} %param.5) | copy-start | bytes 12582916
  62.0 17.9 %copy-start.3 = (f32[32,128,64]{1,2,0:T(8,128)S(1)}, f32[32,128,64]{1,2,0:T(8,128)}, u32[]{:S(2)}) copy-start(f32[32,128,64]{1,2,0:T(8,128)} %copy-done.2) | copy-start | bytes 3145732
  77.4 23.7 %collective-permute-start.3 = (f32[32,128,64]{1,2,0:T(8,128)S(1)}, f32[32,128,64]{1,2,0:T(8,128)S(1)}, u32[]{:S(2)}, u32[]{:S(2)}) collective-permute-start(f32[32,128,64]{1,2,0:T(8,128)S(1)} %add.543), channel_id=1, source_target_pairs={{0,8},{8,0},{16,24},{24,16},{32,40},{40,32},{48,56},{56,48},{64,72... | collective-permute-start | bytes 3145736 | tf_op jit(solution)/shard_map/ppermute | solution.py:17
  81.5 21.9 %copy-start.5 = (f32[32,128,64]{1,2,0:T(8,128)S(1)}, f32[32,128,64]{1,2,0:T(8,128)}, u32[]{:S(2)}) copy-start(f32[32,128,64]{1,2,0:T(8,128)} %copy-done.4) | copy-start | bytes 3145732
  101.2 47.7 %collective-permute-start.4 = (f32[32,128,64]{1,2,0:T(8,128)S(1)}, f32[32,128,64]{1,2,0:T(8,128)S(1)}, u32[]{:S(2)}, u32[]{:S(2)}) collective-permute-start(f32[32,128,64]{1,2,0:T(8,128)S(1)} %add.547), channel_id=1, source_target_pairs={{0,16},{8,24},{16,0},{24,8},{32,48},{40,56},{48,32},{56,40},{64,80... | collective-permute-start | bytes 3145736 | tf_op jit(solution)/shard_map/ppermute | solution.py:17
  149.1 51.5 %collective-permute-start.5 = (f32[32,128,64]{1,2,0:T(8,128)S(1)}, f32[32,128,64]{1,2,0:T(8,128)S(1)}, u32[]{:S(2)}, u32[]{:S(2)}) collective-permute-start(f32[32,128,64]{1,2,0:T(8,128)S(1)} %add.551), channel_id=1, source_target_pairs={{0,32},{8,40},{16,48},{24,56},{32,0},{40,8},{48,16},{56,24},{64,96... | collective-permute-start | bytes 3145736 | tf_op jit(solution)/shard_map/ppermute | solution.py:17
  200.7 23.3 %collective-permute-start.6 = (f32[32,128,64]{1,2,0:T(8,128)S(1)}, f32[32,128,64]{1,2,0:T(8,128)S(1)}, u32[]{:S(2)}, u32[]{:S(2)}) collective-permute-start(f32[32,128,64]{1,2,0:T(8,128)S(1)} %add.555), channel_id=1, source_target_pairs={{0,64},{8,72},{16,80},{24,88},{32,96},{40,104},{48,112},{56,120},{... | collective-permute-start | bytes 3145736 | tf_op jit(solution)/shard_map/ppermute | solution.py:17
  224.2 24.8 %collective-permute-start.7 = (f32[32,128,64]{1,2,0:T(8,128)S(1)}, f32[32,128,64]{1,2,0:T(8,128)S(1)}, u32[]{:S(2)}, u32[]{:S(2)}) collective-permute-start(f32[32,128,64]{1,2,0:T(8,128)S(1)} %add.559), channel_id=1, source_target_pairs={{0,128},{8,136},{16,144},{24,152},{32,160},{40,168},{48,176},{56,1... | collective-permute-start | bytes 3145736 | tf_op jit(solution)/shard_map/ppermute | solution.py:23
  249.0 3.6 %copy-start.6 = (f32[32,128,64]{1,2,0:T(8,128)}, f32[32,128,64]{1,2,0:T(8,128)S(1)}, u32[]{:S(2)}) copy-start(f32[32,128,64]{1,2,0:T(8,128)S(1)} %collective-permute-done.7) | copy-start | bytes 3145732
where the time goes:
time: 285 us; the launch traced here: 282 us
  matrix products  124 us (44%)
  waiting for transfers between devices  121 us (42%)
  starting transfers between devices  21.3 us (7%)
  other arithmetic  11 us (4%)
  local copies, waits for them, and re-layouts  5.41 us (2%)
    ppermute x7, waiting for transfers between devices, swapped(): return lax.ppermute(value, axis, pairs)  112 us
    dot_general x8, matrix products, on_device(): jnp.einsum('jeu,eud->jed', query_matrix_rows, upper_half_state, preferred...  48.6 us
    dot_general x1, matrix products, on_device(): jnp.einsum('thk,shk->hts', query_matrix_rows, key_matrix_rows, preferred_...  36.4 us
    dot_general x8, matrix products, on_device(): jnp.einsum('jeu,eud->jed', query_matrix_rows, lower_half_state, preferred...  26.7 us
    ppermute x7, starting transfers between devices, swapped(): return lax.ppermute(value, axis, pairs)  16.3 us
    ppermute x1, waiting for transfers between devices, from_behind(): return lax.ppermute(block, axis, route)  9.08 us
    dot_general x1, matrix products, on_device(): jnp.einsum('hts,shv->thv', weighted, value_matrix_rows, preferred_element...  8.8 us
  transfers between devices with their start and end apart: 8, of which 7 were waited for; matrix products, arithmetic and copies ran while one was open for 34% of the time, Pallas kernels for 0%

commit v1 on v0

v1 whole, which is shorter than its diff:
```python
import jax
import jax.numpy as jnp
from jax import lax
from jax.experimental import pallas as pl
from jax.experimental.pallas import tpu as pltpu
from jax.sharding import Mesh, PartitionSpec as P

HEADS = 32
DK = 128
DV = 64
TOK = 512
HALF = 256
TILE = 128
LOCAL = 10
LEVELS = 18
GROUP = 4
STEPS = HEADS // GROUP
EPS = 1e-06
F32 = jnp.float32
BF16 = jnp.bfloat16


def xor_permute(value, axis, mask):
    size = lax.axis_size(axis)
    return lax.ppermute(value, axis, [(i, i ^ mask) for i in range(size)])


def dot_t0(a, b):
    return lax.dot_general(a, b, (((0,), (0,)), ((), ())), preferred_element_type=F32)


def dot_t1(a, b):
    return lax.dot_general(a, b, (((1,), (1,)), ((), ())), preferred_element_type=F32)


def state_kernel(k_ref, v_ref, s_ref, first_ref):
    for pair in range(GROUP // 2):
        v = v_ref[:, pair * 2 * DV : (pair + 1) * 2 * DV]
        k = k_ref[:, pair * 2 * DK : (pair + 1) * 2 * DK]
        first = dot_t0(v[:HALF], k[:HALF])
        both = first + dot_t0(v[HALF:], k[HALF:])
        for j in range(2):
            rows = slice(j * DV, (j + 1) * DV)
            cols = slice(j * DK, (j + 1) * DK)
            s_ref[2 * pair + j] = both[rows, cols]
            first_ref[2 * pair + j] = first[rows, cols].astype(BF16)


def block_state(keys, values):
    return pl.pallas_call(
        state_kernel,
        grid=(STEPS,),
        in_specs=[
            pl.BlockSpec((TOK, GROUP * DK), lambda i: (0, i)),
            pl.BlockSpec((TOK, GROUP * DV), lambda i: (0, i)),
        ],
        out_specs=[
            pl.BlockSpec((GROUP, DV, DK), lambda i: (i, 0, 0)),
            pl.BlockSpec((GROUP, DV, DK), lambda i: (i, 0, 0)),
        ],
        out_shape=[
            jax.ShapeDtypeStruct((HEADS, DV, DK), F32),
            jax.ShapeDtypeStruct((HEADS, DV, DK), BF16),
        ],
        cost_estimate=pl.CostEstimate(flops=2 * TOK * 4096 * 128, bytes_accessed=8 << 20, transcendentals=0),
        compiler_params=pltpu.CompilerParams(vmem_limit_bytes=24 << 20),
        name="block_state",
    )(keys, values)


def diagonal_weight(rows):
    group = lax.broadcasted_iota(jnp.int32, (16, TILE), 0)
    lane = lax.broadcasted_iota(jnp.int32, (16, TILE), 1)
    other = lane >> 3
    xored = group ^ other
    coarse = jnp.zeros((16, TILE), F32)
    for level in range(4, 8):
        coarse = jnp.where((xored >> (level - 4)) == 1, rows[level], coarse)
    coarse = jnp.where(other > group, coarse, 0.0)
    sub = lax.broadcasted_iota(jnp.int32, (8, TILE), 0)
    low = lax.broadcasted_iota(jnp.int32, (8, TILE), 1)
    place = low & 7
    near = sub ^ place
    fine = jnp.broadcast_to(rows[0], (8, TILE))
    for level in range(1, 4):
        fine = jnp.where((near >> (level - 1)) == 1, rows[level], fine)
    fine = jnp.where(place >= sub, fine, 0.0)
    owner = low >> 3
    return [
        jnp.where(owner == i, fine, jnp.broadcast_to(coarse[i : i + 1], (8, TILE)))
        for i in range(16)
    ]


def local_kernel(q_ref, k_ref, v_ref, lw_ref, first_ref, o_ref):
    for pair in range(GROUP // 2):
        v_t = v_ref[:, pair * 2 * DV : (pair + 1) * 2 * DV].T
        for j in range(2):
            head = 2 * pair + j
            cols = slice(head * DK, (head + 1) * DK)
            for block in range(2):
                at = block * HALF
                q = q_ref[at : at + HALF, cols]
                k = k_ref[at : at + HALF, cols]
                scores = dot_t1(k, q)
                tiles = []
                for tile in range(2):
                    spot = at + tile * TILE
                    rows = [lw_ref[head, l : l + 1, spot : spot + TILE] for l in range(8)]
                    weight = jnp.concatenate(diagonal_weight(rows), axis=0)
                    part = slice(tile * TILE, (tile + 1) * TILE)
                    tiles.append((scores[part, part] * weight).astype(BF16))
                across = lw_ref[head, 8:9, at + TILE : at + HALF]
                upper = (scores[:TILE, TILE:] * across).astype(BF16)
                zero = jnp.zeros((TILE, TILE), BF16)
                weighted = jnp.concatenate(
                    [
                        jnp.concatenate([tiles[0], upper], axis=1),
                        jnp.concatenate([zero, tiles[1]], axis=1),
                    ],
                    axis=0,
                )
                v_part = v_t[j * DV : (j + 1) * DV, at : at + HALF]
                out = jnp.dot(v_part, weighted, preferred_element_type=F32)
                if block == 1:
                    out = out + lw_ref[head, 9:10, at : at + HALF] * dot_t1(first_ref[head], q)
                o_ref[head, :, at : at + HALF] = out


def local_attention(queries, keys, values, rows, first):
    return pl.pallas_call(
        local_kernel,
        grid=(STEPS,),
        in_specs=[
            pl.BlockSpec((TOK, GROUP * DK), lambda i: (0, i)),
            pl.BlockSpec((TOK, GROUP * DK), lambda i: (0, i)),
            pl.BlockSpec((TOK, GROUP * DV), lambda i: (0, i)),
            pl.BlockSpec((GROUP, LEVELS, TOK), lambda i: (i, 0, 0)),
            pl.BlockSpec((GROUP, DV, DK), lambda i: (i, 0, 0)),
        ],
        out_specs=pl.BlockSpec((GROUP, DV, TOK), lambda i: (i, 0, 0)),
        out_shape=jax.ShapeDtypeStruct((HEADS, DV, TOK), F32),
        cost_estimate=pl.CostEstimate(flops=8 << 30, bytes_accessed=16 << 20, transcendentals=0),
        compiler_params=pltpu.CompilerParams(vmem_limit_bytes=24 << 20),
        name="local_attention",
    )(queries, keys, values, rows, first)


def finish_kernel(
    place_ref, q_ref, local_ref, lw_ref, gain_ref, zero_ref,
    own1_ref, oth1_ref, own2_ref, oth2_ref, own3_ref, oth3_ref, o_ref, lhs_ref,
):
    step = pl.program_id(0)

    def stage(a, b, c):
        for j in range(GROUP):
            lhs_ref[j, 64:128] = a[0, 0, j].astype(BF16)
            lhs_ref[j, 128:192] = a[0, 1, j].astype(BF16)
            lhs_ref[j, 192:384] = b[0, j].astype(BF16)
            lhs_ref[j, 384:512] = c[0, j].astype(BF16)

    for j in range(GROUP):
        lhs_ref[j, 0:64] = zero_ref[j].astype(BF16)

    @pl.when(step < STEPS // 2)
    def _():
        stage(own1_ref, own2_ref, own3_ref)

    @pl.when(step >= STEPS // 2)
    def _():
        stage(oth1_ref, oth2_ref, oth3_ref)

    for pair in range(GROUP // 2):
        for block in range(2):
            at = slice(block * HALF, (block + 1) * HALF)
            outs = []
            for j in range(2):
                head = 2 * pair + j
                q = q_ref[at, head * DK : (head + 1) * DK]
                r = dot_t1(lhs_ref[head], q)
                w = [lw_ref[head, LOCAL + l : LOCAL + l + 1, at] for l in range(8)]
                acc = local_ref[head, :, at] + r[0:64] * w[0] + r[64:128] * w[1] + r[128:192] * w[2]
                halves = []
                for half in range(2):
                    part = acc[half * 32 : (half + 1) * 32]
                    for l in range(3):
                        base = 192 + half * 96 + l * 32
                        part = part + r[base : base + 32] * w[3 + l]
                    for l in range(2):
                        base = 384 + half * 64 + l * 32
                        part = part + r[base : base + 32] * w[6 + l]
                    halves.append(part)
                acc = jnp.concatenate(halves, axis=0)
                mean = jnp.mean(acc * acc, axis=0, keepdims=True)
                outs.append(acc * lax.rsqrt(mean + EPS))
            flat = jnp.concatenate(outs, axis=0).T
            cols = slice(pair * 2 * DV, (pair + 1) * 2 * DV)
            o_ref[at, cols] = (flat * gain_ref[:, cols]).astype(BF16)


def finish(place, queries, local, rows, gain, zero, own, oth):
    def group(i, place):
        return 4 * (place[0] ^ (i // 4)) + (place[1] ^ (i % 4))

    def own_index(i):
        return jnp.minimum(i, 3)

    def oth_index(i):
        return jnp.maximum(i - 4, 0)

    def pieces(array, index):
        block = (1,) + array.shape[1:]
        rank = len(block)
        return pl.BlockSpec(block, lambda i, place: (index(i),) + (0,) * (rank - 1))

    sides = []
    specs = []
    for mine, theirs in zip(own, oth):
        sides += [mine, theirs]
        specs += [pieces(mine, own_index), pieces(theirs, oth_index)]
    return pl.pallas_call(
        finish_kernel,
        grid_spec=pltpu.PrefetchScalarGridSpec(
            num_scalar_prefetch=1,
            grid=(STEPS,),
            in_specs=[
                pl.BlockSpec((TOK, GROUP * DK), lambda i, p: (0, group(i, p))),
                pl.BlockSpec((GROUP, DV, TOK), lambda i, p: (group(i, p), 0, 0)),
                pl.BlockSpec((GROUP, LEVELS, TOK), lambda i, p: (group(i, p), 0, 0)),
                pl.BlockSpec((1, GROUP * DV), lambda i, p: (0, group(i, p))),
                pl.BlockSpec((GROUP, DV, DK), lambda i, p: (group(i, p), 0, 0)),
            ]
            + specs,
            out_specs=pl.BlockSpec((TOK, GROUP * DV), lambda i, p: (0, group(i, p))),
            scratch_shapes=[pltpu.VMEM((GROUP, 8 * DV, DK), BF16)],
        ),
        out_shape=jax.ShapeDtypeStruct((TOK, HEADS * DV), BF16),
        cost_estimate=pl.CostEstimate(flops=9 << 30, bytes_accessed=20 << 20, transcendentals=0),
        compiler_params=pltpu.CompilerParams(vmem_limit_bytes=32 << 20),
        name="finish",
    )(place, queries, local, rows, gain, zero, *sides)


def gathered(payload):
    return jnp.stack([payload[0]] + [xor_permute(payload[d], "x", d) for d in range(1, 4)])


def on_device(queries, keys, values, level_weights, out_gain):
    core, x, z, y = (lax.axis_index(a) for a in ("c", "x", "z", "y"))
    block = ((y * 8 + z) * 4 + x) * 2 + core
    state, first = block_state(keys, values)

    scale = [1.0] * LOCAL + [(block >> j & 1).astype(F32) for j in range(8)]
    scale = jnp.stack([jnp.asarray(s, F32) for s in scale])
    rows = jnp.transpose(level_weights, (2, 1, 0)).astype(F32) * scale[None, :, None]

    local = local_attention(queries, keys, values, rows, first)

    partner = xor_permute(state, "c", 1)
    half = lax.dynamic_slice_in_dim(state, core * 16, 16, 0) + lax.dynamic_slice_in_dim(
        partner, core * 16, 16, 0
    )
    u = lax.all_to_all(half.reshape(4, GROUP * DV, DK), "x", 0, 0, tiled=True)
    pairs = u[0::2] + u[1::2]
    row_sum = pairs[0] + pairs[1]
    low = []
    for d in range(4):
        to = x ^ d
        one = lax.dynamic_index_in_dim(u, to ^ 1, 0, keepdims=False)
        two = lax.dynamic_index_in_dim(pairs, (to >> 1) ^ 1, 0, keepdims=False)
        low.append(jnp.stack([one, two]).reshape(2, GROUP, DV, DK))
    own1 = gathered(low)
    w = lax.all_to_all(row_sum.reshape(8, 32, DK), "z", 0, 0, tiled=True)
    w2 = w.reshape(4, 2, 32, DK)
    t4 = w2[:, 0] + w2[:, 1]
    t5 = t4[0::2] + t4[1::2]
    t6 = t5[0] + t5[1]
    p1 = xor_permute(t6, "y", 1)
    p2 = xor_permute(t6, "y", 2)
    p3 = xor_permute(t6, "y", 3)
    l3 = w2[:, ::-1].reshape(8, 32, DK)
    l4 = jnp.broadcast_to(t4.reshape(2, 2, 1, 32, DK)[:, ::-1], (2, 2, 2, 32, DK)).reshape(8, 32, DK)
    l5 = jnp.broadcast_to(t5.reshape(2, 1, 32, DK)[::-1], (2, 4, 32, DK)).reshape(8, 32, DK)
    mid = lax.all_to_all(jnp.stack([l3, l4, l5], axis=1), "z", 0, 0, tiled=True)
    top = jnp.broadcast_to(jnp.stack([p1, p2 + p3])[None], (8, 2, 32, DK))
    top = lax.all_to_all(top, "z", 0, 0, tiled=True)
    mid = mid.reshape(GROUP, 6 * 32, DK)
    top = top.reshape(GROUP, 4 * 32, DK)
    own2 = gathered([mid] * 4)
    own3 = gathered([top] * 4)
    own = [own1, own2, own3]
    oth = [xor_permute(o, "c", 1) for o in own]
    place = jnp.stack([core, x]).astype(jnp.int32)
    gain = out_gain.astype(F32).reshape(1, HEADS * DV)
    return finish(place, queries, local, rows, gain, partner, own, oth)


def solution(mesh):
    wide = Mesh(mesh.devices.reshape(4, 8, 4, 2), ("y", "z", "x", "c"))
    split = ("y", "z", "x", "c")
    return jax.shard_map(
        on_device,
        mesh=wide,
        in_specs=(P(split, None), P(split, None), P(split, None), P(split, None, None), P()),
        out_specs=P(split, None),
        check_vma=False,
    )
```

time: 285 us -> 135 us (0.47)
  matrix products: 124 us -> 0 us
  waiting for transfers between devices: 121 us -> 34.4 us
  Pallas kernels: 0 us -> 25.8 us
  starting transfers between devices: 21.3 us -> 40.6 us
  blocking collectives: 0 us -> 14.4 us
    dot_general x19 -> x0, matrix products: 124 us -> none  [the longest x8 48.6 us: on_device(): jnp.einsum('jeu,eud->jed', query_matrix_rows, upper_half_state, preferred...]
    ppermute x8 -> x16, waiting for transfers between devices: 121 us -> 21.5 us  [xor_permute(): return lax.ppermute(value, axis, [(i, i ^ mask) for i in range(size)])]
    pallas_call x0 -> x3, Pallas kernels: none -> 25.8 us  [the longest x1 12.8 us: local_attention(): pl.pallas_call(local_kernel, grid=(STEPS,), in_specs=[pl.BlockSpec((TOK,...]
    all_to_all x0 -> x1, blocking collectives: none -> 14.4 us  [on_device(): w = lax.all_to_all(row_sum.reshape(8, 32, DK), 'z', 0, 0, tiled=True)]
    all_to_all x0 -> x3, waiting for transfers between devices: none -> 12.8 us  [the longest x1 9.14 us: on_device(): u = lax.all_to_all(half.reshape(4, GROUP * DV, DK), 'x', 0, 0, tiled=True)]
    all_to_all x0 -> x3, starting transfers between devices: none -> 11 us  [the longest x1 4.05 us: on_device(): top = lax.all_to_all(top, 'z', 0, 0, tiled=True)]
    ppermute x8 -> x16, starting transfers between devices: 21.3 us -> 29.7 us  [xor_permute(): return lax.ppermute(value, axis, [(i, i ^ mask) for i in range(size)])]
    another operation x0 -> x11, other arithmetic: none -> 7.18 us  [the longest x3 4.14 us: gathered(): jnp.stack([payload[0]] + [xor_permute(payload[d], 'x', d) for d in range(...]
  transfers between devices with their start and end apart: 8 -> 19, of which waited for: 7 -> 8; matrix products, arithmetic and copies ran while one was open for 34% -> 7% of each run, Pallas kernels for 0% -> 10%
where the time goes in v1:
time: 135 us; the launch traced here: 134 us
  starting transfers between devices  40.6 us (30%)
  waiting for transfers between devices  34.4 us (25%)
  Pallas kernels  25.8 us (19%)
  blocking collectives  14.4 us (11%)
  other arithmetic  11.8 us (9%)
  local copies, waits for them, and re-layouts  6.85 us (5%)
    ppermute x16, starting transfers between devices, xor_permute(): return lax.ppermute(value, axis, [(i, i ^ mask) for i in range(size)])  29.7 us
    ppermute x16, waiting for transfers between devices, xor_permute(): return lax.ppermute(value, axis, [(i, i ^ mask) for i in range(size)])  21.5 us
    all_to_all x1, blocking collectives, on_device(): w = lax.all_to_all(row_sum.reshape(8, 32, DK), 'z', 0, 0, tiled=True)  14.4 us
    pallas_call x1, Pallas kernels, local_attention(): pl.pallas_call(local_kernel, grid=(STEPS,), in_specs=[pl.BlockSpec((TOK,...  12.8 us
    pallas_call x1, Pallas kernels, finish(): pl.pallas_call(finish_kernel, grid_spec=pltpu.PrefetchScalarGridSpec(num_...  10.2 us
    all_to_all x1, waiting for transfers between devices, on_device(): u = lax.all_to_all(half.reshape(4, GROUP * DV, DK), 'x', 0, 0, tiled=True)  9.14 us
    unnamed x22, local copies, waits for them, and re-layouts  6 us
    another operation x3, other arithmetic, gathered(): jnp.stack([payload[0]] + [xor_permute(payload[d], 'x', d) for d in range(...  4.14 us
  transfers between devices with their start and end apart: 19, of which 8 were waited for; matrix products, arithmetic and copies ran while one was open for 7% of the time, Pallas kernels for 10%

profile of v1, /device:TPU:1, one launch (start us, length us, event | category | flops | bytes accessed | tf_op | source)
XLA Modules:
  0.0 134.3 jit_solution(8200368959436389983)
XLA Ops:
  0.0 2.2 %copy-done = bf16[512,4096]{1,0:T(8,128)(2,1)S(1)} copy-done((bf16[512,4096]{1,0:T(8,128)(2,1)S(1)}, bf16[512,4096]{1,0:T(8,128)(2,1)}, u32[]{:S(2)}) %copy-start) | copy-done | bytes 4194328
  2.2 1.6 %copy-done.2 = bf16[512,2048]{1,0:T(8,128)(2,1)S(1)} copy-done((bf16[512,2048]{1,0:T(8,128)(2,1)S(1)}, bf16[512,2048]{1,0:T(8,128)(2,1)}, u32[]{:S(2)}) %copy-start.2) | copy-done | bytes 2097176
  3.8 2.9 %block_state.1 = (f32[32,64,128]{2,1,0:T(8,128)S(1)}, bf16[32,64,128]{2,1,0:T(8,128)(2,1)S(1)}) custom-call(bf16[512,4096]{1,0:T(8,128)(2,1)S(1)} %copy-done, bf16[512,2048]{1,0:T(8,128)(2,1)S(1)} %copy-done.2), custom_call_target="tpu_custom_call" | custom-call | flops 536870912 | bytes 8388608 | tf_op jit(solution)/shard_map/block_state/pallas_call | solution.py:50
  6.7 3.3 %collective-permute-start = (f32[32,64,128]{2,1,0:T(8,128)S(1)}, f32[32,64,128]{2,1,0:T(8,128)S(1)}, u32[]{:S(2)}, u32[]{:S(2)}) collective-permute-start(f32[32,64,128]{2,1,0:T(8,128)S(1)} %get-tuple-element.8), channel_id=1, source_target_pairs={{0,1},{1,0},{2,3},{3,2},{4,5},{5,4},{6,7},{7,6},{8,9},{9,8},{10,11... | collective-permute-start | bytes 3145736 | tf_op jit(solution)/shard_map/ppermute | solution.py:25
  10.0 2.3 %collective-permute-done.zero_ref = f32[32,64,128]{2,1,0:T(8,128)S(1)} collective-permute-done((f32[32,64,128]{2,1,0:T(8,128)S(1)}, f32[32,64,128]{2,1,0:T(8,128)S(1)}, u32[]{:S(2)}, u32[]{:S(2)}) %collective-permute-start) | collective-permute-done | bytes 1048608 | tf_op jit(solution)/shard_map/ppermute | solution.py:25
  12.3 0.9 dynamic-slice_add_fusion
  13.1 3.5 %all-to-all-start = ((f32[4,256,128]{2,1,0:T(8,128)}), f32[4,256,128]{2,1,0:T(8,128)S(1)}, u32[]{:S(2)}, u32[]{:S(2)}) async-start(f32[4,256,128]{2,1,0:T(8,128)} %bitcast.12), calls=%async_computation | async-start | bytes 1048576 | tf_op jit(solution)/shard_map/all_to_all | solution.py:263
  16.7 9.1 %all-to-all-done = f32[4,256,128]{2,1,0:T(8,128)S(1)} async-done(((f32[4,256,128]{2,1,0:T(8,128)}), f32[4,256,128]{2,1,0:T(8,128)S(1)}, u32[]{:S(2)}, u32[]{:S(2)}) %all-to-all-start) | async-done | bytes 524320 | tf_op jit(solution)/shard_map/all_to_all | solution.py:263
  25.8 0.8 slice_add_fusion.1
  26.6 14.4 %all_to_all.20 = f32[8,32,128]{2,1,0:T(8,128)S(1)} all-to-all(f32[8,32,128]{2,1,0:T(8,128)S(1)} %bitcast.57), channel_id=1, replica_groups=mesh['y'=4,'z'=8,'x'=4,'c'=2] {'z'}, dimensions={0} | all-to-all | bytes 262144 | tf_op jit(solution)/shard_map/all_to_all | solution.py:273
  41.2 0.8 pad_maximum_fusion.3
  41.9 3.5 %all-to-all-start.2 = ((f32[8,3,32,128]{3,2,1,0:T(8,128)}), f32[8,3,32,128]{3,2,1,0:T(8,128)S(1)}, u32[]{:S(2)}, u32[]{:S(2)}) async-start(f32[8,3,32,128]{3,2,1,0:T(8,128)} %pad_maximum_fusion.3), calls=%async_computation.2 | async-start | bytes 786432 | tf_op jit(solution)/shard_map/all_to_all | solution.py:284
  45.4 2.8 %collective-permute-start.11 = (f32[32,128]{1,0:T(8,128)S(1)}, f32[32,128]{1,0:T(8,128)S(1)}, u32[]{:S(2)}, u32[]{:S(2)}) collective-permute-start(f32[32,128]{1,0:T(8,128)S(1)} %fusion.1), channel_id=1, source_target_pairs={{0,192},{64,128},{128,64},{192,0},{1,193},{65,129},{129,65},{193,1... | collective-permute-start | bytes 49160 | tf_op jit(solution)/shard_map/ppermute | solution.py:25
  49.4 3.0 %collective-permute-done.10 = f32[32,128]{1,0:T(8,128)S(1)} collective-permute-done((f32[32,128]{1,0:T(8,128)S(1)}, f32[32,128]{1,0:T(8,128)S(1)}, u32[]{:S(2)}, u32[]{:S(2)}) %collective-permute-start.10) | collective-permute-done | bytes 16416 | tf_op jit(solution)/shard_map/ppermute | solution.py:25
  52.4 3.7 %all-to-all-done.2 = f32[8,3,32,128]{3,2,1,0:T(8,128)S(1)} async-done(((f32[8,3,32,128]{3,2,1,0:T(8,128)}), f32[8,3,32,128]{3,2,1,0:T(8,128)S(1)}, u32[]{:S(2)}, u32[]{:S(2)}) %all-to-all-start.2) | async-done | bytes 393248 | tf_op jit(solution)/shard_map/all_to_all | solution.py:284
  56.8 4.1 %all-to-all-start.3 = ((f32[8,2,32,128]{3,2,1,0:T(8,128)}), f32[8,2,32,128]{3,2,1,0:T(8,128)}, u32[]{:S(2)}, u32[]{:S(2)}) async-start(f32[8,2,32,128]{3,2,1,0:T(8,128)} %broadcast_in_dim.22), calls=%async_computation.3 | async-start | bytes 524288 | tf_op jit(solution)/shard_map/all_to_all | solution.py:286
  60.8 1.0 collective-permute-start.7
  61.8 1.2 collective-permute-start.6
  63.0 1.2 collective-permute-start.5
  65.9 1.8 %collective-permute-start.2 = (f32[2,4,64,128]{3,2,1,0:T(8,128)}, f32[2,4,64,128]{3,2,1,0:T(8,128)}, u32[]{:S(2)}, u32[]{:S(2)}) collective-permute-start(f32[2,4,64,128]{3,2,1,0:T(8,128)} %bitcast.16), channel_id=1, source_target_pairs={{0,4},{2,6},{4,0},{6,2},{1,5},{3,7},{5,1},{7,3},{8,12},{10,14},{12... | collective-permute-start | bytes 786440 | tf_op jit(solution)/shard_map/ppermute | solution.py:25
  68.4 11.9 %collective-permute-done.7 = f32[4,192,128]{2,1,0:T(8,128)S(1)} collective-permute-done((f32[4,192,128]{2,1,0:T(8,128)S(1)}, f32[4,192,128]{2,1,0:T(8,128)S(1)}, u32[]{:S(2)}, u32[]{:S(2)}) %collective-permute-start.7) | collective-permute-done | bytes 393248 | tf_op jit(solution)/shard_map/ppermute | solution.py:25
  80.4 2.7 %collective-permute-start.14 = (f32[4,128,128]{2,1,0:T(8,128)}, f32[4,128,128]{2,1,0:T(8,128)}, u32[]{:S(2)}, u32[]{:S(2)}) collective-permute-start(f32[4,128,128]{2,1,0:T(8,128)} %bitcast.38), channel_id=1, source_target_pairs={{0,6},{2,4},{4,2},{6,0},{1,7},{3,5},{5,3},{7,1},{8,14},{10,12},{12... | collective-permute-start | bytes 786440 | tf_op jit(solution)/shard_map/ppermute | solution.py:25
  83.1 1.3 %pad_maximum_fusion.own2_ref = f32[4,4,192,128]{3,2,1,0:T(8,128)S(1)} fusion(f32[1,4,192,128]{3,2,1,0:T(8,128)} %bitcast.61, f32[1,4,192,128]{3,2,1,0:T(8,128)} %bitcast.32, f32[1,4,192,128]{3,2,1,0:T(8,128)} %bitcast.31, f32[1,4,192,128]{3,2,1,0:T(8,128)S(1)} %bitcast.55), kind=kLoop, calls=%fused_computation | loop fusion | flops 1179648 | bytes 3145728 | tf_op jit(solution)/shard_map/stack | solution.py:245
  85.2 3.1 %collective-permute-done.2 = f32[2,4,64,128]{3,2,1,0:T(8,128)} collective-permute-done((f32[2,4,64,128]{3,2,1,0:T(8,128)}, f32[2,4,64,128]{3,2,1,0:T(8,128)}, u32[]{:S(2)}, u32[]{:S(2)}) %collective-permute-start.2) | collective-permute-done | bytes 262176 | tf_op jit(solution)/shard_map/ppermute | solution.py:25
  88.3 12.1 %collective-permute-start.8 = (f32[4,4,192,128]{3,2,1,0:T(8,128)S(1)}, f32[4,4,192,128]{3,2,1,0:T(8,128)}, u32[]{:S(2)}, u32[]{:S(2)}) collective-permute-start(f32[4,4,192,128]{3,2,1,0:T(8,128)S(1)} %pad_maximum_fusion.own2_ref), channel_id=1, source_target_pairs={{0,1},{1,0},{2,3},{3,2},{4,5},{5,4},{6,7},{7,6},{8,9},{9,8},{10,11... | collective-permute-start | bytes 4718600 | tf_op jit(solution)/shard_map/ppermute | solution.py:25
  100.5 2.2 %convert_element_type.29 = f32[512,18,32]{0,2,1:T(8,128)} convert(bf16[512,18,32]{0,2,1:T(8,128)(2,1)} %param.8) | non-fusion elementwise | flops 294912 | bytes 1769472 | tf_op jit(solution)/shard_map/convert_element_type | solution.py:255
  102.9 1.4 %pad_maximum_fusion.1.own1_ref = f32[4,2,4,64,128]{4,3,2,1,0:T(8,128)S(1)} fusion(f32[1,2,4,64,128]{4,3,2,1,0:T(8,128)} %bitcast.19, f32[1,2,4,64,128]{4,3,2,1,0:T(8,128)} %bitcast.17, f32[1,2,4,64,128]{4,3,2,1,0:T(8,128)} %bitcast.15, f32[1,2,4,64,128]{4,3,2,1,0:T(8,128)S(1)} %bitcast.56), kind=kLoop, calls=%fused_computation.3 | loop fusion | flops 786432 | bytes 2097152 | tf_op jit(solution)/shard_map/stack | solution.py:245
  105.1 1.4 %pad_maximum_fusion.2.own3_ref = f32[4,4,128,128]{3,2,1,0:T(8,128)S(1)} fusion(f32[1,4,128,128]{3,2,1,0:T(8,128)} %bitcast.41, f32[1,4,128,128]{3,2,1,0:T(8,128)} %bitcast.40, f32[1,4,128,128]{3,2,1,0:T(8,128)} %bitcast.39, f32[1,4,128,128]{3,2,1,0:T(8,128)} %bitcast.37), kind=kLoop, calls=%fused_computation.4 | loop fusion | flops 786432 | bytes 2097152 | tf_op jit(solution)/shard_map/stack | solution.py:245
  106.5 1.8 %collective-permute-start.15 = (f32[4,4,128,128]{3,2,1,0:T(8,128)S(1)}, f32[4,4,128,128]{3,2,1,0:T(8,128)S(1)}, u32[]{:S(2)}, u32[]{:S(2)}) collective-permute-start(f32[4,4,128,128]{3,2,1,0:T(8,128)S(1)} %pad_maximum_fusion.2.own3_ref), channel_id=1, source_target_pairs={{0,1},{1,0},{2,3},{3,2},{4,5},{5,4},{6,7},{7,6},{8,9},{9,8},{10,11... | collective-permute-start | bytes 3145736 | tf_op jit(solution)/shard_map/ppermute | solution.py:25
  109.1 2.2 %copy-done.4 = bf16[512,4096]{1,0:T(8,128)(2,1)S(1)} copy-done((bf16[512,4096]{1,0:T(8,128)(2,1)S(1)}, bf16[512,4096]{1,0:T(8,128)(2,1)}, u32[]{:S(2)}) %copy-start.4) | copy-done | bytes 4194328
  111.3 12.8 %local_attention.1.local_ref = f32[32,64,512]{2,1,0:T(8,128)S(1)} custom-call(bf16[512,4096]{1,0:T(8,128)(2,1)S(1)} %copy-done.4, bf16[512,4096]{1,0:T(8,128)(2,1)S(1)} %copy-done.1, bf16[512,2048]{1,0:T(8,128)(2,1)S(1)} %copy-done.3, f32[32,18,512]{2,1,0:T(8,128)S(1)} %fusion.lw_ref, bf16[32,64,128]{2,1,0:T(8,128)(2,1)S(1)} %get-tuple-element.7.first_ref), custom_call_target="tpu_custom_call" | custom-call | flops 8589934592 | bytes 16777216 | tf_op jit(solution)/shard_map/local_attention/pallas_call | solution.py:131
  124.1 10.2 %finish.1 = bf16[512,2048]{1,0:T(8,128)(2,1)} custom-call(s32[2]{0:T(128)S(1)} %pad_add_fusion.place_ref, bf16[512,4096]{1,0:T(8,128)(2,1)S(1)} %copy-done.5, f32[32,64,512]{2,1,0:T(8,128)S(1)} %local_attention.1.local_ref, f32[32,18,512]{2,1,0:T(8,128)S(1)} %fusion.lw_ref, f32[1,2048]{1,0:T(1,128)S(1)} %bitcast.48, ...), custom_call_target="tpu_custom_call" | custom-call | flops 9663676416 | bytes 20971520 | tf_op jit(solution)/shard_map/finish/pallas_call | solution.py:221
  (62 shorter events, 7.0 us)
Async XLA Ops:
  0.0 2.2 %copy-start = (bf16[512,4096]{1,0:T(8,128)(2,1)S(1)}, bf16[512,4096]{1,0:T(8,128)(2,1)}, u32[]{:S(2)}) copy-start(bf16[512,4096]{1,0:T(8,128)(2,1)} %k_ref.3) | copy-start | bytes 12582916
  2.2 1.6 %copy-start.2 = (bf16[512,2048]{1,0:T(8,128)(2,1)S(1)}, bf16[512,2048]{1,0:T(8,128)(2,1)}, u32[]{:S(2)}) copy-start(bf16[512,2048]{1,0:T(8,128)(2,1)} %v_ref.3) | copy-start | bytes 6291460
  6.7 5.6 %collective-permute-start = (f32[32,64,128]{2,1,0:T(8,128)S(1)}, f32[32,64,128]{2,1,0:T(8,128)S(1)}, u32[]{:S(2)}, u32[]{:S(2)}) collective-permute-start(f32[32,64,128]{2,1,0:T(8,128)S(1)} %get-tuple-element.8), channel_id=1, source_target_pairs={{0,1},{1,0},{2,3},{3,2},{4,5},{5,4},{6,7},{7,6},{8,9},{9,8},{10,11... | collective-permute-start | bytes 3145736 | tf_op jit(solution)/shard_map/ppermute | solution.py:25
  13.1 12.7 %all-to-all-start = ((f32[4,256,128]{2,1,0:T(8,128)}), f32[4,256,128]{2,1,0:T(8,128)S(1)}, u32[]{:S(2)}, u32[]{:S(2)}) async-start(f32[4,256,128]{2,1,0:T(8,128)} %bitcast.12), calls=%async_computation | async-start | bytes 1048576 | tf_op jit(solution)/shard_map/all_to_all | solution.py:263
  41.9 14.1 %all-to-all-start.2 = ((f32[8,3,32,128]{3,2,1,0:T(8,128)}), f32[8,3,32,128]{3,2,1,0:T(8,128)S(1)}, u32[]{:S(2)}, u32[]{:S(2)}) async-start(f32[8,3,32,128]{3,2,1,0:T(8,128)} %pad_maximum_fusion.3), calls=%async_computation.2 | async-start | bytes 786432 | tf_op jit(solution)/shard_map/all_to_all | solution.py:284
  45.4 4.0 %collective-permute-start.11 = (f32[32,128]{1,0:T(8,128)S(1)}, f32[32,128]{1,0:T(8,128)S(1)}, u32[]{:S(2)}, u32[]{:S(2)}) collective-permute-start(f32[32,128]{1,0:T(8,128)S(1)} %fusion.1), channel_id=1, source_target_pairs={{0,192},{64,128},{128,64},{192,0},{1,193},{65,129},{129,65},{193,1... | collective-permute-start | bytes 49160 | tf_op jit(solution)/shard_map/ppermute | solution.py:25
  48.2 4.1 %collective-permute-start.10 = (f32[32,128]{1,0:T(8,128)S(1)}, f32[32,128]{1,0:T(8,128)S(1)}, u32[]{:S(2)}, u32[]{:S(2)}) collective-permute-start(f32[32,128]{1,0:T(8,128)S(1)} %fusion.1), channel_id=1, source_target_pairs={{0,128},{64,192},{128,0},{192,64},{1,129},{65,193},{129,1},{193,65... | collective-permute-start | bytes 49160 | tf_op jit(solution)/shard_map/ppermute | solution.py:25
  48.6 3.8 %collective-permute-start.9 = (f32[32,128]{1,0:T(8,128)S(1)}, f32[32,128]{1,0:T(8,128)S(1)}, u32[]{:S(2)}, u32[]{:S(2)}) collective-permute-start(f32[32,128]{1,0:T(8,128)S(1)} %fusion.1), channel_id=1, source_target_pairs={{0,64},{64,0},{128,192},{192,128},{1,65},{65,1},{129,193},{193,129... | collective-permute-start | bytes 49160 | tf_op jit(solution)/shard_map/ppermute | solution.py:25
  56.8 23.6 %all-to-all-start.3 = ((f32[8,2,32,128]{3,2,1,0:T(8,128)}), f32[8,2,32,128]{3,2,1,0:T(8,128)}, u32[]{:S(2)}, u32[]{:S(2)}) async-start(f32[8,2,32,128]{3,2,1,0:T(8,128)} %broadcast_in_dim.22), calls=%async_computation.3 | async-start | bytes 524288 | tf_op jit(solution)/shard_map/all_to_all | solution.py:286
  60.8 19.5 %collective-permute-start.7 = (f32[4,192,128]{2,1,0:T(8,128)S(1)}, f32[4,192,128]{2,1,0:T(8,128)S(1)}, u32[]{:S(2)}, u32[]{:S(2)}) collective-permute-start(f32[4,192,128]{2,1,0:T(8,128)S(1)} %bitcast.52), channel_id=1, source_target_pairs={{0,6},{2,4},{4,2},{6,0},{1,7},{3,5},{5,3},{7,1},{8,14},{10,12},{12... | collective-permute-start | bytes 1179656 | tf_op jit(solution)/shard_map/ppermute | solution.py:25
  61.8 18.5 %collective-permute-start.6 = (f32[4,192,128]{2,1,0:T(8,128)S(1)}, f32[4,192,128]{2,1,0:T(8,128)}, u32[]{:S(2)}, u32[]{:S(2)}) collective-permute-start(f32[4,192,128]{2,1,0:T(8,128)S(1)} %bitcast.53), channel_id=1, source_target_pairs={{0,4},{2,6},{4,0},{6,2},{1,5},{3,7},{5,1},{7,3},{8,12},{10,14},{12... | collective-permute-start | bytes 1179656 | tf_op jit(solution)/shard_map/ppermute | solution.py:25
  63.0 20.0 %collective-permute-start.5 = (f32[4,192,128]{2,1,0:T(8,128)S(1)}, f32[4,192,128]{2,1,0:T(8,128)}, u32[]{:S(2)}, u32[]{:S(2)}) collective-permute-start(f32[4,192,128]{2,1,0:T(8,128)S(1)} %bitcast.54), channel_id=1, source_target_pairs={{0,2},{2,0},{4,6},{6,4},{1,3},{3,1},{5,7},{7,5},{8,10},{10,8},{12,... | collective-permute-start | bytes 1179656 | tf_op jit(solution)/shard_map/ppermute | solution.py:25
  64.9 19.5 %collective-permute-start.1 = (f32[2,4,64,128]{3,2,1,0:T(8,128)}, f32[2,4,64,128]{3,2,1,0:T(8,128)}, u32[]{:S(2)}, u32[]{:S(2)}) collective-permute-start(f32[2,4,64,128]{3,2,1,0:T(8,128)} %bitcast.14), channel_id=1, source_target_pairs={{0,2},{2,0},{4,6},{6,4},{1,3},{3,1},{5,7},{7,5},{8,10},{10,8},{12,... | collective-permute-start | bytes 786440 | tf_op jit(solution)/shard_map/ppermute | solution.py:25
  65.9 22.4 %collective-permute-start.2 = (f32[2,4,64,128]{3,2,1,0:T(8,128)}, f32[2,4,64,128]{3,2,1,0:T(8,128)}, u32[]{:S(2)}, u32[]{:S(2)}) collective-permute-start(f32[2,4,64,128]{3,2,1,0:T(8,128)} %bitcast.16), channel_id=1, source_target_pairs={{0,4},{2,6},{4,0},{6,2},{1,5},{3,7},{5,1},{7,3},{8,12},{10,14},{12... | collective-permute-start | bytes 786440 | tf_op jit(solution)/shard_map/ppermute | solution.py:25
  80.4 2.7 %copy-start.9 = (f32[4,192,128]{2,1,0:T(8,128)}, f32[4,192,128]{2,1,0:T(8,128)S(1)}, u32[]{:S(2)}) copy-start(f32[4,192,128]{2,1,0:T(8,128)S(1)} %collective-permute-done.7) | copy-start | bytes 1179652
  80.4 22.5 %collective-permute-start.3 = (f32[2,4,64,128]{3,2,1,0:T(8,128)}, f32[2,4,64,128]{3,2,1,0:T(8,128)}, u32[]{:S(2)}, u32[]{:S(2)}) collective-permute-start(f32[2,4,64,128]{3,2,1,0:T(8,128)} %bitcast.18), channel_id=1, source_target_pairs={{0,6},{2,4},{4,2},{6,0},{1,7},{3,5},{5,3},{7,1},{8,14},{10,12},{12... | collective-permute-start | bytes 786440 | tf_op jit(solution)/shard_map/ppermute | solution.py:25
  80.4 24.7 %collective-permute-start.14 = (f32[4,128,128]{2,1,0:T(8,128)}, f32[4,128,128]{2,1,0:T(8,128)}, u32[]{:S(2)}, u32[]{:S(2)}) collective-permute-start(f32[4,128,128]{2,1,0:T(8,128)} %bitcast.38), channel_id=1, source_target_pairs={{0,6},{2,4},{4,2},{6,0},{1,7},{3,5},{5,3},{7,1},{8,14},{10,12},{12... | collective-permute-start | bytes 786440 | tf_op jit(solution)/shard_map/ppermute | solution.py:25
  83.0 22.1 %collective-permute-start.13 = (f32[4,128,128]{2,1,0:T(8,128)}, f32[4,128,128]{2,1,0:T(8,128)}, u32[]{:S(2)}, u32[]{:S(2)}) collective-permute-start(f32[4,128,128]{2,1,0:T(8,128)} %bitcast.38), channel_id=1, source_target_pairs={{0,4},{2,6},{4,0},{6,2},{1,5},{3,7},{5,1},{7,3},{8,12},{10,14},{12... | collective-permute-start | bytes 786440 | tf_op jit(solution)/shard_map/ppermute | solution.py:25
  83.1 17.4 %copy-start.10 = (bf16[2048]{0:T(1024)(128)(2,1)S(1)}, bf16[2048]{0:T(1024)(128)(2,1)}, u32[]{:S(2)}) copy-start(bf16[2048]{0:T(1024)(128)(2,1)} %param.9) | copy-start | bytes 12292
  84.4 18.4 %copy-start.7 = (f32[1,256,128]{2,1,0:T(8,128)S(1)}, f32[1,256,128]{2,1,0:T(8,128)}, u32[]{:S(2)}) copy-start(f32[1,256,128]{2,1,0:T(8,128)} %get-tuple-element.17) | copy-start | bytes 393220
  84.4 18.4 %copy-start.8 = (f32[1,256,128]{2,1,0:T(8,128)S(1)}, f32[1,256,128]{2,1,0:T(8,128)}, u32[]{:S(2)}) copy-start(f32[1,256,128]{2,1,0:T(8,128)} %get-tuple-element.21) | copy-start | bytes 393220
  84.4 20.7 %collective-permute-start.12 = (f32[4,128,128]{2,1,0:T(8,128)}, f32[4,128,128]{2,1,0:T(8,128)}, u32[]{:S(2)}, u32[]{:S(2)}) collective-permute-start(f32[4,128,128]{2,1,0:T(8,128)} %bitcast.38), channel_id=1, source_target_pairs={{0,2},{2,0},{4,6},{6,4},{1,3},{3,1},{5,7},{7,5},{8,10},{10,8},{12,... | collective-permute-start | bytes 786440 | tf_op jit(solution)/shard_map/ppermute | solution.py:25
  88.3 35.8 %collective-permute-start.8 = (f32[4,4,192,128]{3,2,1,0:T(8,128)S(1)}, f32[4,4,192,128]{3,2,1,0:T(8,128)}, u32[]{:S(2)}, u32[]{:S(2)}) collective-permute-start(f32[4,4,192,128]{3,2,1,0:T(8,128)S(1)} %pad_maximum_fusion.own2_ref), channel_id=1, source_target_pairs={{0,1},{1,0},{2,3},{3,2},{4,5},{5,4},{6,7},{7,6},{8,9},{9,8},{10,11... | collective-permute-start | bytes 4718600 | tf_op jit(solution)/shard_map/ppermute | solution.py:25
  102.8 5.6 %copy-start.6 = (f32[512,18,32]{0,2,1:T(8,128)S(1)}, f32[512,18,32]{0,2,1:T(8,128)}, u32[]{:S(2)}) copy-start(f32[512,18,32]{0,2,1:T(8,128)} %convert_element_type.29) | copy-start | bytes 3538948
  102.8 6.2 %copy-start.3 = (bf16[512,2048]{1,0:T(8,128)(2,1)S(1)}, bf16[512,2048]{1,0:T(8,128)(2,1)}, u32[]{:S(2)}) copy-start(bf16[512,2048]{1,0:T(8,128)(2,1)} %v_ref.3) | copy-start | bytes 6291460
  104.2 19.9 %collective-permute-start.4 = (f32[4,2,4,64,128]{4,3,2,1,0:T(8,128)S(1)}, f32[4,2,4,64,128]{4,3,2,1,0:T(8,128)S(1)}, u32[]{:S(2)}, u32[]{:S(2)}) collective-permute-start(f32[4,2,4,64,128]{4,3,2,1,0:T(8,128)S(1)} %pad_maximum_fusion.1.own1_ref), channel_id=1, source_target_pairs={{0,1},{1,0},{2,3},{3,2},{4,5},{5,4},{6,7},{7,6},{8,9},{9,8},{10,11... | collective-permute-start | bytes 3145736 | tf_op jit(solution)/shard_map/ppermute | solution.py:25
  105.1 4.0 %copy-start.1 = (bf16[512,4096]{1,0:T(8,128)(2,1)S(1)}, bf16[512,4096]{1,0:T(8,128)(2,1)}, u32[]{:S(2)}) copy-start(bf16[512,4096]{1,0:T(8,128)(2,1)} %k_ref.3) | copy-start | bytes 12582916
  106.5 17.6 %collective-permute-start.15 = (f32[4,4,128,128]{3,2,1,0:T(8,128)S(1)}, f32[4,4,128,128]{3,2,1,0:T(8,128)S(1)}, u32[]{:S(2)}, u32[]{:S(2)}) collective-permute-start(f32[4,4,128,128]{3,2,1,0:T(8,128)S(1)} %pad_maximum_fusion.2.own3_ref), channel_id=1, source_target_pairs={{0,1},{1,0},{2,3},{3,2},{4,5},{5,4},{6,7},{7,6},{8,9},{9,8},{10,11... | collective-permute-start | bytes 3145736 | tf_op jit(solution)/shard_map/ppermute | solution.py:25
  109.1 2.2 %copy-start.4 = (bf16[512,4096]{1,0:T(8,128)(2,1)S(1)}, bf16[512,4096]{1,0:T(8,128)(2,1)}, u32[]{:S(2)}) copy-start(bf16[512,4096]{1,0:T(8,128)(2,1)} %q_ref.3) | copy-start | bytes 12582916
  111.3 12.8 %copy-start.5 = (bf16[512,4096]{1,0:T(8,128)(2,1)S(1)}, bf16[512,4096]{1,0:T(8,128)(2,1)}, u32[]{:S(2)}) copy-start(bf16[512,4096]{1,0:T(8,128)(2,1)} %q_ref.3) | copy-start | bytes 12582916

commit v2 on v0

v2 whole, which is shorter than its diff:
```python
import functools

import jax
import jax.numpy as jnp
from jax import lax
from jax.experimental import pallas as pl
from jax.experimental.pallas import tpu as pltpu
from jax.sharding import Mesh, PartitionSpec as P

HEADS = 32
DK = 128
DV = 64
TOK = 512
HALF = 256
TILE = 128
LOCAL = 10
LEVELS = 18
GROUP = 4
STEPS = HEADS // GROUP
SIDE = HEADS // 2
EPS = 1e-06
F32 = jnp.float32
BF16 = jnp.bfloat16


def xor_permute(value, axis, mask):
    size = lax.axis_size(axis)
    return lax.ppermute(value, axis, [(i, i ^ mask) for i in range(size)])


def dot(a, b):
    return jnp.dot(a, b, preferred_element_type=F32)


def dot_t0(a, b):
    return lax.dot_general(a, b, (((0,), (0,)), ((), ())), preferred_element_type=F32)


def dot_t1(a, b):
    return lax.dot_general(a, b, (((1,), (1,)), ((), ())), preferred_element_type=F32)


def state_kernel(other, place_ref, k_hbm, v_hbm, s_hbm, k_buf, v_buf, s_buf, k_sem, v_sem, s_sem):
    side = place_ref[0] ^ other
    chunks = SIDE // GROUP

    def copies(i):
        at = side * chunks + i
        k_at = pl.ds(pl.multiple_of(at * GROUP * DK, GROUP * DK), GROUP * DK)
        v_at = pl.ds(pl.multiple_of(at * GROUP * DV, GROUP * DV), GROUP * DV)
        return (
            pltpu.make_async_copy(k_hbm.at[:, k_at], k_buf.at[i], k_sem.at[i]),
            pltpu.make_async_copy(v_hbm.at[:, v_at], v_buf.at[i], v_sem.at[i]),
        )

    def back(i):
        heads = pl.ds(i * GROUP, GROUP)
        return pltpu.make_async_copy(s_buf.at[heads], s_hbm.at[heads], s_sem.at[i])

    for i in range(chunks):
        for copy in copies(i):
            copy.start()
    for i in range(chunks):
        for copy in copies(i):
            copy.wait()
        for pair in range(GROUP // 2):
            v = v_buf[i, :, pair * 2 * DV : (pair + 1) * 2 * DV]
            k = k_buf[i, :, pair * 2 * DK : (pair + 1) * 2 * DK]
            both = dot_t0(v, k)
            for j in range(2):
                s_buf[i * GROUP + 2 * pair + j] = both[j * DV : (j + 1) * DV, j * DK : (j + 1) * DK]
        back(i).start()
    for i in range(chunks):
        back(i).wait()


def block_state(place, keys, values, other):
    hbm = pl.BlockSpec(memory_space=pl.ANY)
    chunks = SIDE // GROUP
    return pl.pallas_call(
        functools.partial(state_kernel, other),
        in_specs=[pl.BlockSpec(memory_space=pltpu.SMEM), hbm, hbm],
        out_specs=hbm,
        out_shape=jax.ShapeDtypeStruct((SIDE, DV, DK), F32),
        scratch_shapes=[
            pltpu.VMEM((chunks, TOK, GROUP * DK), BF16),
            pltpu.VMEM((chunks, TOK, GROUP * DV), BF16),
            pltpu.VMEM((SIDE, DV, DK), F32),
            pltpu.SemaphoreType.DMA((chunks,)),
            pltpu.SemaphoreType.DMA((chunks,)),
            pltpu.SemaphoreType.DMA((chunks,)),
        ],
        cost_estimate=pl.CostEstimate(flops=1 << 28, bytes_accessed=4 << 20, transcendentals=0),
        compiler_params=pltpu.CompilerParams(vmem_limit_bytes=60 << 20),
        name="block_state",
    )(place, keys, values)


def diagonal_weight(rows):
    group = lax.broadcasted_iota(jnp.int32, (16, TILE), 0)
    lane = lax.broadcasted_iota(jnp.int32, (16, TILE), 1)
    other = lane >> 3
    xored = group ^ other
    coarse = jnp.zeros((16, TILE), F32)
    for level in range(4, 8):
        coarse = jnp.where((xored >> (level - 4)) == 1, rows[level], coarse)
    coarse = jnp.where(other > group, coarse, 0.0)
    sub = lax.broadcasted_iota(jnp.int32, (8, TILE), 0)
    low = lax.broadcasted_iota(jnp.int32, (8, TILE), 1)
    place = low & 7
    near = sub ^ place
    fine = jnp.broadcast_to(rows[0], (8, TILE))
    for level in range(1, 4):
        fine = jnp.where((near >> (level - 1)) == 1, rows[level], fine)
    fine = jnp.where(place >= sub, fine, 0.0)
    owner = low >> 3
    return jnp.concatenate(
        [
            jnp.where(owner == i, fine, jnp.broadcast_to(coarse[i : i + 1], (8, TILE)))
            for i in range(16)
        ],
        axis=0,
    )


def local_kernel(place_ref, q_ref, k_ref, v_ref, lw_ref, o_ref, w_ref):
    step = pl.program_id(0)

    for r in range(SIDE // GROUP):

        @pl.when(step % 4 == r)
        def _():
            w_ref[...] = lw_ref[:LOCAL, r * GROUP : (r + 1) * GROUP].astype(F32)

    def row(level, head, at, size):
        return w_ref[level, head : head + 1, at : at + size]

    v_t = [v_ref[:, p * 2 * DV : (p + 1) * 2 * DV].T for p in range(GROUP // 2)]
    parts = {}
    for head in range(GROUP):
        cols = slice(head * DK, (head + 1) * DK)
        v_head = v_t[head // 2][(head % 2) * DV : (head % 2 + 1) * DV]
        for block in range(2):
            at = block * HALF
            q = q_ref[at : at + HALF, cols]
            k = k_ref[at : at + HALF, cols]
            if block:
                first = dot(v_head[:, :HALF], k_ref[:HALF, cols]).astype(BF16)
                scores = dot_t1(jnp.concatenate([k, first], axis=0), q)
                extra = scores[HALF:] * row(9, head, at, HALF)
            else:
                scores = dot_t1(k, q)
                extra = None
            tiles = []
            for tile in range(2):
                part = slice(tile * TILE, (tile + 1) * TILE)
                rows = [row(l, head, at + tile * TILE, TILE) for l in range(8)]
                tiles.append((scores[part, part] * diagonal_weight(rows)).astype(BF16))
            upper = (scores[:TILE, TILE:HALF] * row(8, head, at + TILE, TILE)).astype(BF16)
            weighted = jnp.concatenate(
                [
                    jnp.concatenate([tiles[0], upper], axis=1),
                    jnp.concatenate([jnp.zeros((TILE, TILE), BF16), tiles[1]], axis=1),
                ],
                axis=0,
            )
            parts[head, block] = (v_head[:, at : at + HALF], weighted, extra)
    for (head, block), (v_part, weighted, extra) in parts.items():
        out = dot(v_part, weighted)
        o_ref[head, :, block * HALF : (block + 1) * HALF] = out if extra is None else out + extra


def local_attention(place, queries, keys, values, level_rows):
    return pl.pallas_call(
        local_kernel,
        grid_spec=pltpu.PrefetchScalarGridSpec(
            num_scalar_prefetch=1,
            grid=(STEPS,),
            in_specs=[
                pl.BlockSpec((TOK, GROUP * DK), lambda i, p: (0, i)),
                pl.BlockSpec((TOK, GROUP * DK), lambda i, p: (0, i)),
                pl.BlockSpec((TOK, GROUP * DV), lambda i, p: (0, i)),
                pl.BlockSpec((LEVELS, SIDE, TOK), lambda i, p: (0, i // 4, 0)),
            ],
            out_specs=pl.BlockSpec((GROUP, DV, TOK), lambda i, p: (i, 0, 0)),
            scratch_shapes=[pltpu.VMEM((LOCAL, GROUP, TOK), F32)],
        ),
        out_shape=jax.ShapeDtypeStruct((HEADS, DV, TOK), F32),
        cost_estimate=pl.CostEstimate(flops=8 << 30, bytes_accessed=16 << 20, transcendentals=0),
        compiler_params=pltpu.CompilerParams(vmem_limit_bytes=60 << 20),
        name="local_attention",
    )(place, queries, keys, values, level_rows)


def readout_kernel(base, counts, last, *refs):
    refs = list(refs)
    place_ref, q_ref, sum_ref, lw_ref = refs[:4]
    refs = refs[4:]
    gain_ref = refs.pop(0) if last else None
    sides = [(refs[2 * i], refs[2 * i + 1]) for i in range(len(counts))]
    o_ref, lhs_ref, w_ref = refs[-3:]
    step = pl.program_id(0)
    levels = sum(counts)

    for r in range(SIDE // GROUP):

        @pl.when(step % 4 == r)
        def _():
            for l in range(levels):
                flag = ((place_ref[2] >> (base + l)) & 1).astype(F32)
                rows = lw_ref[LOCAL + base + l, r * GROUP : (r + 1) * GROUP]
                w_ref[l] = rows.astype(F32) * flag

    def stage(which):
        at = 0
        for pair, count in zip(sides, counts):
            for level in range(count):
                for j in range(GROUP):
                    lhs_ref[j, at : at + DV] = pair[which][0, level, j].astype(BF16)
                at += DV

    @pl.when(step < STEPS // 2)
    def _():
        stage(0)

    @pl.when(step >= STEPS // 2)
    def _():
        stage(1)

    for pair in range(GROUP // 2):
        for block in range(2):
            at = slice(block * HALF, (block + 1) * HALF)
            outs = []
            for j in range(2):
                head = 2 * pair + j
                q = q_ref[at, head * DK : (head + 1) * DK]
                r = dot_t1(lhs_ref[head], q)
                acc = sum_ref[head, :, at]
                for l in range(levels):
                    weight = w_ref[l, head : head + 1, at]
                    acc = acc + r[l * DV : (l + 1) * DV] * weight
                if last:
                    mean = jnp.mean(acc * acc, axis=0, keepdims=True)
                    outs.append(acc * lax.rsqrt(mean + EPS))
                else:
                    o_ref[head, :, at] = acc
            if last:
                flat = jnp.concatenate(outs, axis=0).T
                cols = slice(pair * 2 * DV, (pair + 1) * 2 * DV)
                o_ref[at, cols] = (flat * gain_ref[:, cols]).astype(BF16)


def readout(place, queries, total, level_rows, base, own, oth, distance, gain=None):
    last = gain is not None
    counts = tuple(o.shape[1] for o in own)
    levels = sum(counts)

    def group(i, place):
        return 4 * (place[0] ^ (i // 4)) + i % 4

    def pieces(array, second, by_distance):
        def index(i, place):
            at = jnp.maximum(i - 4, 0) if second else jnp.minimum(i, 3)
            return (at ^ place[1] if by_distance else at, 0, 0, 0, 0)

        return pl.BlockSpec((1,) + array.shape[1:], index)

    heads = pl.BlockSpec((GROUP, DV, TOK), lambda i, p: (group(i, p), 0, 0))
    flat = pl.BlockSpec((TOK, GROUP * DV), lambda i, p: (0, group(i, p)))
    args = [queries, total, level_rows]
    specs = [
        pl.BlockSpec((TOK, GROUP * DK), lambda i, p: (0, group(i, p))),
        heads,
        pl.BlockSpec((LEVELS, SIDE, TOK), lambda i, p: (0, p[0] ^ (i // 4), 0)),
    ]
    if last:
        args.append(gain)
        specs.append(pl.BlockSpec((1, GROUP * DV), lambda i, p: (0, group(i, p))))
    for mine, theirs, by_distance in zip(own, oth, distance):
        args += [mine, theirs]
        specs += [pieces(mine, False, by_distance), pieces(theirs, True, by_distance)]
    return pl.pallas_call(
        functools.partial(readout_kernel, base, counts, last),
        grid_spec=pltpu.PrefetchScalarGridSpec(
            num_scalar_prefetch=1,
            grid=(STEPS,),
            in_specs=specs,
            out_specs=flat if last else heads,
            scratch_shapes=[
                pltpu.VMEM((GROUP, levels * DV, DK), BF16),
                pltpu.VMEM((levels, GROUP, TOK), F32),
            ],
        ),
        out_shape=jax.ShapeDtypeStruct((TOK, HEADS * DV), BF16)
        if last
        else jax.ShapeDtypeStruct((HEADS, DV, TOK), F32),
        cost_estimate=pl.CostEstimate(flops=levels << 30, bytes_accessed=16 << 20, transcendentals=0),
        compiler_params=pltpu.CompilerParams(vmem_limit_bytes=24 << 20),
        name="readout_last" if last else "readout",
    )(place, *args)


def after(value, *others):
    return lax.optimization_barrier((value, *others))[0]


def row_exchange(payload):
    return lax.all_to_all(payload, "x", 0, 0, tiled=True)


def to_row(*levels):
    return row_exchange(jnp.broadcast_to(jnp.stack(levels)[None], (4, len(levels)) + levels[0].shape))


def sent(payload):
    return [payload] + [xor_permute(payload, "x", d) for d in range(1, 4)]


def on_device(queries, keys, values, level_weights, out_gain):
    core, x, z, y = (lax.axis_index(a) for a in ("c", "x", "z", "y"))
    block = ((y * 8 + z) * 4 + x) * 2 + core
    place = jnp.stack([core, x, block]).astype(jnp.int32)
    level_rows = jnp.transpose(level_weights, (1, 2, 0))
    gain = out_gain.astype(F32).reshape(1, HEADS * DV)

    give = block_state(place, keys, values, 1)
    zero_own = xor_permute(give, "c", 1)
    keep = block_state(after(place, give), keys, values, 0)
    half = keep + zero_own
    u = row_exchange(half.reshape(4, GROUP, DV, DK))
    zero_oth = xor_permute(after(keep, half), "c", 1)
    local = local_attention(after(place, half), queries, keys, values, level_rows)
    u, local = lax.optimization_barrier((u, local))
    t3 = (u[0] + u[1]) + (u[2] + u[3])
    l3 = xor_permute(t3, "z", 1)
    l1 = xor_permute(after(half, u), "x", 1)
    t4 = t3 + l3
    l4 = xor_permute(t4, "z", 2)
    t5 = after(t4 + l4, l1)
    l2 = xor_permute(half + l1, "x", 3)
    l5 = xor_permute(t5, "z", 4)
    own34 = to_row(l3, l4)
    t6 = t5 + l5
    p1, p2, p3 = (xor_permute(t6, "y", d) for d in (1, 2, 3))
    p1 = after(p1, l2)
    top = jnp.stack([l5, p1, p2 + p3])
    own567 = sent(top)
    early = [part.reshape(4, 1, GROUP, DV, DK) for part in (after(l1, t5), after(l2, top))]
    own = [zero_own.reshape(4, 1, GROUP, DV, DK)] + early
    oth = [zero_oth.reshape(4, 1, GROUP, DV, DK)] + [xor_permute(part, "c", 1) for part in early]
    own34 = after(own34, top)
    own.append(own34)
    oth.append(xor_permute(own34, "c", 1))
    mid = readout(place, queries, local, level_rows, 0, own, oth, [False] * 4)
    own567 = jnp.stack([after(part, mid) for part in own567])
    oth567 = xor_permute(own567, "c", 1)
    return readout(place, queries, mid, level_rows, 5, [own567], [oth567], [True], gain=gain)


def solution(mesh):
    wide = Mesh(mesh.devices.reshape(4, 8, 4, 2), ("y", "z", "x", "c"))
    split = ("y", "z", "x", "c")
    return jax.shard_map(
        on_device,
        mesh=wide,
        in_specs=(P(split, None), P(split, None), P(split, None), P(split, None, None), P()),
        out_specs=P(split, None),
        check_vma=False,
    )
```

time: 285 us -> 111 us (0.39)
  matrix products: 124 us -> 0 us
  waiting for transfers between devices: 121 us -> 36 us
  Pallas kernels: 0 us -> 31.5 us
  starting transfers between devices: 21.3 us -> 32.8 us
  other arithmetic: 11 us -> 4.77 us
    dot_general x19 -> x0, matrix products: 124 us -> none  [the longest x8 48.6 us: on_device(): jnp.einsum('jeu,eud->jed', query_matrix_rows, upper_half_state, preferred...]
    ppermute x8 -> x17, waiting for transfers between devices: 121 us -> 36 us  [xor_permute(): return lax.ppermute(value, axis, [(i, i ^ mask) for i in range(size)])]
    pallas_call x0 -> x5, Pallas kernels: none -> 31.5 us  [the longest x2 12.4 us: readout(): pl.pallas_call(functools.partial(readout_kernel, base, counts, last), gri...]
    all_to_all x0 -> x2, starting transfers between devices: none -> 7.27 us  [row_exchange(): return lax.all_to_all(payload, 'x', 0, 0, tiled=True)]
    ppermute x8 -> x17, starting transfers between devices: 21.3 us -> 25.5 us  [xor_permute(): return lax.ppermute(value, axis, [(i, i ^ mask) for i in range(size)])]
  transfers between devices with their start and end apart: 8 -> 19, of which waited for: 7 -> 10; matrix products, arithmetic and copies ran while one was open for 34% -> 3% of each run, Pallas kernels for 0% -> 19%
where the time goes in v2:
time: 111 us
  waiting for transfers between devices  36 us (32%)
  starting transfers between devices  32.8 us (30%)
  Pallas kernels  31.5 us (28%)
  local copies, waits for them, and re-layouts  5.48 us (5%)
  other arithmetic  4.77 us (4%)
    ppermute x17, waiting for transfers between devices, xor_permute(): return lax.ppermute(value, axis, [(i, i ^ mask) for i in range(size)])  36 us
    ppermute x17, starting transfers between devices, xor_permute(): return lax.ppermute(value, axis, [(i, i ^ mask) for i in range(size)])  25.5 us
    pallas_call x2, Pallas kernels, readout(): pl.pallas_call(functools.partial(readout_kernel, base, counts, last), gri...  12.4 us
    pallas_call x1, Pallas kernels, local_attention(): pl.pallas_call(local_kernel, grid_spec=pltpu.PrefetchScalarGridSpec(num_s...  11.8 us
    all_to_all x2, starting transfers between devices, row_exchange(): return lax.all_to_all(payload, 'x', 0, 0, tiled=True)  7.27 us
    pallas_call x2, Pallas kernels, block_state(): pl.pallas_call(functools.partial(state_kernel, other), in_specs=[pl.Block...  7.27 us
    unnamed x12, local copies, waits for them, and re-layouts  4.39 us
  transfers between devices with their start and end apart: 19, of which 10 were waited for; matrix products, arithmetic and copies ran while one was open for 3% of the time, Pallas kernels for 19%

profile of v2, /device:TPU:1, one launch (start us, length us, event | category | flops | bytes accessed | tf_op | source)
XLA Modules:
  0.0 110.7 jit_solution(16947436684647294743)
XLA Ops:
  0.6 3.6 %block_state.2 = f32[16,64,128]{2,1,0:T(8,128)} custom-call(s32[3]{0:T(128)} %pad_add_fusion.place_ref.refs_0_, bf16[512,4096]{1,0:T(8,128)(2,1)} %k_ref.1, bf16[512,2048]{1,0:T(8,128)(2,1)} %v_ref.1), custom_call_target="tpu_custom_call" | custom-call | flops 268435456 | bytes 4194304 | tf_op jit(solution)/shard_map/block_state/pallas_call | solution.py:80
  4.2 3.3 %collective-permute-start = (f32[16,64,128]{2,1,0:T(8,128)}, f32[16,64,128]{2,1,0:T(8,128)S(1)}, u32[]{:S(2)}, u32[]{:S(2)}) collective-permute-start(f32[16,64,128]{2,1,0:T(8,128)} %block_state.2), channel_id=1, source_target_pairs={{0,1},{1,0},{2,3},{3,2},{4,5},{5,4},{6,7},{7,6},{8,9},{9,8},{10,11... | collective-permute-start | bytes 1572872 | tf_op jit(solution)/shard_map/ppermute | solution.py:28
  7.6 3.6 %block_state.3 = f32[16,64,128]{2,1,0:T(8,128)} custom-call(s32[3]{0:T(128)} %pad_add_fusion.place_ref.refs_0_, bf16[512,4096]{1,0:T(8,128)(2,1)} %k_ref.1, bf16[512,2048]{1,0:T(8,128)(2,1)} %v_ref.1), custom_call_target="tpu_custom_call" | custom-call | flops 268435456 | bytes 4194304 | tf_op jit(solution)/shard_map/block_state/pallas_call | solution.py:80
  11.2 1.9 %add.44 = f32[16,64,128]{2,1,0:T(8,128)} add(f32[16,64,128]{2,1,0:T(8,128)} %block_state.3, f32[16,64,128]{2,1,0:T(8,128)S(1)} %collective-permute-done) | non-fusion elementwise | flops 131072 | bytes 1572864 | tf_op jit(solution)/shard_map/add | solution.py:329
  13.1 3.5 %all-to-all-start = ((f32[4,4,64,128]{3,2,1,0:T(8,128)}), f32[4,4,64,128]{3,2,1,0:T(8,128)S(1)}, u32[]{:S(2)}, u32[]{:S(2)}) async-start(f32[4,4,64,128]{3,2,1,0:T(8,128)} %bitcast.3), calls=%async_computation | async-start | bytes 1048576 | tf_op jit(solution)/shard_map/all_to_all | solution.py:308
  16.6 11.8 %local_attention.1.refs_2_ = f32[32,64,512]{2,1,0:T(8,128)} custom-call(s32[3]{0:T(128)} %pad_add_fusion.place_ref.refs_0_, bf16[512,4096]{1,0:T(8,128)(2,1)} %refs_1_.3, bf16[512,4096]{1,0:T(8,128)(2,1)} %k_ref.1, bf16[512,2048]{1,0:T(8,128)(2,1)} %v_ref.1, bf16[18,32,512]{2,1,0:T(8,128)(2,1)} %bitcast.24), custom_call_target="tpu_custom_call" | custom-call | flops 8589934592 | bytes 16777216 | tf_op jit(solution)/shard_map/local_attention/pallas_call | solution.py:174
  28.9 1.5 %collective-permute-start.2 = (f32[16,64,128]{2,1,0:T(8,128)}, f32[16,64,128]{2,1,0:T(8,128)S(1)}, u32[]{:S(2)}, u32[]{:S(2)}) collective-permute-start(f32[16,64,128]{2,1,0:T(8,128)} %add.44), channel_id=1, source_target_pairs={{0,2},{2,0},{4,6},{6,4},{1,3},{3,1},{5,7},{7,5},{8,10},{10,8},{12,... | collective-permute-start | bytes 1572872 | tf_op jit(solution)/shard_map/ppermute | solution.py:28
  30.4 3.2 %collective-permute-done.3 = f32[4,64,128]{2,1,0:T(8,128)S(1)} collective-permute-done((f32[4,64,128]{2,1,0:T(8,128)S(1)}, f32[4,64,128]{2,1,0:T(8,128)S(1)}, u32[]{:S(2)}, u32[]{:S(2)}) %collective-permute-start.3) | collective-permute-done | bytes 131104 | tf_op jit(solution)/shard_map/ppermute | solution.py:28
  33.7 1.9 %collective-permute-start.4 = (f32[4,64,128]{2,1,0:T(8,128)S(1)}, f32[4,64,128]{2,1,0:T(8,128)S(1)}, u32[]{:S(2)}, u32[]{:S(2)}) collective-permute-start(f32[4,64,128]{2,1,0:T(8,128)S(1)} %fusion), channel_id=1, source_target_pairs={{0,16},{8,24},{16,0},{24,8},{32,48},{40,56},{48,32},{56,40},{1,17}... | collective-permute-start | bytes 393224 | tf_op jit(solution)/shard_map/ppermute | solution.py:28
  35.6 6.8 %collective-permute-done.4 = f32[4,64,128]{2,1,0:T(8,128)S(1)} collective-permute-done((f32[4,64,128]{2,1,0:T(8,128)S(1)}, f32[4,64,128]{2,1,0:T(8,128)S(1)}, u32[]{:S(2)}, u32[]{:S(2)}) %collective-permute-start.4) | collective-permute-done | bytes 131104 | tf_op jit(solution)/shard_map/ppermute | solution.py:28
  42.4 1.1 broadcast_in_dim.2
  43.5 3.8 %all-to-all-start.1 = ((f32[4,2,4,64,128]{4,3,2,1,0:T(8,128)}), f32[4,2,4,64,128]{4,3,2,1,0:T(8,128)S(1)}, u32[]{:S(2)}, u32[]{:S(2)}) async-start(f32[4,2,4,64,128]{4,3,2,1,0:T(8,128)} %broadcast_in_dim.2), calls=%async_computation.1 | async-start | bytes 2097152 | tf_op jit(solution)/shard_map/all_to_all | solution.py:308
  47.3 1.2 %add.51 = f32[16,64,128]{2,1,0:T(8,128)S(1)} add(f32[16,64,128]{2,1,0:T(8,128)} %add.44, f32[16,64,128]{2,1,0:T(8,128)S(1)} %collective-permute-done.2) | non-fusion elementwise | flops 131072 | bytes 1572864 | tf_op jit(solution)/shard_map/add | solution.py:340
  48.5 2.8 %collective-permute-start.6 = (f32[16,64,128]{2,1,0:T(8,128)S(1)}, f32[16,64,128]{2,1,0:T(8,128)S(1)}, u32[]{:S(2)}, u32[]{:S(2)}) collective-permute-start(f32[16,64,128]{2,1,0:T(8,128)S(1)} %add.51), channel_id=1, source_target_pairs={{0,6},{2,4},{4,2},{6,0},{1,7},{3,5},{5,3},{7,1},{8,14},{10,12},{12... | collective-permute-start | bytes 1572872 | tf_op jit(solution)/shard_map/ppermute | solution.py:28
  51.3 5.6 %collective-permute-start.7 = (f32[4,64,128]{2,1,0:T(8,128)S(1)}, f32[4,64,128]{2,1,0:T(8,128)S(1)}, u32[]{:S(2)}, u32[]{:S(2)}) collective-permute-start(f32[4,64,128]{2,1,0:T(8,128)S(1)} %add.50), channel_id=1, source_target_pairs={{0,32},{8,40},{16,48},{24,56},{32,0},{40,8},{48,16},{56,24},{1,33}... | collective-permute-start | bytes 393224 | tf_op jit(solution)/shard_map/ppermute | solution.py:28
  56.9 2.5 %collective-permute-done.7 = f32[4,64,128]{2,1,0:T(8,128)S(1)} collective-permute-done((f32[4,64,128]{2,1,0:T(8,128)S(1)}, f32[4,64,128]{2,1,0:T(8,128)S(1)}, u32[]{:S(2)}, u32[]{:S(2)}) %collective-permute-start.7) | collective-permute-done | bytes 131104 | tf_op jit(solution)/shard_map/ppermute | solution.py:28
  59.3 2.8 %collective-permute-start.10 = (f32[4,64,128]{2,1,0:T(8,128)S(1)}, f32[4,64,128]{2,1,0:T(8,128)S(1)}, u32[]{:S(2)}, u32[]{:S(2)}) collective-permute-start(f32[4,64,128]{2,1,0:T(8,128)S(1)} %add.52), channel_id=1, source_target_pairs={{0,192},{64,128},{128,64},{192,0},{1,193},{65,129},{129,65},{193,1... | collective-permute-start | bytes 393224 | tf_op jit(solution)/shard_map/ppermute | solution.py:28
  62.8 2.6 %collective-permute-done.10 = f32[4,64,128]{2,1,0:T(8,128)S(1)} collective-permute-done((f32[4,64,128]{2,1,0:T(8,128)S(1)}, f32[4,64,128]{2,1,0:T(8,128)S(1)}, u32[]{:S(2)}, u32[]{:S(2)}) %collective-permute-start.10) | collective-permute-done | bytes 131104 | tf_op jit(solution)/shard_map/ppermute | solution.py:28
  65.4 2.0 %collective-permute-done.9 = f32[4,64,128]{2,1,0:T(8,128)S(1)} collective-permute-done((f32[4,64,128]{2,1,0:T(8,128)S(1)}, f32[4,64,128]{2,1,0:T(8,128)S(1)}, u32[]{:S(2)}, u32[]{:S(2)}) %collective-permute-start.9) | collective-permute-done | bytes 131104 | tf_op jit(solution)/shard_map/ppermute | solution.py:28
  67.5 4.6 %collective-permute-done.6 = f32[16,64,128]{2,1,0:T(8,128)S(1)} collective-permute-done((f32[16,64,128]{2,1,0:T(8,128)S(1)}, f32[16,64,128]{2,1,0:T(8,128)S(1)}, u32[]{:S(2)}, u32[]{:S(2)}) %collective-permute-start.6) | collective-permute-done | bytes 524320 | tf_op jit(solution)/shard_map/ppermute | solution.py:28
  72.0 0.8 pad_maximum_fusion.1
  72.8 2.3 %collective-permute-start.12 = (f32[4,2,4,64,128]{4,3,2,1,0:T(8,128)S(1)}, f32[4,2,4,64,128]{4,3,2,1,0:T(8,128)S(1)}, u32[]{:S(2)}, u32[]{:S(2)}) collective-permute-start(f32[4,2,4,64,128]{4,3,2,1,0:T(8,128)S(1)} %all-to-all-done.1.refs_10_), channel_id=1, source_target_pairs={{0,1},{1,0},{2,3},{3,2},{4,5},{5,4},{6,7},{7,6},{8,9},{9,8},{10,11... | collective-permute-start | bytes 3145736 | tf_op jit(solution)/shard_map/ppermute | solution.py:28
  75.6 3.3 %collective-permute-done.1 = f32[16,64,128]{2,1,0:T(8,128)S(1)} collective-permute-done((f32[16,64,128]{2,1,0:T(8,128)}, f32[16,64,128]{2,1,0:T(8,128)S(1)}, u32[]{:S(2)}, u32[]{:S(2)}) %collective-permute-start.1) | collective-permute-done | bytes 524320 | tf_op jit(solution)/shard_map/ppermute | solution.py:28
  79.5 1.8 %collective-permute-start.15 = (f32[3,4,64,128]{3,2,1,0:T(8,128)}, f32[3,4,64,128]{3,2,1,0:T(8,128)S(1)}, u32[]{:S(2)}, u32[]{:S(2)}) collective-permute-start(f32[3,4,64,128]{3,2,1,0:T(8,128)} %pad_maximum_fusion.1), channel_id=1, source_target_pairs={{0,6},{2,4},{4,2},{6,0},{1,7},{3,5},{5,3},{7,1},{8,14},{10,12},{12... | collective-permute-start | bytes 1179656 | tf_op jit(solution)/shard_map/ppermute | solution.py:28
  81.4 2.2 %copy-done = bf16[512,4096]{1,0:T(8,128)(2,1)S(1)} copy-done((bf16[512,4096]{1,0:T(8,128)(2,1)S(1)}, bf16[512,4096]{1,0:T(8,128)(2,1)}, u32[]{:S(2)}) %copy-start) | copy-done | bytes 4194328
  83.5 2.2 %copy-done.3 = f32[32,64,512]{2,1,0:T(8,128)S(1)} copy-done((f32[32,64,512]{2,1,0:T(8,128)S(1)}, f32[32,64,512]{2,1,0:T(8,128)}, u32[]{:S(2)}) %copy-start.3) | copy-done | bytes 4194328
  85.7 5.9 %readout.1.refs_2_ = f32[32,64,512]{2,1,0:T(8,128)S(1)} custom-call(s32[3]{0:T(128)S(1)} %copy-done.2, bf16[512,4096]{1,0:T(8,128)(2,1)S(1)} %copy-done, f32[32,64,512]{2,1,0:T(8,128)S(1)} %copy-done.3, bf16[18,32,512]{2,1,0:T(8,128)(2,1)S(1)} %bitcast.25, f32[4,1,4,64,128]{4,3,2,1,0:T(8,128)S(1)} %bitcast.27, f32[4,1,4,64,128]{4,3,2,1,0:T(8,128)S(1)} %bitcast.33, ...), custom_call_target="tpu_custom_call" | custom-call | flops 5368709120 | bytes 16777216 | tf_op jit(solution)/shard_map/readout/pallas_call | solution.py:282
  91.7 2.5 %collective-permute-done.14 = f32[3,4,64,128]{3,2,1,0:T(8,128)S(1)} collective-permute-done((f32[3,4,64,128]{3,2,1,0:T(8,128)}, f32[3,4,64,128]{3,2,1,0:T(8,128)S(1)}, u32[]{:S(2)}, u32[]{:S(2)}) %collective-permute-start.14) | collective-permute-done | bytes 393248 | tf_op jit(solution)/shard_map/ppermute | solution.py:28
  94.2 5.5 %collective-permute-done.15 = f32[3,4,64,128]{3,2,1,0:T(8,128)S(1)} collective-permute-done((f32[3,4,64,128]{3,2,1,0:T(8,128)}, f32[3,4,64,128]{3,2,1,0:T(8,128)S(1)}, u32[]{:S(2)}, u32[]{:S(2)}) %collective-permute-start.15) | collective-permute-done | bytes 393248 | tf_op jit(solution)/shard_map/ppermute | solution.py:28
  99.8 1.4 %collective-permute-start.16 = (f32[4,3,4,64,128]{4,3,2,1,0:T(8,128)S(1)}, f32[4,3,4,64,128]{4,3,2,1,0:T(8,128)S(1)}, u32[]{:S(2)}, u32[]{:S(2)}) collective-permute-start(f32[4,3,4,64,128]{4,3,2,1,0:T(8,128)S(1)} %pad_maximum_fusion.refs_5_), channel_id=1, source_target_pairs={{0,1},{1,0},{2,3},{3,2},{4,5},{5,4},{6,7},{7,6},{8,9},{9,8},{10,11... | collective-permute-start | bytes 4718600 | tf_op jit(solution)/shard_map/ppermute | solution.py:28
  101.2 3.0 %collective-permute-done.16.refs_6_ = f32[4,3,4,64,128]{4,3,2,1,0:T(8,128)S(1)} collective-permute-done((f32[4,3,4,64,128]{4,3,2,1,0:T(8,128)S(1)}, f32[4,3,4,64,128]{4,3,2,1,0:T(8,128)S(1)}, u32[]{:S(2)}, u32[]{:S(2)}) %collective-permute-start.16) | collective-permute-done | bytes 1572896 | tf_op jit(solution)/shard_map/ppermute | solution.py:28
  104.2 6.5 %readout_last.1 = bf16[512,2048]{1,0:T(8,128)(2,1)} custom-call(s32[3]{0:T(128)S(1)} %copy-done.2, bf16[512,4096]{1,0:T(8,128)(2,1)S(1)} %copy-done, f32[32,64,512]{2,1,0:T(8,128)S(1)} %readout.1.refs_2_, bf16[18,32,512]{2,1,0:T(8,128)(2,1)S(1)} %bitcast.26, f32[1,2048]{1,0:T(1,128)S(1)} %bitcast.30, f32[4,3,4,64,128]{4,3,2,1,0:T(8,128)S(1)} %pad_maximum_fusion.refs_5_, ...), custom_call_target="tpu_custom_call" | custom-call | flops 3221225472 | bytes 16777216 | tf_op jit(solution)/shard_map/readout_last/pallas_call | solution.py:282
  (36 shorter events, 3.2 us)
Async XLA Ops:
  4.2 7.0 %collective-permute-start = (f32[16,64,128]{2,1,0:T(8,128)}, f32[16,64,128]{2,1,0:T(8,128)S(1)}, u32[]{:S(2)}, u32[]{:S(2)}) collective-permute-start(f32[16,64,128]{2,1,0:T(8,128)} %block_state.2), channel_id=1, source_target_pairs={{0,1},{1,0},{2,3},{3,2},{4,5},{5,4},{6,7},{7,6},{8,9},{9,8},{10,11... | collective-permute-start | bytes 1572872 | tf_op jit(solution)/shard_map/ppermute | solution.py:28
  13.1 15.3 %all-to-all-start = ((f32[4,4,64,128]{3,2,1,0:T(8,128)}), f32[4,4,64,128]{3,2,1,0:T(8,128)S(1)}, u32[]{:S(2)}, u32[]{:S(2)}) async-start(f32[4,4,64,128]{3,2,1,0:T(8,128)} %bitcast.3), calls=%async_computation | async-start | bytes 1048576 | tf_op jit(solution)/shard_map/all_to_all | solution.py:308
  28.4 5.2 %collective-permute-start.3 = (f32[4,64,128]{2,1,0:T(8,128)S(1)}, f32[4,64,128]{2,1,0:T(8,128)S(1)}, u32[]{:S(2)}, u32[]{:S(2)}) collective-permute-start(f32[4,64,128]{2,1,0:T(8,128)S(1)} %add_bitcast_fusion.1), channel_id=1, source_target_pairs={{0,8},{8,0},{16,24},{24,16},{32,40},{40,32},{48,56},{56,48},{1,9},... | collective-permute-start | bytes 393224 | tf_op jit(solution)/shard_map/ppermute | solution.py:28
  28.9 18.4 %collective-permute-start.2 = (f32[16,64,128]{2,1,0:T(8,128)}, f32[16,64,128]{2,1,0:T(8,128)S(1)}, u32[]{:S(2)}, u32[]{:S(2)}) collective-permute-start(f32[16,64,128]{2,1,0:T(8,128)} %add.44), channel_id=1, source_target_pairs={{0,2},{2,0},{4,6},{6,4},{1,3},{3,1},{5,7},{7,5},{8,10},{10,8},{12,... | collective-permute-start | bytes 1572872 | tf_op jit(solution)/shard_map/ppermute | solution.py:28
  33.7 8.7 %collective-permute-start.4 = (f32[4,64,128]{2,1,0:T(8,128)S(1)}, f32[4,64,128]{2,1,0:T(8,128)S(1)}, u32[]{:S(2)}, u32[]{:S(2)}) collective-permute-start(f32[4,64,128]{2,1,0:T(8,128)S(1)} %fusion), channel_id=1, source_target_pairs={{0,16},{8,24},{16,0},{24,8},{32,48},{40,56},{48,32},{56,40},{1,17}... | collective-permute-start | bytes 393224 | tf_op jit(solution)/shard_map/ppermute | solution.py:28
  43.5 29.3 %all-to-all-start.1 = ((f32[4,2,4,64,128]{4,3,2,1,0:T(8,128)}), f32[4,2,4,64,128]{4,3,2,1,0:T(8,128)S(1)}, u32[]{:S(2)}, u32[]{:S(2)}) async-start(f32[4,2,4,64,128]{4,3,2,1,0:T(8,128)} %broadcast_in_dim.2), calls=%async_computation.1 | async-start | bytes 2097152 | tf_op jit(solution)/shard_map/all_to_all | solution.py:308
  47.3 34.0 %copy-start.1 = (bf16[512,18,32]{0,2,1:T(8,128)(2,1)S(1)}, bf16[512,18,32]{0,2,1:T(8,128)(2,1)}, u32[]{:S(2)}) copy-start(bf16[512,18,32]{0,2,1:T(8,128)(2,1)} %param.8) | copy-start | bytes 1769476
  47.3 34.0 %copy-start.2 = (s32[3]{0:T(128)S(1)}, s32[3]{0:T(128)}, u32[]{:S(2)}) copy-start(s32[3]{0:T(128)} %pad_add_fusion.place_ref.refs_0_) | copy-start | bytes 40
  48.5 23.5 %collective-permute-start.6 = (f32[16,64,128]{2,1,0:T(8,128)S(1)}, f32[16,64,128]{2,1,0:T(8,128)S(1)}, u32[]{:S(2)}, u32[]{:S(2)}) collective-permute-start(f32[16,64,128]{2,1,0:T(8,128)S(1)} %add.51), channel_id=1, source_target_pairs={{0,6},{2,4},{4,2},{6,0},{1,7},{3,5},{5,3},{7,1},{8,14},{10,12},{12... | collective-permute-start | bytes 1572872 | tf_op jit(solution)/shard_map/ppermute | solution.py:28
  51.3 8.0 %collective-permute-start.7 = (f32[4,64,128]{2,1,0:T(8,128)S(1)}, f32[4,64,128]{2,1,0:T(8,128)S(1)}, u32[]{:S(2)}, u32[]{:S(2)}) collective-permute-start(f32[4,64,128]{2,1,0:T(8,128)S(1)} %add.50), channel_id=1, source_target_pairs={{0,32},{8,40},{16,48},{24,56},{32,0},{40,8},{48,16},{56,24},{1,33}... | collective-permute-start | bytes 393224 | tf_op jit(solution)/shard_map/ppermute | solution.py:28
  59.3 6.1 %collective-permute-start.10 = (f32[4,64,128]{2,1,0:T(8,128)S(1)}, f32[4,64,128]{2,1,0:T(8,128)S(1)}, u32[]{:S(2)}, u32[]{:S(2)}) collective-permute-start(f32[4,64,128]{2,1,0:T(8,128)S(1)} %add.52), channel_id=1, source_target_pairs={{0,192},{64,128},{128,64},{192,0},{1,193},{65,129},{129,65},{193,1... | collective-permute-start | bytes 393224 | tf_op jit(solution)/shard_map/ppermute | solution.py:28
  62.1 5.3 %collective-permute-start.9 = (f32[4,64,128]{2,1,0:T(8,128)S(1)}, f32[4,64,128]{2,1,0:T(8,128)S(1)}, u32[]{:S(2)}, u32[]{:S(2)}) collective-permute-start(f32[4,64,128]{2,1,0:T(8,128)S(1)} %add.52), channel_id=1, source_target_pairs={{0,128},{64,192},{128,0},{192,64},{1,129},{65,193},{129,1},{193,65... | collective-permute-start | bytes 393224 | tf_op jit(solution)/shard_map/ppermute | solution.py:28
  62.5 5.0 %collective-permute-start.8 = (f32[4,64,128]{2,1,0:T(8,128)S(1)}, f32[4,64,128]{2,1,0:T(8,128)S(1)}, u32[]{:S(2)}, u32[]{:S(2)}) collective-permute-start(f32[4,64,128]{2,1,0:T(8,128)S(1)} %add.52), channel_id=1, source_target_pairs={{0,64},{64,0},{128,192},{192,128},{1,65},{65,1},{129,193},{193,129... | collective-permute-start | bytes 393224 | tf_op jit(solution)/shard_map/ppermute | solution.py:28
  72.8 8.5 %collective-permute-start.12 = (f32[4,2,4,64,128]{4,3,2,1,0:T(8,128)S(1)}, f32[4,2,4,64,128]{4,3,2,1,0:T(8,128)S(1)}, u32[]{:S(2)}, u32[]{:S(2)}) collective-permute-start(f32[4,2,4,64,128]{4,3,2,1,0:T(8,128)S(1)} %all-to-all-done.1.refs_10_), channel_id=1, source_target_pairs={{0,1},{1,0},{2,3},{3,2},{4,5},{5,4},{6,7},{7,6},{8,9},{9,8},{10,11... | collective-permute-start | bytes 3145736 | tf_op jit(solution)/shard_map/ppermute | solution.py:28
  75.1 3.9 %collective-permute-start.1 = (f32[16,64,128]{2,1,0:T(8,128)}, f32[16,64,128]{2,1,0:T(8,128)S(1)}, u32[]{:S(2)}, u32[]{:S(2)}) collective-permute-start(f32[16,64,128]{2,1,0:T(8,128)} %block_state.3), channel_id=1, source_target_pairs={{0,1},{1,0},{2,3},{3,2},{4,5},{5,4},{6,7},{7,6},{8,9},{9,8},{10,11... | collective-permute-start | bytes 1572872 | tf_op jit(solution)/shard_map/ppermute | solution.py:28
  75.1 4.4 %collective-permute-start.5 = (f32[4,1,4,64,128]{4,3,2,1,0:T(8,128)S(1)}, f32[4,1,4,64,128]{4,3,2,1,0:T(8,128)S(1)}, u32[]{:S(2)}, u32[]{:S(2)}) collective-permute-start(f32[4,1,4,64,128]{4,3,2,1,0:T(8,128)S(1)} %bitcast.28), channel_id=1, source_target_pairs={{0,1},{1,0},{2,3},{3,2},{4,5},{5,4},{6,7},{7,6},{8,9},{9,8},{10,11... | collective-permute-start | bytes 1572872 | tf_op jit(solution)/shard_map/ppermute | solution.py:28
  75.6 5.7 %collective-permute-start.11 = (f32[4,1,4,64,128]{4,3,2,1,0:T(8,128)S(1)}, f32[4,1,4,64,128]{4,3,2,1,0:T(8,128)S(1)}, u32[]{:S(2)}, u32[]{:S(2)}) collective-permute-start(f32[4,1,4,64,128]{4,3,2,1,0:T(8,128)S(1)} %bitcast.31), channel_id=1, source_target_pairs={{0,1},{1,0},{2,3},{3,2},{4,5},{5,4},{6,7},{7,6},{8,9},{9,8},{10,11... | collective-permute-start | bytes 1572872 | tf_op jit(solution)/shard_map/ppermute | solution.py:28
  75.6 16.1 %collective-permute-start.13 = (f32[3,4,64,128]{3,2,1,0:T(8,128)}, f32[3,4,64,128]{3,2,1,0:T(8,128)S(1)}, u32[]{:S(2)}, u32[]{:S(2)}) collective-permute-start(f32[3,4,64,128]{3,2,1,0:T(8,128)} %pad_maximum_fusion.1), channel_id=1, source_target_pairs={{0,2},{2,0},{4,6},{6,4},{1,3},{3,1},{5,7},{7,5},{8,10},{10,8},{12,... | collective-permute-start | bytes 1179656 | tf_op jit(solution)/shard_map/ppermute | solution.py:28
  79.0 15.2 %collective-permute-start.14 = (f32[3,4,64,128]{3,2,1,0:T(8,128)}, f32[3,4,64,128]{3,2,1,0:T(8,128)S(1)}, u32[]{:S(2)}, u32[]{:S(2)}) collective-permute-start(f32[3,4,64,128]{3,2,1,0:T(8,128)} %pad_maximum_fusion.1), channel_id=1, source_target_pairs={{0,4},{2,6},{4,0},{6,2},{1,5},{3,7},{5,1},{7,3},{8,12},{10,14},{12... | collective-permute-start | bytes 1179656 | tf_op jit(solution)/shard_map/ppermute | solution.py:28
  79.5 20.1 %collective-permute-start.15 = (f32[3,4,64,128]{3,2,1,0:T(8,128)}, f32[3,4,64,128]{3,2,1,0:T(8,128)S(1)}, u32[]{:S(2)}, u32[]{:S(2)}) collective-permute-start(f32[3,4,64,128]{3,2,1,0:T(8,128)} %pad_maximum_fusion.1), channel_id=1, source_target_pairs={{0,6},{2,4},{4,2},{6,0},{1,7},{3,5},{5,3},{7,1},{8,14},{10,12},{12... | collective-permute-start | bytes 1179656 | tf_op jit(solution)/shard_map/ppermute | solution.py:28
  81.3 2.2 %copy-start = (bf16[512,4096]{1,0:T(8,128)(2,1)S(1)}, bf16[512,4096]{1,0:T(8,128)(2,1)}, u32[]{:S(2)}) copy-start(bf16[512,4096]{1,0:T(8,128)(2,1)} %refs_1_.3) | copy-start | bytes 12582916
  83.5 2.2 %copy-start.3 = (f32[32,64,512]{2,1,0:T(8,128)S(1)}, f32[32,64,512]{2,1,0:T(8,128)}, u32[]{:S(2)}) copy-start(f32[32,64,512]{2,1,0:T(8,128)} %local_attention.1.refs_2_) | copy-start | bytes 12582916
  85.7 13.9 %copy-start.4 = (f32[3,4,64,128]{3,2,1,0:T(8,128)S(1)}, f32[3,4,64,128]{3,2,1,0:T(8,128)}, u32[]{:S(2)}) copy-start(f32[3,4,64,128]{3,2,1,0:T(8,128)} %pad_maximum_fusion.1) | copy-start | bytes 1179652
  99.6 1.5 %copy-start.5 = (bf16[2048]{0:T(1024)(128)(2,1)S(1)}, bf16[2048]{0:T(1024)(128)(2,1)}, u32[]{:S(2)}) copy-start(bf16[2048]{0:T(1024)(128)(2,1)} %param.9) | copy-start | bytes 12292
  99.8 4.4 %collective-permute-start.16 = (f32[4,3,4,64,128]{4,3,2,1,0:T(8,128)S(1)}, f32[4,3,4,64,128]{4,3,2,1,0:T(8,128)S(1)}, u32[]{:S(2)}, u32[]{:S(2)}) collective-permute-start(f32[4,3,4,64,128]{4,3,2,1,0:T(8,128)S(1)} %pad_maximum_fusion.refs_5_), channel_id=1, source_target_pairs={{0,1},{1,0},{2,3},{3,2},{4,5},{5,4},{6,7},{7,6},{8,9},{9,8},{10,11... | collective-permute-start | bytes 4718600 | tf_op jit(solution)/shard_map/ppermute | solution.py:28

commit v3 on v2

--- a/solution.py
+++ b/solution.py
@@ -40,7 +40,7 @@
     return lax.dot_general(a, b, (((1,), (1,)), ((), ())), preferred_element_type=F32)
 
 
-def state_kernel(other, place_ref, k_hbm, v_hbm, s_hbm, k_buf, v_buf, s_buf, k_sem, v_sem, s_sem):
+def state_kernel(other, place_ref, k_hbm, v_hbm, s_ref, k_buf, v_buf, k_sem, v_sem):
     side = place_ref[0] ^ other
     chunks = SIDE // GROUP
 
@@ -52,10 +52,6 @@
             pltpu.make_async_copy(k_hbm.at[:, k_at], k_buf.at[i], k_sem.at[i]),
             pltpu.make_async_copy(v_hbm.at[:, v_at], v_buf.at[i], v_sem.at[i]),
         )
-
-    def back(i):
-        heads = pl.ds(i * GROUP, GROUP)
-        return pltpu.make_async_copy(s_buf.at[heads], s_hbm.at[heads], s_sem.at[i])
 
     for i in range(chunks):
         for copy in copies(i):
@@ -68,30 +64,25 @@
             k = k_buf[i, :, pair * 2 * DK : (pair + 1) * 2 * DK]
             both = dot_t0(v, k)
             for j in range(2):
-                s_buf[i * GROUP + 2 * pair + j] = both[j * DV : (j + 1) * DV, j * DK : (j + 1) * DK]
-        back(i).start()
-    for i in range(chunks):
-        back(i).wait()
+                s_ref[i * GROUP + 2 * pair + j] = both[j * DV : (j + 1) * DV, j * DK : (j + 1) * DK]
 
 
 def block_state(place, keys, values, other):
-    hbm = pl.BlockSpec(memory_space=pl.ANY)
+    hbm = pl.BlockSpec(memory_space=pltpu.HBM)
     chunks = SIDE // GROUP
     return pl.pallas_call(
         functools.partial(state_kernel, other),
         in_specs=[pl.BlockSpec(memory_space=pltpu.SMEM), hbm, hbm],
-        out_specs=hbm,
+        out_specs=pl.BlockSpec(memory_space=pltpu.VMEM),
         out_shape=jax.ShapeDtypeStruct((SIDE, DV, DK), F32),
         scratch_shapes=[
             pltpu.VMEM((chunks, TOK, GROUP * DK), BF16),
             pltpu.VMEM((chunks, TOK, GROUP * DV), BF16),
-            pltpu.VMEM((SIDE, DV, DK), F32),
-            pltpu.SemaphoreType.DMA((chunks,)),
             pltpu.SemaphoreType.DMA((chunks,)),
             pltpu.SemaphoreType.DMA((chunks,)),
         ],
         cost_estimate=pl.CostEstimate(flops=1 << 28, bytes_accessed=4 << 20, transcendentals=0),
-        compiler_params=pltpu.CompilerParams(vmem_limit_bytes=60 << 20),
+        compiler_params=pltpu.CompilerParams(vmem_limit_bytes=16 << 20),
         name="block_state",
     )(place, keys, values)
 
@@ -167,7 +158,8 @@
             parts[head, block] = (v_head[:, at : at + HALF], weighted, extra)
     for (head, block), (v_part, weighted, extra) in parts.items():
         out = dot(v_part, weighted)
-        o_ref[head, :, block * HALF : (block + 1) * HALF] = out if extra is None else out + extra
+        out = out if extra is None else out + extra
+        o_ref[head, :, block * HALF : (block + 1) * HALF] = out.astype(BF16)
 
 
 def local_attention(place, queries, keys, values, level_rows):
@@ -185,7 +177,7 @@
             out_specs=pl.BlockSpec((GROUP, DV, TOK), lambda i, p: (i, 0, 0)),
             scratch_shapes=[pltpu.VMEM((LOCAL, GROUP, TOK), F32)],
         ),
-        out_shape=jax.ShapeDtypeStruct((HEADS, DV, TOK), F32),
+        out_shape=jax.ShapeDtypeStruct((HEADS, DV, TOK), BF16),
         cost_estimate=pl.CostEstimate(flops=8 << 30, bytes_accessed=16 << 20, transcendentals=0),
         compiler_params=pltpu.CompilerParams(vmem_limit_bytes=60 << 20),
         name="local_attention",
@@ -227,26 +219,25 @@
     def _():
         stage(1)
 
-    for pair in range(GROUP // 2):
+    sums = {}
+    for head in range(GROUP):
         for block in range(2):
             at = slice(block * HALF, (block + 1) * HALF)
-            outs = []
-            for j in range(2):
-                head = 2 * pair + j
-                q = q_ref[at, head * DK : (head + 1) * DK]
-                r = dot_t1(lhs_ref[head], q)
-                acc = sum_ref[head, :, at]
-                for l in range(levels):
-                    weight = w_ref[l, head : head + 1, at]
-                    acc = acc + r[l * DV : (l + 1) * DV] * weight
-                if last:
-                    mean = jnp.mean(acc * acc, axis=0, keepdims=True)
-                    outs.append(acc * lax.rsqrt(mean + EPS))
-                else:
-                    o_ref[head, :, at] = acc
+            r = dot_t1(lhs_ref[head], q_ref[at, head * DK : (head + 1) * DK])
+            acc = sum_ref[head, :, at].astype(F32)
+            for l in range(levels):
+                acc = acc + r[l * DV : (l + 1) * DV] * w_ref[l, head : head + 1, at]
             if last:
-                flat = jnp.concatenate(outs, axis=0).T
-                cols = slice(pair * 2 * DV, (pair + 1) * 2 * DV)
+                mean = jnp.mean(acc * acc, axis=0, keepdims=True)
+                sums[head, block] = acc * lax.rsqrt(mean + EPS)
+            else:
+                o_ref[head, :, at] = acc
+    if last:
+        for pair in range(GROUP // 2):
+            cols = slice(pair * 2 * DV, (pair + 1) * 2 * DV)
+            for block in range(2):
+                flat = jnp.concatenate([sums[2 * pair, block], sums[2 * pair + 1, block]], axis=0).T
+                at = slice(block * HALF, (block + 1) * HALF)
                 o_ref[at, cols] = (flat * gain_ref[:, cols]).astype(BF16)
 
 
@@ -330,7 +321,7 @@
     u = row_exchange(half.reshape(4, GROUP, DV, DK))
     zero_oth = xor_permute(after(keep, half), "c", 1)
     local = local_attention(after(place, half), queries, keys, values, level_rows)
-    u, local = lax.optimization_barrier((u, local))
+    u, local, zero_oth = lax.optimization_barrier((u, local, zero_oth))
     t3 = (u[0] + u[1]) + (u[2] + u[3])
     l3 = xor_permute(t3, "z", 1)
     l1 = xor_permute(after(half, u), "x", 1)
@@ -342,12 +333,14 @@
     own34 = to_row(l3, l4)
     t6 = t5 + l5
     p1, p2, p3 = (xor_permute(t6, "y", d) for d in (1, 2, 3))
-    p1 = after(p1, l2)
+    own1 = l1.reshape(4, 1, GROUP, DV, DK)
+    oth1 = xor_permute(own1, "c", 1)
+    p1 = after(p1, l2, oth1)
     top = jnp.stack([l5, p1, p2 + p3])
     own567 = sent(top)
-    early = [part.reshape(4, 1, GROUP, DV, DK) for part in (after(l1, t5), after(l2, top))]
-    own = [zero_own.reshape(4, 1, GROUP, DV, DK)] + early
-    oth = [zero_oth.reshape(4, 1, GROUP, DV, DK)] + [xor_permute(part, "c", 1) for part in early]
+    own2 = after(l2, top).reshape(4, 1, GROUP, DV, DK)
+    own = [zero_own.reshape(4, 1, GROUP, DV, DK), own1, own2]
+    oth = [zero_oth.reshape(4, 1, GROUP, DV, DK), oth1, xor_permute(own2, "c", 1)]
     own34 = after(own34, top)
     own.append(own34)
     oth.append(xor_permute(own34, "c", 1))

time: 111 us -> 108 us (0.973)
  waiting for transfers between devices: 36 us -> 27 us
  local copies, waits for them, and re-layouts: 5.48 us -> 11.7 us
  starting transfers between devices: 32.8 us -> 36.5 us
  Pallas kernels: 31.5 us -> 28.2 us
  other arithmetic: 4.77 us -> 3.2 us
    ppermute x17, waiting for transfers between devices: 36 us -> 27 us  [xor_permute(): return lax.ppermute(value, axis, [(i, i ^ mask) for i in range(size)])]
    unnamed x12 -> x26, local copies, waits for them, and re-layouts: 4.39 us -> 10.6 us
    ppermute x17, starting transfers between devices: 25.5 us -> 29.3 us  [xor_permute(): return lax.ppermute(value, axis, [(i, i ^ mask) for i in range(size)])]
    pallas_call x2, Pallas kernels: 7.27 us -> 4.29 us  [block_state(): pl.pallas_call(functools.partial(state_kernel, other), in_specs=[pl.Block...]
  transfers between devices with their start and end apart: 19 -> 19, of which waited for: 10 -> 9; matrix products, arithmetic and copies ran while one was open for 3% -> 3% of each run, Pallas kernels for 19% -> 18%
where the time goes in v3:
time: 108 us; the launch traced here: 107 us
  starting transfers between devices  36.5 us (34%)
  Pallas kernels  28.2 us (26%)
  waiting for transfers between devices  27 us (25%)
  local copies, waits for them, and re-layouts  11.7 us (11%)
  other arithmetic  3.2 us (3%)
    ppermute x17, starting transfers between devices, xor_permute(): return lax.ppermute(value, axis, [(i, i ^ mask) for i in range(size)])  29.3 us
    ppermute x17, waiting for transfers between devices, xor_permute(): return lax.ppermute(value, axis, [(i, i ^ mask) for i in range(size)])  27 us
    pallas_call x2, Pallas kernels, readout(): pl.pallas_call(functools.partial(readout_kernel, base, counts, last), gri...  12.5 us
    pallas_call x1, Pallas kernels, local_attention(): pl.pallas_call(local_kernel, grid_spec=pltpu.PrefetchScalarGridSpec(num_s...  11.4 us
    unnamed x26, local copies, waits for them, and re-layouts  10.6 us
    all_to_all x2, starting transfers between devices, row_exchange(): return lax.all_to_all(payload, 'x', 0, 0, tiled=True)  7.2 us
    pallas_call x2, Pallas kernels, block_state(): pl.pallas_call(functools.partial(state_kernel, other), in_specs=[pl.Block...  4.29 us
  transfers between devices with their start and end apart: 19, of which 9 were waited for; matrix products, arithmetic and copies ran while one was open for 3% of the time, Pallas kernels for 18%

profile of v3, /device:TPU:1, one launch (start us, length us, event | category | flops | bytes accessed | tf_op | source)
XLA Modules:
  0.0 106.8 jit_solution(8649409074164019764)
XLA Ops:
  0.1 2.2 %copy-done = bf16[512,4096]{1,0:T(8,128)(2,1)S(1)} copy-done((bf16[512,4096]{1,0:T(8,128)(2,1)S(1)}, bf16[512,4096]{1,0:T(8,128)(2,1)}, u32[]{:S(2)}) %copy-start) | copy-done | bytes 4194328
  2.3 1.6 %copy-done.1 = bf16[512,2048]{1,0:T(8,128)(2,1)S(1)} copy-done((bf16[512,2048]{1,0:T(8,128)(2,1)S(1)}, bf16[512,2048]{1,0:T(8,128)(2,1)}, u32[]{:S(2)}) %copy-start.1) | copy-done | bytes 2097176
  3.9 2.1 %block_state.2 = f32[16,64,128]{2,1,0:T(8,128)S(1)} custom-call(s32[3]{0:T(128)S(1)} %pad_add_fusion.place_ref.refs_0_, bf16[512,4096]{1,0:T(8,128)(2,1)S(1)} %copy-done, bf16[512,2048]{1,0:T(8,128)(2,1)S(1)} %copy-done.1), custom_call_target="tpu_custom_call" | custom-call | flops 268435456 | bytes 4194304 | tf_op jit(solution)/shard_map/block_state/pallas_call | solution.py:73
  6.0 3.3 %collective-permute-start = (f32[16,64,128]{2,1,0:T(8,128)S(1)}, f32[16,64,128]{2,1,0:T(8,128)S(1)}, u32[]{:S(2)}, u32[]{:S(2)}) collective-permute-start(f32[16,64,128]{2,1,0:T(8,128)S(1)} %block_state.2), channel_id=1, source_target_pairs={{0,1},{1,0},{2,3},{3,2},{4,5},{5,4},{6,7},{7,6},{8,9},{9,8},{10,11... | collective-permute-start | bytes 1572872 | tf_op jit(solution)/shard_map/ppermute | solution.py:28
  9.3 2.1 %block_state.3 = f32[16,64,128]{2,1,0:T(8,128)S(1)} custom-call(s32[3]{0:T(128)S(1)} %pad_add_fusion.place_ref.refs_0_, bf16[512,4096]{1,0:T(8,128)(2,1)S(1)} %copy-done, bf16[512,2048]{1,0:T(8,128)(2,1)S(1)} %copy-done.1), custom_call_target="tpu_custom_call" | custom-call | flops 268435456 | bytes 4194304 | tf_op jit(solution)/shard_map/block_state/pallas_call | solution.py:73
  12.4 3.5 %all-to-all-start = ((f32[4,4,64,128]{3,2,1,0:T(8,128)}), f32[4,4,64,128]{3,2,1,0:T(8,128)S(1)}, u32[]{:S(2)}, u32[]{:S(2)}) async-start(f32[4,4,64,128]{3,2,1,0:T(8,128)} %bitcast.3), calls=%async_computation | async-start | bytes 1048576 | tf_op jit(solution)/shard_map/all_to_all | solution.py:299
  15.9 11.4 %local_attention.1.refs_2_ = bf16[32,64,512]{2,1,0:T(8,128)(2,1)} custom-call(s32[3]{0:T(128)} %copy-done.4, bf16[512,4096]{1,0:T(8,128)(2,1)} %refs_1_.3, bf16[512,4096]{1,0:T(8,128)(2,1)} %k_ref.1, bf16[512,2048]{1,0:T(8,128)(2,1)} %v_ref.1, bf16[18,32,512]{2,1,0:T(8,128)(2,1)} %bitcast.24), custom_call_target="tpu_custom_call" | custom-call | flops 8589934592 | bytes 16777216 | tf_op jit(solution)/shard_map/local_attention/pallas_call | solution.py:166
  27.9 1.5 %collective-permute-start.2 = (f32[16,64,128]{2,1,0:T(8,128)}, f32[16,64,128]{2,1,0:T(8,128)S(1)}, u32[]{:S(2)}, u32[]{:S(2)}) collective-permute-start(f32[16,64,128]{2,1,0:T(8,128)} %add.44), channel_id=1, source_target_pairs={{0,2},{2,0},{4,6},{6,4},{1,3},{3,1},{5,7},{7,5},{8,10},{10,8},{12,... | collective-permute-start | bytes 1572872 | tf_op jit(solution)/shard_map/ppermute | solution.py:28
  29.3 2.7 %collective-permute-done.5 = f32[4,64,128]{2,1,0:T(8,128)S(1)} collective-permute-done((f32[4,64,128]{2,1,0:T(8,128)S(1)}, f32[4,64,128]{2,1,0:T(8,128)S(1)}, u32[]{:S(2)}, u32[]{:S(2)}) %collective-permute-start.5) | collective-permute-done | bytes 131104 | tf_op jit(solution)/shard_map/ppermute | solution.py:28
  32.1 1.9 %collective-permute-start.6 = (f32[4,64,128]{2,1,0:T(8,128)S(1)}, f32[4,64,128]{2,1,0:T(8,128)S(1)}, u32[]{:S(2)}, u32[]{:S(2)}) collective-permute-start(f32[4,64,128]{2,1,0:T(8,128)S(1)} %fusion), channel_id=1, source_target_pairs={{0,16},{8,24},{16,0},{24,8},{32,48},{40,56},{48,32},{56,40},{1,17}... | collective-permute-start | bytes 393224 | tf_op jit(solution)/shard_map/ppermute | solution.py:28
  34.0 6.8 %collective-permute-done.6 = f32[4,64,128]{2,1,0:T(8,128)S(1)} collective-permute-done((f32[4,64,128]{2,1,0:T(8,128)S(1)}, f32[4,64,128]{2,1,0:T(8,128)S(1)}, u32[]{:S(2)}, u32[]{:S(2)}) %collective-permute-start.6) | collective-permute-done | bytes 131104 | tf_op jit(solution)/shard_map/ppermute | solution.py:28
  40.8 1.1 %broadcast_in_dim.2 = f32[4,2,4,64,128]{4,3,2,1,0:T(8,128)} broadcast(f32[2,4,64,128]{3,2,1,0:T(8,128)S(1)} %pad_maximum_fusion.2), dimensions={1,2,3,4} | broadcast | bytes 1310720 | tf_op jit(solution)/shard_map/broadcast_in_dim | solution.py:303
  41.9 3.7 %all-to-all-start.1 = ((f32[4,2,4,64,128]{4,3,2,1,0:T(8,128)}), f32[4,2,4,64,128]{4,3,2,1,0:T(8,128)S(1)}, u32[]{:S(2)}, u32[]{:S(2)}) async-start(f32[4,2,4,64,128]{4,3,2,1,0:T(8,128)} %broadcast_in_dim.2), calls=%async_computation.1 | async-start | bytes 2097152 | tf_op jit(solution)/shard_map/all_to_all | solution.py:299
  45.6 1.2 %add.45 = f32[16,64,128]{2,1,0:T(8,128)S(1)} add(f32[16,64,128]{2,1,0:T(8,128)} %add.44, f32[16,64,128]{2,1,0:T(8,128)S(1)} %collective-permute-done.2) | non-fusion elementwise | flops 131072 | bytes 1572864 | tf_op jit(solution)/shard_map/add | solution.py:331
  46.8 2.8 %collective-permute-start.4 = (f32[16,64,128]{2,1,0:T(8,128)S(1)}, f32[16,64,128]{2,1,0:T(8,128)S(1)}, u32[]{:S(2)}, u32[]{:S(2)}) collective-permute-start(f32[16,64,128]{2,1,0:T(8,128)S(1)} %add.45), channel_id=1, source_target_pairs={{0,6},{2,4},{4,2},{6,0},{1,7},{3,5},{5,3},{7,1},{8,14},{10,12},{12... | collective-permute-start | bytes 1572872 | tf_op jit(solution)/shard_map/ppermute | solution.py:28
  49.5 2.0 %collective-permute-start.3 = (f32[4,1,4,64,128]{4,3,2,1,0:T(8,128)S(1)}, f32[4,1,4,64,128]{4,3,2,1,0:T(8,128)S(1)}, u32[]{:S(2)}, u32[]{:S(2)}) collective-permute-start(f32[4,1,4,64,128]{4,3,2,1,0:T(8,128)S(1)} %bitcast.28), channel_id=1, source_target_pairs={{0,1},{1,0},{2,3},{3,2},{4,5},{5,4},{6,7},{7,6},{8,9},{9,8},{10,11... | collective-permute-start | bytes 1572872 | tf_op jit(solution)/shard_map/ppermute | solution.py:28
  51.6 5.4 %collective-permute-start.7 = (f32[4,64,128]{2,1,0:T(8,128)S(1)}, f32[4,64,128]{2,1,0:T(8,128)S(1)}, u32[]{:S(2)}, u32[]{:S(2)}) collective-permute-start(f32[4,64,128]{2,1,0:T(8,128)S(1)} %add.51), channel_id=1, source_target_pairs={{0,32},{8,40},{16,48},{24,56},{32,0},{40,8},{48,16},{56,24},{1,33}... | collective-permute-start | bytes 393224 | tf_op jit(solution)/shard_map/ppermute | solution.py:28
  57.0 3.7 %collective-permute-done.7 = f32[4,64,128]{2,1,0:T(8,128)S(1)} collective-permute-done((f32[4,64,128]{2,1,0:T(8,128)S(1)}, f32[4,64,128]{2,1,0:T(8,128)S(1)}, u32[]{:S(2)}, u32[]{:S(2)}) %collective-permute-start.7) | collective-permute-done | bytes 131104 | tf_op jit(solution)/shard_map/ppermute | solution.py:28
  60.7 3.0 %collective-permute-start.10 = (f32[4,64,128]{2,1,0:T(8,128)S(1)}, f32[4,64,128]{2,1,0:T(8,128)S(1)}, u32[]{:S(2)}, u32[]{:S(2)}) collective-permute-start(f32[4,64,128]{2,1,0:T(8,128)S(1)} %add.52), channel_id=1, source_target_pairs={{0,192},{64,128},{128,64},{192,0},{1,193},{65,129},{129,65},{193,1... | collective-permute-start | bytes 393224 | tf_op jit(solution)/shard_map/ppermute | solution.py:28
  64.4 3.5 %collective-permute-done.10 = f32[4,64,128]{2,1,0:T(8,128)S(1)} collective-permute-done((f32[4,64,128]{2,1,0:T(8,128)S(1)}, f32[4,64,128]{2,1,0:T(8,128)S(1)}, u32[]{:S(2)}, u32[]{:S(2)}) %collective-permute-start.10) | collective-permute-done | bytes 131104 | tf_op jit(solution)/shard_map/ppermute | solution.py:28
  67.9 1.2 %collective-permute-done.9 = f32[4,64,128]{2,1,0:T(8,128)S(1)} collective-permute-done((f32[4,64,128]{2,1,0:T(8,128)S(1)}, f32[4,64,128]{2,1,0:T(8,128)S(1)}, u32[]{:S(2)}, u32[]{:S(2)}) %collective-permute-start.9) | collective-permute-done | bytes 131104 | tf_op jit(solution)/shard_map/ppermute | solution.py:28
  72.0 2.4 %collective-permute-start.12 = (f32[4,2,4,64,128]{4,3,2,1,0:T(8,128)S(1)}, f32[4,2,4,64,128]{4,3,2,1,0:T(8,128)S(1)}, u32[]{:S(2)}, u32[]{:S(2)}) collective-permute-start(f32[4,2,4,64,128]{4,3,2,1,0:T(8,128)S(1)} %all-to-all-done.1.refs_10_), channel_id=1, source_target_pairs={{0,1},{1,0},{2,3},{3,2},{4,5},{5,4},{6,7},{7,6},{8,9},{9,8},{10,11... | collective-permute-start | bytes 3145736 | tf_op jit(solution)/shard_map/ppermute | solution.py:28
  74.4 1.2 %collective-permute-start.14 = (f32[3,4,64,128]{3,2,1,0:T(8,128)}, f32[3,4,64,128]{3,2,1,0:T(8,128)S(1)}, u32[]{:S(2)}, u32[]{:S(2)}) collective-permute-start(f32[3,4,64,128]{3,2,1,0:T(8,128)} %pad_maximum_fusion.1), channel_id=1, source_target_pairs={{0,4},{2,6},{4,0},{6,2},{1,5},{3,7},{5,1},{7,3},{8,12},{10,14},{12... | collective-permute-start | bytes 1179656 | tf_op jit(solution)/shard_map/ppermute | solution.py:28
  75.5 2.7 %collective-permute-start.15 = (f32[3,4,64,128]{3,2,1,0:T(8,128)}, f32[3,4,64,128]{3,2,1,0:T(8,128)S(1)}, u32[]{:S(2)}, u32[]{:S(2)}) collective-permute-start(f32[3,4,64,128]{3,2,1,0:T(8,128)} %pad_maximum_fusion.1), channel_id=1, source_target_pairs={{0,6},{2,4},{4,2},{6,0},{1,7},{3,5},{5,3},{7,1},{8,14},{10,12},{12... | collective-permute-start | bytes 1179656 | tf_op jit(solution)/shard_map/ppermute | solution.py:28
  78.3 2.2 %copy-done.2 = bf16[512,4096]{1,0:T(8,128)(2,1)S(1)} copy-done((bf16[512,4096]{1,0:T(8,128)(2,1)S(1)}, bf16[512,4096]{1,0:T(8,128)(2,1)}, u32[]{:S(2)}) %copy-start.2) | copy-done | bytes 4194328
  82.5 1.6 %copy-done.10 = bf16[32,64,512]{2,1,0:T(8,128)(2,1)S(1)} copy-done((bf16[32,64,512]{2,1,0:T(8,128)(2,1)S(1)}, bf16[32,64,512]{2,1,0:T(8,128)(2,1)}, u32[]{:S(2)}) %copy-start.10) | copy-done | bytes 2097176
  84.1 5.9 %readout.1.refs_2_ = f32[32,64,512]{2,1,0:T(8,128)S(1)} custom-call(s32[3]{0:T(128)S(1)} %copy-done.5, bf16[512,4096]{1,0:T(8,128)(2,1)S(1)} %copy-done.2, bf16[32,64,512]{2,1,0:T(8,128)(2,1)S(1)} %copy-done.10, bf16[18,32,512]{2,1,0:T(8,128)(2,1)S(1)} %bitcast.25, f32[4,1,4,64,128]{4,3,2,1,0:T(8,128)S(1)} %bitcast.27, f32[4,1,4,64,128]{4,3,2,1,0:T(8,128)S(1)} %bitcast.31, ...), custom_call_target="tpu_custom_call" | custom-call | flops 5368709120 | bytes 16777216 | tf_op jit(solution)/shard_map/readout/pallas_call | solution.py:273
  90.1 2.9 %collective-permute-done.14 = f32[3,4,64,128]{3,2,1,0:T(8,128)S(1)} collective-permute-done((f32[3,4,64,128]{3,2,1,0:T(8,128)}, f32[3,4,64,128]{3,2,1,0:T(8,128)S(1)}, u32[]{:S(2)}, u32[]{:S(2)}) %collective-permute-start.14) | collective-permute-done | bytes 393248 | tf_op jit(solution)/shard_map/ppermute | solution.py:28
  92.9 2.1 %collective-permute-done.15 = f32[3,4,64,128]{3,2,1,0:T(8,128)S(1)} collective-permute-done((f32[3,4,64,128]{3,2,1,0:T(8,128)}, f32[3,4,64,128]{3,2,1,0:T(8,128)S(1)}, u32[]{:S(2)}, u32[]{:S(2)}) %collective-permute-start.15) | collective-permute-done | bytes 393248 | tf_op jit(solution)/shard_map/ppermute | solution.py:28
  95.2 2.0 %collective-permute-start.16 = (f32[4,3,4,64,128]{4,3,2,1,0:T(8,128)S(1)}, f32[4,3,4,64,128]{4,3,2,1,0:T(8,128)S(1)}, u32[]{:S(2)}, u32[]{:S(2)}) collective-permute-start(f32[4,3,4,64,128]{4,3,2,1,0:T(8,128)S(1)} %pad_maximum_fusion.refs_5_), channel_id=1, source_target_pairs={{0,1},{1,0},{2,3},{3,2},{4,5},{5,4},{6,7},{7,6},{8,9},{9,8},{10,11... | collective-permute-start | bytes 4718600 | tf_op jit(solution)/shard_map/ppermute | solution.py:28
  97.2 3.0 %collective-permute-done.16.refs_6_ = f32[4,3,4,64,128]{4,3,2,1,0:T(8,128)S(1)} collective-permute-done((f32[4,3,4,64,128]{4,3,2,1,0:T(8,128)S(1)}, f32[4,3,4,64,128]{4,3,2,1,0:T(8,128)S(1)}, u32[]{:S(2)}, u32[]{:S(2)}) %collective-permute-start.16) | collective-permute-done | bytes 1572896 | tf_op jit(solution)/shard_map/ppermute | solution.py:28
  100.3 6.6 %readout_last.1 = bf16[512,2048]{1,0:T(8,128)(2,1)} custom-call(s32[3]{0:T(128)S(1)} %copy-done.5, bf16[512,4096]{1,0:T(8,128)(2,1)S(1)} %copy-done.2, f32[32,64,512]{2,1,0:T(8,128)S(1)} %readout.1.refs_2_, bf16[18,32,512]{2,1,0:T(8,128)(2,1)S(1)} %bitcast.26, f32[1,2048]{1,0:T(1,128)S(1)} %bitcast.30, f32[4,3,4,64,128]{4,3,2,1,0:T(8,128)S(1)} %pad_maximum_fusion.refs_5_, ...), custom_call_target="tpu_custom_call" | custom-call | flops 3221225472 | bytes 16777216 | tf_op jit(solution)/shard_map/readout_last/pallas_call | solution.py:273
  (50 shorter events, 7.4 us)
Async XLA Ops:
  0.1 2.2 %copy-start = (bf16[512,4096]{1,0:T(8,128)(2,1)S(1)}, bf16[512,4096]{1,0:T(8,128)(2,1)}, u32[]{:S(2)}) copy-start(bf16[512,4096]{1,0:T(8,128)(2,1)} %k_ref.1) | copy-start | bytes 12582916
  2.3 1.6 %copy-start.1 = (bf16[512,2048]{1,0:T(8,128)(2,1)S(1)}, bf16[512,2048]{1,0:T(8,128)(2,1)}, u32[]{:S(2)}) copy-start(bf16[512,2048]{1,0:T(8,128)(2,1)} %v_ref.1) | copy-start | bytes 6291460
  3.9 5.5 %copy-start.4 = (s32[3]{0:T(128)}, s32[3]{0:T(128)S(1)}, u32[]{:S(2)}) copy-start(s32[3]{0:T(128)S(1)} %pad_add_fusion.place_ref.refs_0_) | copy-start | bytes 40
  6.0 5.5 %collective-permute-start = (f32[16,64,128]{2,1,0:T(8,128)S(1)}, f32[16,64,128]{2,1,0:T(8,128)S(1)}, u32[]{:S(2)}, u32[]{:S(2)}) collective-permute-start(f32[16,64,128]{2,1,0:T(8,128)S(1)} %block_state.2), channel_id=1, source_target_pairs={{0,1},{1,0},{2,3},{3,2},{4,5},{5,4},{6,7},{7,6},{8,9},{9,8},{10,11... | collective-permute-start | bytes 1572872 | tf_op jit(solution)/shard_map/ppermute | solution.py:28
  12.4 14.9 %collective-permute-start.1 = (f32[16,64,128]{2,1,0:T(8,128)S(1)}, f32[16,64,128]{2,1,0:T(8,128)S(1)}, u32[]{:S(2)}, u32[]{:S(2)}) collective-permute-start(f32[16,64,128]{2,1,0:T(8,128)S(1)} %block_state.3), channel_id=1, source_target_pairs={{0,1},{1,0},{2,3},{3,2},{4,5},{5,4},{6,7},{7,6},{8,9},{9,8},{10,11... | collective-permute-start | bytes 1572872 | tf_op jit(solution)/shard_map/ppermute | solution.py:28
  12.4 14.9 %all-to-all-start = ((f32[4,4,64,128]{3,2,1,0:T(8,128)}), f32[4,4,64,128]{3,2,1,0:T(8,128)S(1)}, u32[]{:S(2)}, u32[]{:S(2)}) async-start(f32[4,4,64,128]{3,2,1,0:T(8,128)} %bitcast.3), calls=%async_computation | async-start | bytes 1048576 | tf_op jit(solution)/shard_map/all_to_all | solution.py:299
  27.4 4.7 %collective-permute-start.5 = (f32[4,64,128]{2,1,0:T(8,128)S(1)}, f32[4,64,128]{2,1,0:T(8,128)S(1)}, u32[]{:S(2)}, u32[]{:S(2)}) collective-permute-start(f32[4,64,128]{2,1,0:T(8,128)S(1)} %add_bitcast_fusion.1), channel_id=1, source_target_pairs={{0,8},{8,0},{16,24},{24,16},{32,40},{40,32},{48,56},{56,48},{1,9},... | collective-permute-start | bytes 393224 | tf_op jit(solution)/shard_map/ppermute | solution.py:28
  27.9 17.7 %collective-permute-start.2 = (f32[16,64,128]{2,1,0:T(8,128)}, f32[16,64,128]{2,1,0:T(8,128)S(1)}, u32[]{:S(2)}, u32[]{:S(2)}) collective-permute-start(f32[16,64,128]{2,1,0:T(8,128)} %add.44), channel_id=1, source_target_pairs={{0,2},{2,0},{4,6},{6,4},{1,3},{3,1},{5,7},{7,5},{8,10},{10,8},{12,... | collective-permute-start | bytes 1572872 | tf_op jit(solution)/shard_map/ppermute | solution.py:28
  32.1 8.7 %collective-permute-start.6 = (f32[4,64,128]{2,1,0:T(8,128)S(1)}, f32[4,64,128]{2,1,0:T(8,128)S(1)}, u32[]{:S(2)}, u32[]{:S(2)}) collective-permute-start(f32[4,64,128]{2,1,0:T(8,128)S(1)} %fusion), channel_id=1, source_target_pairs={{0,16},{8,24},{16,0},{24,8},{32,48},{40,56},{48,32},{56,40},{1,17}... | collective-permute-start | bytes 393224 | tf_op jit(solution)/shard_map/ppermute | solution.py:28
  41.9 30.1 %all-to-all-start.1 = ((f32[4,2,4,64,128]{4,3,2,1,0:T(8,128)}), f32[4,2,4,64,128]{4,3,2,1,0:T(8,128)S(1)}, u32[]{:S(2)}, u32[]{:S(2)}) async-start(f32[4,2,4,64,128]{4,3,2,1,0:T(8,128)} %broadcast_in_dim.2), calls=%async_computation.1 | async-start | bytes 2097152 | tf_op jit(solution)/shard_map/all_to_all | solution.py:299
  45.6 32.6 %copy-start.3 = (bf16[512,18,32]{0,2,1:T(8,128)(2,1)S(1)}, bf16[512,18,32]{0,2,1:T(8,128)(2,1)}, u32[]{:S(2)}) copy-start(bf16[512,18,32]{0,2,1:T(8,128)(2,1)} %param.8) | copy-start | bytes 1769476
  45.6 32.6 %copy-start.5 = (s32[3]{0:T(128)S(1)}, s32[3]{0:T(128)}, u32[]{:S(2)}) copy-start(s32[3]{0:T(128)} %copy-done.4) | copy-start | bytes 40
  46.8 23.4 %collective-permute-start.4 = (f32[16,64,128]{2,1,0:T(8,128)S(1)}, f32[16,64,128]{2,1,0:T(8,128)S(1)}, u32[]{:S(2)}, u32[]{:S(2)}) collective-permute-start(f32[16,64,128]{2,1,0:T(8,128)S(1)} %add.45), channel_id=1, source_target_pairs={{0,6},{2,4},{4,2},{6,0},{1,7},{3,5},{5,3},{7,1},{8,14},{10,12},{12... | collective-permute-start | bytes 1572872 | tf_op jit(solution)/shard_map/ppermute | solution.py:28
  49.5 20.7 %collective-permute-start.3 = (f32[4,1,4,64,128]{4,3,2,1,0:T(8,128)S(1)}, f32[4,1,4,64,128]{4,3,2,1,0:T(8,128)S(1)}, u32[]{:S(2)}, u32[]{:S(2)}) collective-permute-start(f32[4,1,4,64,128]{4,3,2,1,0:T(8,128)S(1)} %bitcast.28), channel_id=1, source_target_pairs={{0,1},{1,0},{2,3},{3,2},{4,5},{5,4},{6,7},{7,6},{8,9},{9,8},{10,11... | collective-permute-start | bytes 1572872 | tf_op jit(solution)/shard_map/ppermute | solution.py:28
  51.6 9.1 %collective-permute-start.7 = (f32[4,64,128]{2,1,0:T(8,128)S(1)}, f32[4,64,128]{2,1,0:T(8,128)S(1)}, u32[]{:S(2)}, u32[]{:S(2)}) collective-permute-start(f32[4,64,128]{2,1,0:T(8,128)S(1)} %add.51), channel_id=1, source_target_pairs={{0,32},{8,40},{16,48},{24,56},{32,0},{40,8},{48,16},{56,24},{1,33}... | collective-permute-start | bytes 393224 | tf_op jit(solution)/shard_map/ppermute | solution.py:28
  60.7 7.2 %collective-permute-start.10 = (f32[4,64,128]{2,1,0:T(8,128)S(1)}, f32[4,64,128]{2,1,0:T(8,128)S(1)}, u32[]{:S(2)}, u32[]{:S(2)}) collective-permute-start(f32[4,64,128]{2,1,0:T(8,128)S(1)} %add.52), channel_id=1, source_target_pairs={{0,192},{64,128},{128,64},{192,0},{1,193},{65,129},{129,65},{193,1... | collective-permute-start | bytes 393224 | tf_op jit(solution)/shard_map/ppermute | solution.py:28
  63.7 5.4 %collective-permute-start.9 = (f32[4,64,128]{2,1,0:T(8,128)S(1)}, f32[4,64,128]{2,1,0:T(8,128)S(1)}, u32[]{:S(2)}, u32[]{:S(2)}) collective-permute-start(f32[4,64,128]{2,1,0:T(8,128)S(1)} %add.52), channel_id=1, source_target_pairs={{0,128},{64,192},{128,0},{192,64},{1,129},{65,193},{129,1},{193,65... | collective-permute-start | bytes 393224 | tf_op jit(solution)/shard_map/ppermute | solution.py:28
  64.0 5.1 %collective-permute-start.8 = (f32[4,64,128]{2,1,0:T(8,128)S(1)}, f32[4,64,128]{2,1,0:T(8,128)S(1)}, u32[]{:S(2)}, u32[]{:S(2)}) collective-permute-start(f32[4,64,128]{2,1,0:T(8,128)S(1)} %add.52), channel_id=1, source_target_pairs={{0,64},{64,0},{128,192},{192,128},{1,65},{65,1},{129,193},{193,129... | collective-permute-start | bytes 393224 | tf_op jit(solution)/shard_map/ppermute | solution.py:28
  70.2 1.0 copy-start.6
  70.2 0.8 copy-start.8
  72.0 6.2 %collective-permute-start.12 = (f32[4,2,4,64,128]{4,3,2,1,0:T(8,128)S(1)}, f32[4,2,4,64,128]{4,3,2,1,0:T(8,128)S(1)}, u32[]{:S(2)}, u32[]{:S(2)}) collective-permute-start(f32[4,2,4,64,128]{4,3,2,1,0:T(8,128)S(1)} %all-to-all-done.1.refs_10_), channel_id=1, source_target_pairs={{0,1},{1,0},{2,3},{3,2},{4,5},{5,4},{6,7},{7,6},{8,9},{9,8},{10,11... | collective-permute-start | bytes 3145736 | tf_op jit(solution)/shard_map/ppermute | solution.py:28
  74.4 3.9 %collective-permute-start.11 = (f32[4,1,4,64,128]{4,3,2,1,0:T(8,128)}, f32[4,1,4,64,128]{4,3,2,1,0:T(8,128)S(1)}, u32[]{:S(2)}, u32[]{:S(2)}) collective-permute-start(f32[4,1,4,64,128]{4,3,2,1,0:T(8,128)} %bitcast.32), channel_id=1, source_target_pairs={{0,1},{1,0},{2,3},{3,2},{4,5},{5,4},{6,7},{7,6},{8,9},{9,8},{10,11... | collective-permute-start | bytes 1572872 | tf_op jit(solution)/shard_map/ppermute | solution.py:28
  74.4 15.7 %collective-permute-start.13 = (f32[3,4,64,128]{3,2,1,0:T(8,128)}, f32[3,4,64,128]{3,2,1,0:T(8,128)S(1)}, u32[]{:S(2)}, u32[]{:S(2)}) collective-permute-start(f32[3,4,64,128]{3,2,1,0:T(8,128)} %pad_maximum_fusion.1), channel_id=1, source_target_pairs={{0,2},{2,0},{4,6},{6,4},{1,3},{3,1},{5,7},{7,5},{8,10},{10,8},{12,... | collective-permute-start | bytes 1179656 | tf_op jit(solution)/shard_map/ppermute | solution.py:28
  74.4 18.6 %collective-permute-start.14 = (f32[3,4,64,128]{3,2,1,0:T(8,128)}, f32[3,4,64,128]{3,2,1,0:T(8,128)S(1)}, u32[]{:S(2)}, u32[]{:S(2)}) collective-permute-start(f32[3,4,64,128]{3,2,1,0:T(8,128)} %pad_maximum_fusion.1), channel_id=1, source_target_pairs={{0,4},{2,6},{4,0},{6,2},{1,5},{3,7},{5,1},{7,3},{8,12},{10,14},{12... | collective-permute-start | bytes 1179656 | tf_op jit(solution)/shard_map/ppermute | solution.py:28
  75.5 19.5 %collective-permute-start.15 = (f32[3,4,64,128]{3,2,1,0:T(8,128)}, f32[3,4,64,128]{3,2,1,0:T(8,128)S(1)}, u32[]{:S(2)}, u32[]{:S(2)}) collective-permute-start(f32[3,4,64,128]{3,2,1,0:T(8,128)} %pad_maximum_fusion.1), channel_id=1, source_target_pairs={{0,6},{2,4},{4,2},{6,0},{1,7},{3,5},{5,3},{7,1},{8,14},{10,12},{12... | collective-permute-start | bytes 1179656 | tf_op jit(solution)/shard_map/ppermute | solution.py:28
  78.2 2.2 %copy-start.2 = (bf16[512,4096]{1,0:T(8,128)(2,1)S(1)}, bf16[512,4096]{1,0:T(8,128)(2,1)}, u32[]{:S(2)}) copy-start(bf16[512,4096]{1,0:T(8,128)(2,1)} %refs_1_.3) | copy-start | bytes 12582916
  80.4 1.0 copy-start.7
  81.5 1.0 copy-start.9
  82.5 1.6 %copy-start.10 = (bf16[32,64,512]{2,1,0:T(8,128)(2,1)S(1)}, bf16[32,64,512]{2,1,0:T(8,128)(2,1)}, u32[]{:S(2)}) copy-start(bf16[32,64,512]{2,1,0:T(8,128)(2,1)} %local_attention.1.refs_2_) | copy-start | bytes 6291460
  84.1 10.9 %copy-start.11 = (f32[3,4,64,128]{3,2,1,0:T(8,128)S(1)}, f32[3,4,64,128]{3,2,1,0:T(8,128)}, u32[]{:S(2)}) copy-start(f32[3,4,64,128]{3,2,1,0:T(8,128)} %pad_maximum_fusion.1) | copy-start | bytes 1179652
  95.0 2.2 %copy-start.12 = (bf16[2048]{0:T(1024)(128)(2,1)S(1)}, bf16[2048]{0:T(1024)(128)(2,1)}, u32[]{:S(2)}) copy-start(bf16[2048]{0:T(1024)(128)(2,1)} %param.9) | copy-start | bytes 12292
  95.2 5.1 %collective-permute-start.16 = (f32[4,3,4,64,128]{4,3,2,1,0:T(8,128)S(1)}, f32[4,3,4,64,128]{4,3,2,1,0:T(8,128)S(1)}, u32[]{:S(2)}, u32[]{:S(2)}) collective-permute-start(f32[4,3,4,64,128]{4,3,2,1,0:T(8,128)S(1)} %pad_maximum_fusion.refs_5_), channel_id=1, source_target_pairs={{0,1},{1,0},{2,3},{3,2},{4,5},{5,4},{6,7},{7,6},{8,9},{9,8},{10,11... | collective-permute-start | bytes 4718600 | tf_op jit(solution)/shard_map/ppermute | solution.py:28

commit v4 on v3

--- a/solution.py
+++ b/solution.py
@@ -184,12 +184,15 @@
     )(place, queries, keys, values, level_rows)
 
 
-def readout_kernel(base, counts, last, *refs):
+def readout_kernel(base, counts, last, part, *refs):
     refs = list(refs)
     place_ref, q_ref, sum_ref, lw_ref = refs[:4]
     refs = refs[4:]
     gain_ref = refs.pop(0) if last else None
-    sides = [(refs[2 * i], refs[2 * i + 1]) for i in range(len(counts))]
+    if part == 1:
+        refs.pop(0)
+    per = 2 if part is None else 1
+    sides = [refs[per * i : per * i + per] for i in range(len(counts))]
     o_ref, lhs_ref, w_ref = refs[-3:]
     step = pl.program_id(0)
     levels = sum(counts)
@@ -211,13 +214,18 @@
                     lhs_ref[j, at : at + DV] = pair[which][0, level, j].astype(BF16)
                 at += DV
 
-    @pl.when(step < STEPS // 2)
-    def _():
+    if part is None:
+
+        @pl.when(step < STEPS // 2)
+        def _():
+            stage(0)
+
+        @pl.when(step >= STEPS // 2)
+        def _():
+            stage(1)
+
+    else:
         stage(0)
-
-    @pl.when(step >= STEPS // 2)
-    def _():
-        stage(1)
 
     sums = {}
     for head in range(GROUP):
@@ -241,17 +249,22 @@
                 o_ref[at, cols] = (flat * gain_ref[:, cols]).astype(BF16)
 
 
-def readout(place, queries, total, level_rows, base, own, oth, distance, gain=None):
+def readout(place, queries, total, level_rows, base, own, oth, distance, gain=None, part=None, prior=None):
     last = gain is not None
     counts = tuple(o.shape[1] for o in own)
     levels = sum(counts)
 
+    def side(i, place):
+        return place[0] ^ (i // 4 if part is None else part)
+
     def group(i, place):
-        return 4 * (place[0] ^ (i // 4)) + i % 4
+        return 4 * side(i, place) + i % 4
 
     def pieces(array, second, by_distance):
         def index(i, place):
-            at = jnp.maximum(i - 4, 0) if second else jnp.minimum(i, 3)
+            at = i
+            if part is None:
+                at = jnp.maximum(i - 4, 0) if second else jnp.minimum(i, 3)
             return (at ^ place[1] if by_distance else at, 0, 0, 0, 0)
 
         return pl.BlockSpec((1,) + array.shape[1:], index)
@@ -262,19 +275,28 @@
     specs = [
         pl.BlockSpec((TOK, GROUP * DK), lambda i, p: (0, group(i, p))),
         heads,
-        pl.BlockSpec((LEVELS, SIDE, TOK), lambda i, p: (0, p[0] ^ (i // 4), 0)),
+        pl.BlockSpec((LEVELS, SIDE, TOK), lambda i, p: (0, side(i, p), 0)),
     ]
     if last:
         args.append(gain)
         specs.append(pl.BlockSpec((1, GROUP * DV), lambda i, p: (0, group(i, p))))
+    aliases = {}
+    if part == 1:
+        aliases = {1 + len(args): 0}
+        args.append(prior)
+        specs.append(pl.BlockSpec(memory_space=pl.ANY))
     for mine, theirs, by_distance in zip(own, oth, distance):
-        args += [mine, theirs]
-        specs += [pieces(mine, False, by_distance), pieces(theirs, True, by_distance)]
+        if part != 1:
+            args.append(mine)
+            specs.append(pieces(mine, False, by_distance))
+        if part != 0:
+            args.append(theirs)
+            specs.append(pieces(theirs, True, by_distance))
     return pl.pallas_call(
-        functools.partial(readout_kernel, base, counts, last),
+        functools.partial(readout_kernel, base, counts, last, part),
         grid_spec=pltpu.PrefetchScalarGridSpec(
             num_scalar_prefetch=1,
-            grid=(STEPS,),
+            grid=(STEPS if part is None else STEPS // 2,),
             in_specs=specs,
             out_specs=flat if last else heads,
             scratch_shapes=[
@@ -287,6 +309,7 @@
         else jax.ShapeDtypeStruct((HEADS, DV, TOK), F32),
         cost_estimate=pl.CostEstimate(flops=levels << 30, bytes_accessed=16 << 20, transcendentals=0),
         compiler_params=pltpu.CompilerParams(vmem_limit_bytes=24 << 20),
+        input_output_aliases=aliases,
         name="readout_last" if last else "readout",
     )(place, *args)
 
@@ -347,7 +370,12 @@
     mid = readout(place, queries, local, level_rows, 0, own, oth, [False] * 4)
     own567 = jnp.stack([after(part, mid) for part in own567])
     oth567 = xor_permute(own567, "c", 1)
-    return readout(place, queries, mid, level_rows, 5, [own567], [oth567], [True], gain=gain)
+    half_done = readout(
+        place, queries, mid, level_rows, 5, [own567], [oth567], [True], gain=gain, part=0
+    )
+    return readout(
+        place, queries, mid, level_rows, 5, [own567], [oth567], [True], gain=gain, part=1, prior=half_done
+    )
 
 
 def solution(mesh):

time: 108 us -> 106 us (0.981)
  waiting for transfers between devices: 27 us -> 24 us
  Pallas kernels: 28.2 us -> 29.3 us
    ppermute x17, waiting for transfers between devices: 27 us -> 24 us  [xor_permute(): return lax.ppermute(value, axis, [(i, i ^ mask) for i in range(size)])]
    pallas_call x2 -> x3, Pallas kernels: 12.5 us -> 13.5 us  [readout(): pl.pallas_call(functools.partial(readout_kernel, base, counts, last, part...]
  transfers between devices with their start and end apart: 19 -> 19, of which waited for: 9 -> 8; matrix products, arithmetic and copies ran while one was open for 3% -> 3% of each run, Pallas kernels for 18% -> 22%
where the time goes in v4:
time: 106 us; the launch traced here: 105 us
  starting transfers between devices  36.5 us (34%)
  Pallas kernels  29.3 us (28%)
  waiting for transfers between devices  24 us (23%)
  local copies, waits for them, and re-layouts  11.7 us (11%)
  other arithmetic  3.2 us (3%)
    ppermute x17, starting transfers between devices, xor_permute(): return lax.ppermute(value, axis, [(i, i ^ mask) for i in range(size)])  29.3 us
    ppermute x17, waiting for transfers between devices, xor_permute(): return lax.ppermute(value, axis, [(i, i ^ mask) for i in range(size)])  24 us
    pallas_call x3, Pallas kernels, readout(): pl.pallas_call(functools.partial(readout_kernel, base, counts, last, part...  13.5 us
    pallas_call x1, Pallas kernels, local_attention(): pl.pallas_call(local_kernel, grid_spec=pltpu.PrefetchScalarGridSpec(num_s...  11.4 us
    unnamed x26, local copies, waits for them, and re-layouts  10.6 us
    all_to_all x2, starting transfers between devices, row_exchange(): return lax.all_to_all(payload, 'x', 0, 0, tiled=True)  7.19 us
    pallas_call x2, Pallas kernels, block_state(): pl.pallas_call(functools.partial(state_kernel, other), in_specs=[pl.Block...  4.29 us
  transfers between devices with their start and end apart: 19, of which 8 were waited for; matrix products, arithmetic and copies ran while one was open for 3% of the time, Pallas kernels for 22%

profile of v4, /device:TPU:1, one launch (start us, length us, event | category | flops | bytes accessed | tf_op | source)
XLA Modules:
  0.0 104.8 jit_solution(7297380739018154109)
XLA Ops:
  0.1 2.2 %copy-done = bf16[512,4096]{1,0:T(8,128)(2,1)S(1)} copy-done((bf16[512,4096]{1,0:T(8,128)(2,1)S(1)}, bf16[512,4096]{1,0:T(8,128)(2,1)}, u32[]{:S(2)}) %copy-start) | copy-done | bytes 4194328
  2.3 1.6 %copy-done.2 = bf16[512,2048]{1,0:T(8,128)(2,1)S(1)} copy-done((bf16[512,2048]{1,0:T(8,128)(2,1)S(1)}, bf16[512,2048]{1,0:T(8,128)(2,1)}, u32[]{:S(2)}) %copy-start.2) | copy-done | bytes 2097176
  3.9 2.1 %block_state.2 = f32[16,64,128]{2,1,0:T(8,128)S(1)} custom-call(s32[3]{0:T(128)S(1)} %pad_add_fusion.place_ref.refs_0_, bf16[512,4096]{1,0:T(8,128)(2,1)S(1)} %copy-done, bf16[512,2048]{1,0:T(8,128)(2,1)S(1)} %copy-done.2), custom_call_target="tpu_custom_call" | custom-call | flops 268435456 | bytes 4194304 | tf_op jit(solution)/shard_map/block_state/pallas_call | solution.py:73
  6.0 3.3 %collective-permute-start = (f32[16,64,128]{2,1,0:T(8,128)S(1)}, f32[16,64,128]{2,1,0:T(8,128)S(1)}, u32[]{:S(2)}, u32[]{:S(2)}) collective-permute-start(f32[16,64,128]{2,1,0:T(8,128)S(1)} %block_state.2), channel_id=1, source_target_pairs={{0,1},{1,0},{2,3},{3,2},{4,5},{5,4},{6,7},{7,6},{8,9},{9,8},{10,11... | collective-permute-start | bytes 1572872 | tf_op jit(solution)/shard_map/ppermute | solution.py:28
  9.3 2.1 %block_state.3 = f32[16,64,128]{2,1,0:T(8,128)S(1)} custom-call(s32[3]{0:T(128)S(1)} %pad_add_fusion.place_ref.refs_0_, bf16[512,4096]{1,0:T(8,128)(2,1)S(1)} %copy-done, bf16[512,2048]{1,0:T(8,128)(2,1)S(1)} %copy-done.2), custom_call_target="tpu_custom_call" | custom-call | flops 268435456 | bytes 4194304 | tf_op jit(solution)/shard_map/block_state/pallas_call | solution.py:73
  12.4 3.5 %all-to-all-start = ((f32[4,4,64,128]{3,2,1,0:T(8,128)}), f32[4,4,64,128]{3,2,1,0:T(8,128)S(1)}, u32[]{:S(2)}, u32[]{:S(2)}) async-start(f32[4,4,64,128]{3,2,1,0:T(8,128)} %bitcast.3), calls=%async_computation | async-start | bytes 1048576 | tf_op jit(solution)/shard_map/all_to_all | solution.py:322
  15.9 11.4 %local_attention.1.refs_2_ = bf16[32,64,512]{2,1,0:T(8,128)(2,1)} custom-call(s32[3]{0:T(128)} %copy-done.4, bf16[512,4096]{1,0:T(8,128)(2,1)} %refs_1_.5, bf16[512,4096]{1,0:T(8,128)(2,1)} %k_ref.1, bf16[512,2048]{1,0:T(8,128)(2,1)} %v_ref.1, bf16[18,32,512]{2,1,0:T(8,128)(2,1)} %bitcast.24), custom_call_target="tpu_custom_call" | custom-call | flops 8589934592 | bytes 16777216 | tf_op jit(solution)/shard_map/local_attention/pallas_call | solution.py:166
  27.9 1.5 %collective-permute-start.2 = (f32[16,64,128]{2,1,0:T(8,128)}, f32[16,64,128]{2,1,0:T(8,128)S(1)}, u32[]{:S(2)}, u32[]{:S(2)}) collective-permute-start(f32[16,64,128]{2,1,0:T(8,128)} %add.44), channel_id=1, source_target_pairs={{0,2},{2,0},{4,6},{6,4},{1,3},{3,1},{5,7},{7,5},{8,10},{10,8},{12,... | collective-permute-start | bytes 1572872 | tf_op jit(solution)/shard_map/ppermute | solution.py:28
  29.3 2.7 %collective-permute-done.5 = f32[4,64,128]{2,1,0:T(8,128)S(1)} collective-permute-done((f32[4,64,128]{2,1,0:T(8,128)S(1)}, f32[4,64,128]{2,1,0:T(8,128)S(1)}, u32[]{:S(2)}, u32[]{:S(2)}) %collective-permute-start.5) | collective-permute-done | bytes 131104 | tf_op jit(solution)/shard_map/ppermute | solution.py:28
  32.1 1.9 %collective-permute-start.6 = (f32[4,64,128]{2,1,0:T(8,128)S(1)}, f32[4,64,128]{2,1,0:T(8,128)S(1)}, u32[]{:S(2)}, u32[]{:S(2)}) collective-permute-start(f32[4,64,128]{2,1,0:T(8,128)S(1)} %fusion), channel_id=1, source_target_pairs={{0,16},{8,24},{16,0},{24,8},{32,48},{40,56},{48,32},{56,40},{1,17}... | collective-permute-start | bytes 393224 | tf_op jit(solution)/shard_map/ppermute | solution.py:28
  34.0 6.8 %collective-permute-done.6 = f32[4,64,128]{2,1,0:T(8,128)S(1)} collective-permute-done((f32[4,64,128]{2,1,0:T(8,128)S(1)}, f32[4,64,128]{2,1,0:T(8,128)S(1)}, u32[]{:S(2)}, u32[]{:S(2)}) %collective-permute-start.6) | collective-permute-done | bytes 131104 | tf_op jit(solution)/shard_map/ppermute | solution.py:28
  40.8 1.1 %broadcast_in_dim.2 = f32[4,2,4,64,128]{4,3,2,1,0:T(8,128)} broadcast(f32[2,4,64,128]{3,2,1,0:T(8,128)S(1)} %pad_maximum_fusion.2), dimensions={1,2,3,4} | broadcast | bytes 1310720 | tf_op jit(solution)/shard_map/broadcast_in_dim | solution.py:326
  41.9 3.7 %all-to-all-start.1 = ((f32[4,2,4,64,128]{4,3,2,1,0:T(8,128)}), f32[4,2,4,64,128]{4,3,2,1,0:T(8,128)S(1)}, u32[]{:S(2)}, u32[]{:S(2)}) async-start(f32[4,2,4,64,128]{4,3,2,1,0:T(8,128)} %broadcast_in_dim.2), calls=%async_computation.1 | async-start | bytes 2097152 | tf_op jit(solution)/shard_map/all_to_all | solution.py:322
  45.6 1.2 %add.45 = f32[16,64,128]{2,1,0:T(8,128)S(1)} add(f32[16,64,128]{2,1,0:T(8,128)} %add.44, f32[16,64,128]{2,1,0:T(8,128)S(1)} %collective-permute-done.2) | non-fusion elementwise | flops 131072 | bytes 1572864 | tf_op jit(solution)/shard_map/add | solution.py:354
  46.8 2.8 %collective-permute-start.4 = (f32[16,64,128]{2,1,0:T(8,128)S(1)}, f32[16,64,128]{2,1,0:T(8,128)S(1)}, u32[]{:S(2)}, u32[]{:S(2)}) collective-permute-start(f32[16,64,128]{2,1,0:T(8,128)S(1)} %add.45), channel_id=1, source_target_pairs={{0,6},{2,4},{4,2},{6,0},{1,7},{3,5},{5,3},{7,1},{8,14},{10,12},{12... | collective-permute-start | bytes 1572872 | tf_op jit(solution)/shard_map/ppermute | solution.py:28
  49.6 2.0 %collective-permute-start.3 = (f32[4,1,4,64,128]{4,3,2,1,0:T(8,128)S(1)}, f32[4,1,4,64,128]{4,3,2,1,0:T(8,128)S(1)}, u32[]{:S(2)}, u32[]{:S(2)}) collective-permute-start(f32[4,1,4,64,128]{4,3,2,1,0:T(8,128)S(1)} %bitcast.29), channel_id=1, source_target_pairs={{0,1},{1,0},{2,3},{3,2},{4,5},{5,4},{6,7},{7,6},{8,9},{9,8},{10,11... | collective-permute-start | bytes 1572872 | tf_op jit(solution)/shard_map/ppermute | solution.py:28
  51.6 5.4 %collective-permute-start.7 = (f32[4,64,128]{2,1,0:T(8,128)S(1)}, f32[4,64,128]{2,1,0:T(8,128)S(1)}, u32[]{:S(2)}, u32[]{:S(2)}) collective-permute-start(f32[4,64,128]{2,1,0:T(8,128)S(1)} %add.51), channel_id=1, source_target_pairs={{0,32},{8,40},{16,48},{24,56},{32,0},{40,8},{48,16},{56,24},{1,33}... | collective-permute-start | bytes 393224 | tf_op jit(solution)/shard_map/ppermute | solution.py:28
  57.0 3.7 %collective-permute-done.7 = f32[4,64,128]{2,1,0:T(8,128)S(1)} collective-permute-done((f32[4,64,128]{2,1,0:T(8,128)S(1)}, f32[4,64,128]{2,1,0:T(8,128)S(1)}, u32[]{:S(2)}, u32[]{:S(2)}) %collective-permute-start.7) | collective-permute-done | bytes 131104 | tf_op jit(solution)/shard_map/ppermute | solution.py:28
  60.7 3.0 %collective-permute-start.10 = (f32[4,64,128]{2,1,0:T(8,128)S(1)}, f32[4,64,128]{2,1,0:T(8,128)S(1)}, u32[]{:S(2)}, u32[]{:S(2)}) collective-permute-start(f32[4,64,128]{2,1,0:T(8,128)S(1)} %add.52), channel_id=1, source_target_pairs={{0,192},{64,128},{128,64},{192,0},{1,193},{65,129},{129,65},{193,1... | collective-permute-start | bytes 393224 | tf_op jit(solution)/shard_map/ppermute | solution.py:28
  64.4 3.5 %collective-permute-done.10 = f32[4,64,128]{2,1,0:T(8,128)S(1)} collective-permute-done((f32[4,64,128]{2,1,0:T(8,128)S(1)}, f32[4,64,128]{2,1,0:T(8,128)S(1)}, u32[]{:S(2)}, u32[]{:S(2)}) %collective-permute-start.10) | collective-permute-done | bytes 131104 | tf_op jit(solution)/shard_map/ppermute | solution.py:28
  67.9 1.2 %collective-permute-done.9 = f32[4,64,128]{2,1,0:T(8,128)S(1)} collective-permute-done((f32[4,64,128]{2,1,0:T(8,128)S(1)}, f32[4,64,128]{2,1,0:T(8,128)S(1)}, u32[]{:S(2)}, u32[]{:S(2)}) %collective-permute-start.9) | collective-permute-done | bytes 131104 | tf_op jit(solution)/shard_map/ppermute | solution.py:28
  72.0 2.4 %collective-permute-start.12 = (f32[4,2,4,64,128]{4,3,2,1,0:T(8,128)S(1)}, f32[4,2,4,64,128]{4,3,2,1,0:T(8,128)S(1)}, u32[]{:S(2)}, u32[]{:S(2)}) collective-permute-start(f32[4,2,4,64,128]{4,3,2,1,0:T(8,128)S(1)} %all-to-all-done.1.refs_10_), channel_id=1, source_target_pairs={{0,1},{1,0},{2,3},{3,2},{4,5},{5,4},{6,7},{7,6},{8,9},{9,8},{10,11... | collective-permute-start | bytes 3145736 | tf_op jit(solution)/shard_map/ppermute | solution.py:28
  74.4 1.2 %collective-permute-start.14 = (f32[3,4,64,128]{3,2,1,0:T(8,128)}, f32[3,4,64,128]{3,2,1,0:T(8,128)S(1)}, u32[]{:S(2)}, u32[]{:S(2)}) collective-permute-start(f32[3,4,64,128]{3,2,1,0:T(8,128)} %pad_maximum_fusion.1), channel_id=1, source_target_pairs={{0,4},{2,6},{4,0},{6,2},{1,5},{3,7},{5,1},{7,3},{8,12},{10,14},{12... | collective-permute-start | bytes 1179656 | tf_op jit(solution)/shard_map/ppermute | solution.py:28
  75.5 2.7 %collective-permute-start.15 = (f32[3,4,64,128]{3,2,1,0:T(8,128)}, f32[3,4,64,128]{3,2,1,0:T(8,128)S(1)}, u32[]{:S(2)}, u32[]{:S(2)}) collective-permute-start(f32[3,4,64,128]{3,2,1,0:T(8,128)} %pad_maximum_fusion.1), channel_id=1, source_target_pairs={{0,6},{2,4},{4,2},{6,0},{1,7},{3,5},{5,3},{7,1},{8,14},{10,12},{12... | collective-permute-start | bytes 1179656 | tf_op jit(solution)/shard_map/ppermute | solution.py:28
  78.3 2.2 %copy-done.1 = bf16[512,4096]{1,0:T(8,128)(2,1)S(1)} copy-done((bf16[512,4096]{1,0:T(8,128)(2,1)S(1)}, bf16[512,4096]{1,0:T(8,128)(2,1)}, u32[]{:S(2)}) %copy-start.1) | copy-done | bytes 4194328
  82.5 1.6 %copy-done.10 = bf16[32,64,512]{2,1,0:T(8,128)(2,1)S(1)} copy-done((bf16[32,64,512]{2,1,0:T(8,128)(2,1)S(1)}, bf16[32,64,512]{2,1,0:T(8,128)(2,1)}, u32[]{:S(2)}) %copy-start.10) | copy-done | bytes 2097176
  84.1 5.9 %readout.1.refs_2_ = f32[32,64,512]{2,1,0:T(8,128)S(1)} custom-call(s32[3]{0:T(128)S(1)} %copy-done.5, bf16[512,4096]{1,0:T(8,128)(2,1)S(1)} %copy-done.1, bf16[32,64,512]{2,1,0:T(8,128)(2,1)S(1)} %copy-done.10, bf16[18,32,512]{2,1,0:T(8,128)(2,1)S(1)} %bitcast.25, f32[4,1,4,64,128]{4,3,2,1,0:T(8,128)S(1)} %bitcast.28, f32[4,1,4,64,128]{4,3,2,1,0:T(8,128)S(1)} %bitcast.33, ...), custom_call_target="tpu_custom_call" | custom-call | flops 5368709120 | bytes 16777216 | tf_op jit(solution)/shard_map/readout/pallas_call | solution.py:295
  90.1 2.9 %collective-permute-done.14 = f32[3,4,64,128]{3,2,1,0:T(8,128)S(1)} collective-permute-done((f32[3,4,64,128]{3,2,1,0:T(8,128)}, f32[3,4,64,128]{3,2,1,0:T(8,128)S(1)}, u32[]{:S(2)}, u32[]{:S(2)}) %collective-permute-start.14) | collective-permute-done | bytes 393248 | tf_op jit(solution)/shard_map/ppermute | solution.py:28
  92.9 2.1 %collective-permute-done.15 = f32[3,4,64,128]{3,2,1,0:T(8,128)S(1)} collective-permute-done((f32[3,4,64,128]{3,2,1,0:T(8,128)}, f32[3,4,64,128]{3,2,1,0:T(8,128)S(1)}, u32[]{:S(2)}, u32[]{:S(2)}) %collective-permute-start.15) | collective-permute-done | bytes 393248 | tf_op jit(solution)/shard_map/ppermute | solution.py:28
  95.2 2.0 %collective-permute-start.16 = (f32[4,3,4,64,128]{4,3,2,1,0:T(8,128)S(1)}, f32[4,3,4,64,128]{4,3,2,1,0:T(8,128)S(1)}, u32[]{:S(2)}, u32[]{:S(2)}) collective-permute-start(f32[4,3,4,64,128]{4,3,2,1,0:T(8,128)S(1)} %pad_maximum_fusion.refs_5_), channel_id=1, source_target_pairs={{0,1},{1,0},{2,3},{3,2},{4,5},{5,4},{6,7},{7,6},{8,9},{9,8},{10,11... | collective-permute-start | bytes 4718600 | tf_op jit(solution)/shard_map/ppermute | solution.py:28
  97.2 3.8 %readout_last.2.refs_5_ = bf16[512,2048]{1,0:T(8,128)(2,1)} custom-call(s32[3]{0:T(128)S(1)} %copy-done.5, bf16[512,4096]{1,0:T(8,128)(2,1)S(1)} %copy-done.1, f32[32,64,512]{2,1,0:T(8,128)S(1)} %readout.1.refs_2_, bf16[18,32,512]{2,1,0:T(8,128)(2,1)S(1)} %bitcast.26, f32[1,2048]{1,0:T(1,128)S(1)} %bitcast.31, f32[4,3,4,64,128]{4,3,2,1,0:T(8,128)S(1)} %pad_maximum_fusion.refs_5_), custom_call_target="tpu_custom_call" | custom-call | flops 3221225472 | bytes 16777216 | tf_op jit(solution)/shard_map/readout_last/pallas_call | solution.py:295
  101.0 3.8 %readout_last.3 = bf16[512,2048]{1,0:T(8,128)(2,1)} custom-call(s32[3]{0:T(128)S(1)} %copy-done.5, bf16[512,4096]{1,0:T(8,128)(2,1)S(1)} %copy-done.1, f32[32,64,512]{2,1,0:T(8,128)S(1)} %readout.1.refs_2_, bf16[18,32,512]{2,1,0:T(8,128)(2,1)S(1)} %bitcast.27, f32[1,2048]{1,0:T(1,128)S(1)} %bitcast.32, ...), custom_call_target="tpu_custom_call", output_to_operand_aliasing={{}: (5, {})} | custom-call | flops 3221225472 | bytes 16777216 | tf_op jit(solution)/shard_map/readout_last/pallas_call | solution.py:295
  (51 shorter events, 7.5 us)
Async XLA Ops:
  0.1 2.2 %copy-start = (bf16[512,4096]{1,0:T(8,128)(2,1)S(1)}, bf16[512,4096]{1,0:T(8,128)(2,1)}, u32[]{:S(2)}) copy-start(bf16[512,4096]{1,0:T(8,128)(2,1)} %k_ref.1) | copy-start | bytes 12582916
  2.3 1.6 %copy-start.2 = (bf16[512,2048]{1,0:T(8,128)(2,1)S(1)}, bf16[512,2048]{1,0:T(8,128)(2,1)}, u32[]{:S(2)}) copy-start(bf16[512,2048]{1,0:T(8,128)(2,1)} %v_ref.1) | copy-start | bytes 6291460
  3.9 5.5 %copy-start.4 = (s32[3]{0:T(128)}, s32[3]{0:T(128)S(1)}, u32[]{:S(2)}) copy-start(s32[3]{0:T(128)S(1)} %pad_add_fusion.place_ref.refs_0_) | copy-start | bytes 40
  6.0 5.5 %collective-permute-start = (f32[16,64,128]{2,1,0:T(8,128)S(1)}, f32[16,64,128]{2,1,0:T(8,128)S(1)}, u32[]{:S(2)}, u32[]{:S(2)}) collective-permute-start(f32[16,64,128]{2,1,0:T(8,128)S(1)} %block_state.2), channel_id=1, source_target_pairs={{0,1},{1,0},{2,3},{3,2},{4,5},{5,4},{6,7},{7,6},{8,9},{9,8},{10,11... | collective-permute-start | bytes 1572872 | tf_op jit(solution)/shard_map/ppermute | solution.py:28
  12.4 14.9 %collective-permute-start.1 = (f32[16,64,128]{2,1,0:T(8,128)S(1)}, f32[16,64,128]{2,1,0:T(8,128)S(1)}, u32[]{:S(2)}, u32[]{:S(2)}) collective-permute-start(f32[16,64,128]{2,1,0:T(8,128)S(1)} %block_state.3), channel_id=1, source_target_pairs={{0,1},{1,0},{2,3},{3,2},{4,5},{5,4},{6,7},{7,6},{8,9},{9,8},{10,11... | collective-permute-start | bytes 1572872 | tf_op jit(solution)/shard_map/ppermute | solution.py:28
  12.4 14.9 %all-to-all-start = ((f32[4,4,64,128]{3,2,1,0:T(8,128)}), f32[4,4,64,128]{3,2,1,0:T(8,128)S(1)}, u32[]{:S(2)}, u32[]{:S(2)}) async-start(f32[4,4,64,128]{3,2,1,0:T(8,128)} %bitcast.3), calls=%async_computation | async-start | bytes 1048576 | tf_op jit(solution)/shard_map/all_to_all | solution.py:322
  27.4 4.7 %collective-permute-start.5 = (f32[4,64,128]{2,1,0:T(8,128)S(1)}, f32[4,64,128]{2,1,0:T(8,128)S(1)}, u32[]{:S(2)}, u32[]{:S(2)}) collective-permute-start(f32[4,64,128]{2,1,0:T(8,128)S(1)} %add_bitcast_fusion.1), channel_id=1, source_target_pairs={{0,8},{8,0},{16,24},{24,16},{32,40},{40,32},{48,56},{56,48},{1,9},... | collective-permute-start | bytes 393224 | tf_op jit(solution)/shard_map/ppermute | solution.py:28
  27.9 17.7 %collective-permute-start.2 = (f32[16,64,128]{2,1,0:T(8,128)}, f32[16,64,128]{2,1,0:T(8,128)S(1)}, u32[]{:S(2)}, u32[]{:S(2)}) collective-permute-start(f32[16,64,128]{2,1,0:T(8,128)} %add.44), channel_id=1, source_target_pairs={{0,2},{2,0},{4,6},{6,4},{1,3},{3,1},{5,7},{7,5},{8,10},{10,8},{12,... | collective-permute-start | bytes 1572872 | tf_op jit(solution)/shard_map/ppermute | solution.py:28
  32.1 8.7 %collective-permute-start.6 = (f32[4,64,128]{2,1,0:T(8,128)S(1)}, f32[4,64,128]{2,1,0:T(8,128)S(1)}, u32[]{:S(2)}, u32[]{:S(2)}) collective-permute-start(f32[4,64,128]{2,1,0:T(8,128)S(1)} %fusion), channel_id=1, source_target_pairs={{0,16},{8,24},{16,0},{24,8},{32,48},{40,56},{48,32},{56,40},{1,17}... | collective-permute-start | bytes 393224 | tf_op jit(solution)/shard_map/ppermute | solution.py:28
  41.9 30.1 %all-to-all-start.1 = ((f32[4,2,4,64,128]{4,3,2,1,0:T(8,128)}), f32[4,2,4,64,128]{4,3,2,1,0:T(8,128)S(1)}, u32[]{:S(2)}, u32[]{:S(2)}) async-start(f32[4,2,4,64,128]{4,3,2,1,0:T(8,128)} %broadcast_in_dim.2), calls=%async_computation.1 | async-start | bytes 2097152 | tf_op jit(solution)/shard_map/all_to_all | solution.py:322
  45.6 32.6 %copy-start.3 = (bf16[512,18,32]{0,2,1:T(8,128)(2,1)S(1)}, bf16[512,18,32]{0,2,1:T(8,128)(2,1)}, u32[]{:S(2)}) copy-start(bf16[512,18,32]{0,2,1:T(8,128)(2,1)} %param.8) | copy-start | bytes 1769476
  45.6 32.6 %copy-start.5 = (s32[3]{0:T(128)S(1)}, s32[3]{0:T(128)}, u32[]{:S(2)}) copy-start(s32[3]{0:T(128)} %copy-done.4) | copy-start | bytes 40
  46.8 23.4 %collective-permute-start.4 = (f32[16,64,128]{2,1,0:T(8,128)S(1)}, f32[16,64,128]{2,1,0:T(8,128)S(1)}, u32[]{:S(2)}, u32[]{:S(2)}) collective-permute-start(f32[16,64,128]{2,1,0:T(8,128)S(1)} %add.45), channel_id=1, source_target_pairs={{0,6},{2,4},{4,2},{6,0},{1,7},{3,5},{5,3},{7,1},{8,14},{10,12},{12... | collective-permute-start | bytes 1572872 | tf_op jit(solution)/shard_map/ppermute | solution.py:28
  49.6 20.7 %collective-permute-start.3 = (f32[4,1,4,64,128]{4,3,2,1,0:T(8,128)S(1)}, f32[4,1,4,64,128]{4,3,2,1,0:T(8,128)S(1)}, u32[]{:S(2)}, u32[]{:S(2)}) collective-permute-start(f32[4,1,4,64,128]{4,3,2,1,0:T(8,128)S(1)} %bitcast.29), channel_id=1, source_target_pairs={{0,1},{1,0},{2,3},{3,2},{4,5},{5,4},{6,7},{7,6},{8,9},{9,8},{10,11... | collective-permute-start | bytes 1572872 | tf_op jit(solution)/shard_map/ppermute | solution.py:28
  51.6 9.1 %collective-permute-start.7 = (f32[4,64,128]{2,1,0:T(8,128)S(1)}, f32[4,64,128]{2,1,0:T(8,128)S(1)}, u32[]{:S(2)}, u32[]{:S(2)}) collective-permute-start(f32[4,64,128]{2,1,0:T(8,128)S(1)} %add.51), channel_id=1, source_target_pairs={{0,32},{8,40},{16,48},{24,56},{32,0},{40,8},{48,16},{56,24},{1,33}... | collective-permute-start | bytes 393224 | tf_op jit(solution)/shard_map/ppermute | solution.py:28
  60.7 7.2 %collective-permute-start.10 = (f32[4,64,128]{2,1,0:T(8,128)S(1)}, f32[4,64,128]{2,1,0:T(8,128)S(1)}, u32[]{:S(2)}, u32[]{:S(2)}) collective-permute-start(f32[4,64,128]{2,1,0:T(8,128)S(1)} %add.52), channel_id=1, source_target_pairs={{0,192},{64,128},{128,64},{192,0},{1,193},{65,129},{129,65},{193,1... | collective-permute-start | bytes 393224 | tf_op jit(solution)/shard_map/ppermute | solution.py:28
  63.7 5.4 %collective-permute-start.9 = (f32[4,64,128]{2,1,0:T(8,128)S(1)}, f32[4,64,128]{2,1,0:T(8,128)S(1)}, u32[]{:S(2)}, u32[]{:S(2)}) collective-permute-start(f32[4,64,128]{2,1,0:T(8,128)S(1)} %add.52), channel_id=1, source_target_pairs={{0,128},{64,192},{128,0},{192,64},{1,129},{65,193},{129,1},{193,65... | collective-permute-start | bytes 393224 | tf_op jit(solution)/shard_map/ppermute | solution.py:28
  64.0 5.1 %collective-permute-start.8 = (f32[4,64,128]{2,1,0:T(8,128)S(1)}, f32[4,64,128]{2,1,0:T(8,128)S(1)}, u32[]{:S(2)}, u32[]{:S(2)}) collective-permute-start(f32[4,64,128]{2,1,0:T(8,128)S(1)} %add.52), channel_id=1, source_target_pairs={{0,64},{64,0},{128,192},{192,128},{1,65},{65,1},{129,193},{193,129... | collective-permute-start | bytes 393224 | tf_op jit(solution)/shard_map/ppermute | solution.py:28
  70.2 1.0 copy-start.6
  70.2 0.8 copy-start.8
  72.0 6.2 %collective-permute-start.12 = (f32[4,2,4,64,128]{4,3,2,1,0:T(8,128)S(1)}, f32[4,2,4,64,128]{4,3,2,1,0:T(8,128)S(1)}, u32[]{:S(2)}, u32[]{:S(2)}) collective-permute-start(f32[4,2,4,64,128]{4,3,2,1,0:T(8,128)S(1)} %all-to-all-done.1.refs_10_), channel_id=1, source_target_pairs={{0,1},{1,0},{2,3},{3,2},{4,5},{5,4},{6,7},{7,6},{8,9},{9,8},{10,11... | collective-permute-start | bytes 3145736 | tf_op jit(solution)/shard_map/ppermute | solution.py:28
  74.4 3.9 %collective-permute-start.11 = (f32[4,1,4,64,128]{4,3,2,1,0:T(8,128)}, f32[4,1,4,64,128]{4,3,2,1,0:T(8,128)S(1)}, u32[]{:S(2)}, u32[]{:S(2)}) collective-permute-start(f32[4,1,4,64,128]{4,3,2,1,0:T(8,128)} %bitcast.34), channel_id=1, source_target_pairs={{0,1},{1,0},{2,3},{3,2},{4,5},{5,4},{6,7},{7,6},{8,9},{9,8},{10,11... | collective-permute-start | bytes 1572872 | tf_op jit(solution)/shard_map/ppermute | solution.py:28
  74.4 15.7 %collective-permute-start.13 = (f32[3,4,64,128]{3,2,1,0:T(8,128)}, f32[3,4,64,128]{3,2,1,0:T(8,128)S(1)}, u32[]{:S(2)}, u32[]{:S(2)}) collective-permute-start(f32[3,4,64,128]{3,2,1,0:T(8,128)} %pad_maximum_fusion.1), channel_id=1, source_target_pairs={{0,2},{2,0},{4,6},{6,4},{1,3},{3,1},{5,7},{7,5},{8,10},{10,8},{12,... | collective-permute-start | bytes 1179656 | tf_op jit(solution)/shard_map/ppermute | solution.py:28
  74.4 18.6 %collective-permute-start.14 = (f32[3,4,64,128]{3,2,1,0:T(8,128)}, f32[3,4,64,128]{3,2,1,0:T(8,128)S(1)}, u32[]{:S(2)}, u32[]{:S(2)}) collective-permute-start(f32[3,4,64,128]{3,2,1,0:T(8,128)} %pad_maximum_fusion.1), channel_id=1, source_target_pairs={{0,4},{2,6},{4,0},{6,2},{1,5},{3,7},{5,1},{7,3},{8,12},{10,14},{12... | collective-permute-start | bytes 1179656 | tf_op jit(solution)/shard_map/ppermute | solution.py:28
  75.5 19.5 %collective-permute-start.15 = (f32[3,4,64,128]{3,2,1,0:T(8,128)}, f32[3,4,64,128]{3,2,1,0:T(8,128)S(1)}, u32[]{:S(2)}, u32[]{:S(2)}) collective-permute-start(f32[3,4,64,128]{3,2,1,0:T(8,128)} %pad_maximum_fusion.1), channel_id=1, source_target_pairs={{0,6},{2,4},{4,2},{6,0},{1,7},{3,5},{5,3},{7,1},{8,14},{10,12},{12... | collective-permute-start | bytes 1179656 | tf_op jit(solution)/shard_map/ppermute | solution.py:28
  78.2 2.2 %copy-start.1 = (bf16[512,4096]{1,0:T(8,128)(2,1)S(1)}, bf16[512,4096]{1,0:T(8,128)(2,1)}, u32[]{:S(2)}) copy-start(bf16[512,4096]{1,0:T(8,128)(2,1)} %refs_1_.5) | copy-start | bytes 12582916
  80.4 1.0 copy-start.7
  81.5 1.0 copy-start.9
  82.5 1.6 %copy-start.10 = (bf16[32,64,512]{2,1,0:T(8,128)(2,1)S(1)}, bf16[32,64,512]{2,1,0:T(8,128)(2,1)}, u32[]{:S(2)}) copy-start(bf16[32,64,512]{2,1,0:T(8,128)(2,1)} %local_attention.1.refs_2_) | copy-start | bytes 6291460
  84.1 10.9 %copy-start.11 = (f32[3,4,64,128]{3,2,1,0:T(8,128)S(1)}, f32[3,4,64,128]{3,2,1,0:T(8,128)}, u32[]{:S(2)}) copy-start(f32[3,4,64,128]{3,2,1,0:T(8,128)} %pad_maximum_fusion.1) | copy-start | bytes 1179652
  95.0 2.2 %copy-start.12 = (bf16[2048]{0:T(1024)(128)(2,1)S(1)}, bf16[2048]{0:T(1024)(128)(2,1)}, u32[]{:S(2)}) copy-start(bf16[2048]{0:T(1024)(128)(2,1)} %param.9) | copy-start | bytes 12292
  95.2 5.8 %collective-permute-start.16 = (f32[4,3,4,64,128]{4,3,2,1,0:T(8,128)S(1)}, f32[4,3,4,64,128]{4,3,2,1,0:T(8,128)S(1)}, u32[]{:S(2)}, u32[]{:S(2)}) collective-permute-start(f32[4,3,4,64,128]{4,3,2,1,0:T(8,128)S(1)} %pad_maximum_fusion.refs_5_), channel_id=1, source_target_pairs={{0,1},{1,0},{2,3},{3,2},{4,5},{5,4},{6,7},{7,6},{8,9},{9,8},{10,11... | collective-permute-start | bytes 4718600 | tf_op jit(solution)/shard_map/ppermute | solution.py:28

commit v5 on v4

--- a/solution.py
+++ b/solution.py
@@ -121,7 +121,7 @@
 
         @pl.when(step % 4 == r)
         def _():
-            w_ref[...] = lw_ref[:LOCAL, r * GROUP : (r + 1) * GROUP].astype(F32)
+            w_ref[...] = lw_ref[:, r * GROUP : (r + 1) * GROUP].astype(F32)
 
     def row(level, head, at, size):
         return w_ref[level, head : head + 1, at : at + size]
@@ -172,7 +172,7 @@
                 pl.BlockSpec((TOK, GROUP * DK), lambda i, p: (0, i)),
                 pl.BlockSpec((TOK, GROUP * DK), lambda i, p: (0, i)),
                 pl.BlockSpec((TOK, GROUP * DV), lambda i, p: (0, i)),
-                pl.BlockSpec((LEVELS, SIDE, TOK), lambda i, p: (0, i // 4, 0)),
+                pl.BlockSpec((LOCAL, SIDE, TOK), lambda i, p: (0, i // 4, 0)),
             ],
             out_specs=pl.BlockSpec((GROUP, DV, TOK), lambda i, p: (i, 0, 0)),
             scratch_shapes=[pltpu.VMEM((LOCAL, GROUP, TOK), F32)],

time: 106 us -> 106 us (level)
  no operation moved by 1% of the time
where the time goes in v5:
time: 106 us; the launch traced here: 105 us
  starting transfers between devices  36.5 us (34%)
  Pallas kernels  29.2 us (28%)
  waiting for transfers between devices  24 us (23%)
  local copies, waits for them, and re-layouts  11.7 us (11%)
  other arithmetic  3.2 us (3%)
    ppermute x17, starting transfers between devices, xor_permute(): return lax.ppermute(value, axis, [(i, i ^ mask) for i in range(size)])  29.3 us
    ppermute x17, waiting for transfers between devices, xor_permute(): return lax.ppermute(value, axis, [(i, i ^ mask) for i in range(size)])  24 us
    pallas_call x3, Pallas kernels, readout(): pl.pallas_call(functools.partial(readout_kernel, base, counts, last, part...  13.5 us
    pallas_call x1, Pallas kernels, local_attention(): pl.pallas_call(local_kernel, grid_spec=pltpu.PrefetchScalarGridSpec(num_s...  11.4 us
    unnamed x26, local copies, waits for them, and re-layouts  10.6 us
    all_to_all x2, starting transfers between devices, row_exchange(): return lax.all_to_all(payload, 'x', 0, 0, tiled=True)  7.18 us
    pallas_call x2, Pallas kernels, block_state(): pl.pallas_call(functools.partial(state_kernel, other), in_specs=[pl.Block...  4.29 us
  transfers between devices with their start and end apart: 19, of which 8 were waited for; matrix products, arithmetic and copies ran while one was open for 3% of the time, Pallas kernels for 22%

profile of v5, /device:TPU:1, one launch (start us, length us, event | category | flops | bytes accessed | tf_op | source)
XLA Modules:
  0.0 104.8 jit_solution(7392259792430459804)
XLA Ops:
  0.1 2.2 %copy-done = bf16[512,4096]{1,0:T(8,128)(2,1)S(1)} copy-done((bf16[512,4096]{1,0:T(8,128)(2,1)S(1)}, bf16[512,4096]{1,0:T(8,128)(2,1)}, u32[]{:S(2)}) %copy-start) | copy-done | bytes 4194328
  2.3 1.6 %copy-done.2 = bf16[512,2048]{1,0:T(8,128)(2,1)S(1)} copy-done((bf16[512,2048]{1,0:T(8,128)(2,1)S(1)}, bf16[512,2048]{1,0:T(8,128)(2,1)}, u32[]{:S(2)}) %copy-start.2) | copy-done | bytes 2097176
  3.9 2.1 %block_state.2 = f32[16,64,128]{2,1,0:T(8,128)S(1)} custom-call(s32[3]{0:T(128)S(1)} %pad_add_fusion.place_ref.refs_0_, bf16[512,4096]{1,0:T(8,128)(2,1)S(1)} %copy-done, bf16[512,2048]{1,0:T(8,128)(2,1)S(1)} %copy-done.2), custom_call_target="tpu_custom_call" | custom-call | flops 268435456 | bytes 4194304 | tf_op jit(solution)/shard_map/block_state/pallas_call | solution.py:73
  6.0 3.3 %collective-permute-start = (f32[16,64,128]{2,1,0:T(8,128)S(1)}, f32[16,64,128]{2,1,0:T(8,128)S(1)}, u32[]{:S(2)}, u32[]{:S(2)}) collective-permute-start(f32[16,64,128]{2,1,0:T(8,128)S(1)} %block_state.2), channel_id=1, source_target_pairs={{0,1},{1,0},{2,3},{3,2},{4,5},{5,4},{6,7},{7,6},{8,9},{9,8},{10,11... | collective-permute-start | bytes 1572872 | tf_op jit(solution)/shard_map/ppermute | solution.py:28
  9.3 2.1 %block_state.3 = f32[16,64,128]{2,1,0:T(8,128)S(1)} custom-call(s32[3]{0:T(128)S(1)} %pad_add_fusion.place_ref.refs_0_, bf16[512,4096]{1,0:T(8,128)(2,1)S(1)} %copy-done, bf16[512,2048]{1,0:T(8,128)(2,1)S(1)} %copy-done.2), custom_call_target="tpu_custom_call" | custom-call | flops 268435456 | bytes 4194304 | tf_op jit(solution)/shard_map/block_state/pallas_call | solution.py:73
  12.4 3.5 %all-to-all-start = ((f32[4,4,64,128]{3,2,1,0:T(8,128)}), f32[4,4,64,128]{3,2,1,0:T(8,128)S(1)}, u32[]{:S(2)}, u32[]{:S(2)}) async-start(f32[4,4,64,128]{3,2,1,0:T(8,128)} %bitcast.3), calls=%async_computation | async-start | bytes 1048576 | tf_op jit(solution)/shard_map/all_to_all | solution.py:322
  15.9 11.4 %local_attention.1.refs_2_ = bf16[32,64,512]{2,1,0:T(8,128)(2,1)} custom-call(s32[3]{0:T(128)} %copy-done.4, bf16[512,4096]{1,0:T(8,128)(2,1)} %refs_1_.5, bf16[512,4096]{1,0:T(8,128)(2,1)} %k_ref.1, bf16[512,2048]{1,0:T(8,128)(2,1)} %v_ref.1, bf16[18,32,512]{2,1,0:T(8,128)(2,1)} %bitcast.24), custom_call_target="tpu_custom_call" | custom-call | flops 8589934592 | bytes 16777216 | tf_op jit(solution)/shard_map/local_attention/pallas_call | solution.py:166
  27.8 1.5 %collective-permute-start.2 = (f32[16,64,128]{2,1,0:T(8,128)}, f32[16,64,128]{2,1,0:T(8,128)S(1)}, u32[]{:S(2)}, u32[]{:S(2)}) collective-permute-start(f32[16,64,128]{2,1,0:T(8,128)} %add.44), channel_id=1, source_target_pairs={{0,2},{2,0},{4,6},{6,4},{1,3},{3,1},{5,7},{7,5},{8,10},{10,8},{12,... | collective-permute-start | bytes 1572872 | tf_op jit(solution)/shard_map/ppermute | solution.py:28
  29.3 2.7 %collective-permute-done.5 = f32[4,64,128]{2,1,0:T(8,128)S(1)} collective-permute-done((f32[4,64,128]{2,1,0:T(8,128)S(1)}, f32[4,64,128]{2,1,0:T(8,128)S(1)}, u32[]{:S(2)}, u32[]{:S(2)}) %collective-permute-start.5) | collective-permute-done | bytes 131104 | tf_op jit(solution)/shard_map/ppermute | solution.py:28
  32.0 1.9 %collective-permute-start.6 = (f32[4,64,128]{2,1,0:T(8,128)S(1)}, f32[4,64,128]{2,1,0:T(8,128)S(1)}, u32[]{:S(2)}, u32[]{:S(2)}) collective-permute-start(f32[4,64,128]{2,1,0:T(8,128)S(1)} %fusion), channel_id=1, source_target_pairs={{0,16},{8,24},{16,0},{24,8},{32,48},{40,56},{48,32},{56,40},{1,17}... | collective-permute-start | bytes 393224 | tf_op jit(solution)/shard_map/ppermute | solution.py:28
  33.9 6.8 %collective-permute-done.6 = f32[4,64,128]{2,1,0:T(8,128)S(1)} collective-permute-done((f32[4,64,128]{2,1,0:T(8,128)S(1)}, f32[4,64,128]{2,1,0:T(8,128)S(1)}, u32[]{:S(2)}, u32[]{:S(2)}) %collective-permute-start.6) | collective-permute-done | bytes 131104 | tf_op jit(solution)/shard_map/ppermute | solution.py:28
  40.7 1.1 %broadcast_in_dim.2 = f32[4,2,4,64,128]{4,3,2,1,0:T(8,128)} broadcast(f32[2,4,64,128]{3,2,1,0:T(8,128)S(1)} %pad_maximum_fusion.2), dimensions={1,2,3,4} | broadcast | bytes 1310720 | tf_op jit(solution)/shard_map/broadcast_in_dim | solution.py:326
  41.8 3.7 %all-to-all-start.1 = ((f32[4,2,4,64,128]{4,3,2,1,0:T(8,128)}), f32[4,2,4,64,128]{4,3,2,1,0:T(8,128)S(1)}, u32[]{:S(2)}, u32[]{:S(2)}) async-start(f32[4,2,4,64,128]{4,3,2,1,0:T(8,128)} %broadcast_in_dim.2), calls=%async_computation.1 | async-start | bytes 2097152 | tf_op jit(solution)/shard_map/all_to_all | solution.py:322
  45.5 1.2 %add.45 = f32[16,64,128]{2,1,0:T(8,128)S(1)} add(f32[16,64,128]{2,1,0:T(8,128)} %add.44, f32[16,64,128]{2,1,0:T(8,128)S(1)} %collective-permute-done.2) | non-fusion elementwise | flops 131072 | bytes 1572864 | tf_op jit(solution)/shard_map/add | solution.py:354
  46.7 2.8 %collective-permute-start.4 = (f32[16,64,128]{2,1,0:T(8,128)S(1)}, f32[16,64,128]{2,1,0:T(8,128)S(1)}, u32[]{:S(2)}, u32[]{:S(2)}) collective-permute-start(f32[16,64,128]{2,1,0:T(8,128)S(1)} %add.45), channel_id=1, source_target_pairs={{0,6},{2,4},{4,2},{6,0},{1,7},{3,5},{5,3},{7,1},{8,14},{10,12},{12... | collective-permute-start | bytes 1572872 | tf_op jit(solution)/shard_map/ppermute | solution.py:28
  49.5 2.0 %collective-permute-start.3 = (f32[4,1,4,64,128]{4,3,2,1,0:T(8,128)S(1)}, f32[4,1,4,64,128]{4,3,2,1,0:T(8,128)S(1)}, u32[]{:S(2)}, u32[]{:S(2)}) collective-permute-start(f32[4,1,4,64,128]{4,3,2,1,0:T(8,128)S(1)} %bitcast.29), channel_id=1, source_target_pairs={{0,1},{1,0},{2,3},{3,2},{4,5},{5,4},{6,7},{7,6},{8,9},{9,8},{10,11... | collective-permute-start | bytes 1572872 | tf_op jit(solution)/shard_map/ppermute | solution.py:28
  51.5 5.4 %collective-permute-start.7 = (f32[4,64,128]{2,1,0:T(8,128)S(1)}, f32[4,64,128]{2,1,0:T(8,128)S(1)}, u32[]{:S(2)}, u32[]{:S(2)}) collective-permute-start(f32[4,64,128]{2,1,0:T(8,128)S(1)} %add.51), channel_id=1, source_target_pairs={{0,32},{8,40},{16,48},{24,56},{32,0},{40,8},{48,16},{56,24},{1,33}... | collective-permute-start | bytes 393224 | tf_op jit(solution)/shard_map/ppermute | solution.py:28
  56.9 3.7 %collective-permute-done.7 = f32[4,64,128]{2,1,0:T(8,128)S(1)} collective-permute-done((f32[4,64,128]{2,1,0:T(8,128)S(1)}, f32[4,64,128]{2,1,0:T(8,128)S(1)}, u32[]{:S(2)}, u32[]{:S(2)}) %collective-permute-start.7) | collective-permute-done | bytes 131104 | tf_op jit(solution)/shard_map/ppermute | solution.py:28
  60.7 3.0 %collective-permute-start.10 = (f32[4,64,128]{2,1,0:T(8,128)S(1)}, f32[4,64,128]{2,1,0:T(8,128)S(1)}, u32[]{:S(2)}, u32[]{:S(2)}) collective-permute-start(f32[4,64,128]{2,1,0:T(8,128)S(1)} %add.52), channel_id=1, source_target_pairs={{0,192},{64,128},{128,64},{192,0},{1,193},{65,129},{129,65},{193,1... | collective-permute-start | bytes 393224 | tf_op jit(solution)/shard_map/ppermute | solution.py:28
  64.3 3.5 %collective-permute-done.10 = f32[4,64,128]{2,1,0:T(8,128)S(1)} collective-permute-done((f32[4,64,128]{2,1,0:T(8,128)S(1)}, f32[4,64,128]{2,1,0:T(8,128)S(1)}, u32[]{:S(2)}, u32[]{:S(2)}) %collective-permute-start.10) | collective-permute-done | bytes 131104 | tf_op jit(solution)/shard_map/ppermute | solution.py:28
  67.8 1.2 %collective-permute-done.9 = f32[4,64,128]{2,1,0:T(8,128)S(1)} collective-permute-done((f32[4,64,128]{2,1,0:T(8,128)S(1)}, f32[4,64,128]{2,1,0:T(8,128)S(1)}, u32[]{:S(2)}, u32[]{:S(2)}) %collective-permute-start.9) | collective-permute-done | bytes 131104 | tf_op jit(solution)/shard_map/ppermute | solution.py:28
  71.9 2.4 %collective-permute-start.12 = (f32[4,2,4,64,128]{4,3,2,1,0:T(8,128)S(1)}, f32[4,2,4,64,128]{4,3,2,1,0:T(8,128)S(1)}, u32[]{:S(2)}, u32[]{:S(2)}) collective-permute-start(f32[4,2,4,64,128]{4,3,2,1,0:T(8,128)S(1)} %all-to-all-done.1.refs_10_), channel_id=1, source_target_pairs={{0,1},{1,0},{2,3},{3,2},{4,5},{5,4},{6,7},{7,6},{8,9},{9,8},{10,11... | collective-permute-start | bytes 3145736 | tf_op jit(solution)/shard_map/ppermute | solution.py:28
  74.3 1.2 %collective-permute-start.14 = (f32[3,4,64,128]{3,2,1,0:T(8,128)}, f32[3,4,64,128]{3,2,1,0:T(8,128)S(1)}, u32[]{:S(2)}, u32[]{:S(2)}) collective-permute-start(f32[3,4,64,128]{3,2,1,0:T(8,128)} %pad_maximum_fusion.1), channel_id=1, source_target_pairs={{0,4},{2,6},{4,0},{6,2},{1,5},{3,7},{5,1},{7,3},{8,12},{10,14},{12... | collective-permute-start | bytes 1179656 | tf_op jit(solution)/shard_map/ppermute | solution.py:28
  75.5 2.7 %collective-permute-start.15 = (f32[3,4,64,128]{3,2,1,0:T(8,128)}, f32[3,4,64,128]{3,2,1,0:T(8,128)S(1)}, u32[]{:S(2)}, u32[]{:S(2)}) collective-permute-start(f32[3,4,64,128]{3,2,1,0:T(8,128)} %pad_maximum_fusion.1), channel_id=1, source_target_pairs={{0,6},{2,4},{4,2},{6,0},{1,7},{3,5},{5,3},{7,1},{8,14},{10,12},{12... | collective-permute-start | bytes 1179656 | tf_op jit(solution)/shard_map/ppermute | solution.py:28
  78.2 2.2 %copy-done.1 = bf16[512,4096]{1,0:T(8,128)(2,1)S(1)} copy-done((bf16[512,4096]{1,0:T(8,128)(2,1)S(1)}, bf16[512,4096]{1,0:T(8,128)(2,1)}, u32[]{:S(2)}) %copy-start.1) | copy-done | bytes 4194328
  82.5 1.6 %copy-done.10 = bf16[32,64,512]{2,1,0:T(8,128)(2,1)S(1)} copy-done((bf16[32,64,512]{2,1,0:T(8,128)(2,1)S(1)}, bf16[32,64,512]{2,1,0:T(8,128)(2,1)}, u32[]{:S(2)}) %copy-start.10) | copy-done | bytes 2097176
  84.1 5.9 %readout.1.refs_2_ = f32[32,64,512]{2,1,0:T(8,128)S(1)} custom-call(s32[3]{0:T(128)S(1)} %copy-done.5, bf16[512,4096]{1,0:T(8,128)(2,1)S(1)} %copy-done.1, bf16[32,64,512]{2,1,0:T(8,128)(2,1)S(1)} %copy-done.10, bf16[18,32,512]{2,1,0:T(8,128)(2,1)S(1)} %bitcast.25, f32[4,1,4,64,128]{4,3,2,1,0:T(8,128)S(1)} %bitcast.28, f32[4,1,4,64,128]{4,3,2,1,0:T(8,128)S(1)} %bitcast.33, ...), custom_call_target="tpu_custom_call" | custom-call | flops 5368709120 | bytes 16777216 | tf_op jit(solution)/shard_map/readout/pallas_call | solution.py:295
  90.0 2.9 %collective-permute-done.14 = f32[3,4,64,128]{3,2,1,0:T(8,128)S(1)} collective-permute-done((f32[3,4,64,128]{3,2,1,0:T(8,128)}, f32[3,4,64,128]{3,2,1,0:T(8,128)S(1)}, u32[]{:S(2)}, u32[]{:S(2)}) %collective-permute-start.14) | collective-permute-done | bytes 393248 | tf_op jit(solution)/shard_map/ppermute | solution.py:28
  92.9 2.1 %collective-permute-done.15 = f32[3,4,64,128]{3,2,1,0:T(8,128)S(1)} collective-permute-done((f32[3,4,64,128]{3,2,1,0:T(8,128)}, f32[3,4,64,128]{3,2,1,0:T(8,128)S(1)}, u32[]{:S(2)}, u32[]{:S(2)}) %collective-permute-start.15) | collective-permute-done | bytes 393248 | tf_op jit(solution)/shard_map/ppermute | solution.py:28
  95.1 2.0 %collective-permute-start.16 = (f32[4,3,4,64,128]{4,3,2,1,0:T(8,128)S(1)}, f32[4,3,4,64,128]{4,3,2,1,0:T(8,128)S(1)}, u32[]{:S(2)}, u32[]{:S(2)}) collective-permute-start(f32[4,3,4,64,128]{4,3,2,1,0:T(8,128)S(1)} %pad_maximum_fusion.refs_5_), channel_id=1, source_target_pairs={{0,1},{1,0},{2,3},{3,2},{4,5},{5,4},{6,7},{7,6},{8,9},{9,8},{10,11... | collective-permute-start | bytes 4718600 | tf_op jit(solution)/shard_map/ppermute | solution.py:28
  97.2 3.8 %readout_last.2.refs_5_ = bf16[512,2048]{1,0:T(8,128)(2,1)} custom-call(s32[3]{0:T(128)S(1)} %copy-done.5, bf16[512,4096]{1,0:T(8,128)(2,1)S(1)} %copy-done.1, f32[32,64,512]{2,1,0:T(8,128)S(1)} %readout.1.refs_2_, bf16[18,32,512]{2,1,0:T(8,128)(2,1)S(1)} %bitcast.26, f32[1,2048]{1,0:T(1,128)S(1)} %bitcast.31, f32[4,3,4,64,128]{4,3,2,1,0:T(8,128)S(1)} %pad_maximum_fusion.refs_5_), custom_call_target="tpu_custom_call" | custom-call | flops 3221225472 | bytes 16777216 | tf_op jit(solution)/shard_map/readout_last/pallas_call | solution.py:295
  101.0 3.8 %readout_last.3 = bf16[512,2048]{1,0:T(8,128)(2,1)} custom-call(s32[3]{0:T(128)S(1)} %copy-done.5, bf16[512,4096]{1,0:T(8,128)(2,1)S(1)} %copy-done.1, f32[32,64,512]{2,1,0:T(8,128)S(1)} %readout.1.refs_2_, bf16[18,32,512]{2,1,0:T(8,128)(2,1)S(1)} %bitcast.27, f32[1,2048]{1,0:T(1,128)S(1)} %bitcast.32, ...), custom_call_target="tpu_custom_call", output_to_operand_aliasing={{}: (5, {})} | custom-call | flops 3221225472 | bytes 16777216 | tf_op jit(solution)/shard_map/readout_last/pallas_call | solution.py:295
  (51 shorter events, 7.5 us)
Async XLA Ops:
  0.1 2.2 %copy-start = (bf16[512,4096]{1,0:T(8,128)(2,1)S(1)}, bf16[512,4096]{1,0:T(8,128)(2,1)}, u32[]{:S(2)}) copy-start(bf16[512,4096]{1,0:T(8,128)(2,1)} %k_ref.1) | copy-start | bytes 12582916
  2.3 1.6 %copy-start.2 = (bf16[512,2048]{1,0:T(8,128)(2,1)S(1)}, bf16[512,2048]{1,0:T(8,128)(2,1)}, u32[]{:S(2)}) copy-start(bf16[512,2048]{1,0:T(8,128)(2,1)} %v_ref.1) | copy-start | bytes 6291460
  3.9 5.5 %copy-start.4 = (s32[3]{0:T(128)}, s32[3]{0:T(128)S(1)}, u32[]{:S(2)}) copy-start(s32[3]{0:T(128)S(1)} %pad_add_fusion.place_ref.refs_0_) | copy-start | bytes 40
  6.0 5.5 %collective-permute-start = (f32[16,64,128]{2,1,0:T(8,128)S(1)}, f32[16,64,128]{2,1,0:T(8,128)S(1)}, u32[]{:S(2)}, u32[]{:S(2)}) collective-permute-start(f32[16,64,128]{2,1,0:T(8,128)S(1)} %block_state.2), channel_id=1, source_target_pairs={{0,1},{1,0},{2,3},{3,2},{4,5},{5,4},{6,7},{7,6},{8,9},{9,8},{10,11... | collective-permute-start | bytes 1572872 | tf_op jit(solution)/shard_map/ppermute | solution.py:28
  12.4 14.9 %collective-permute-start.1 = (f32[16,64,128]{2,1,0:T(8,128)S(1)}, f32[16,64,128]{2,1,0:T(8,128)S(1)}, u32[]{:S(2)}, u32[]{:S(2)}) collective-permute-start(f32[16,64,128]{2,1,0:T(8,128)S(1)} %block_state.3), channel_id=1, source_target_pairs={{0,1},{1,0},{2,3},{3,2},{4,5},{5,4},{6,7},{7,6},{8,9},{9,8},{10,11... | collective-permute-start | bytes 1572872 | tf_op jit(solution)/shard_map/ppermute | solution.py:28
  12.4 14.9 %all-to-all-start = ((f32[4,4,64,128]{3,2,1,0:T(8,128)}), f32[4,4,64,128]{3,2,1,0:T(8,128)S(1)}, u32[]{:S(2)}, u32[]{:S(2)}) async-start(f32[4,4,64,128]{3,2,1,0:T(8,128)} %bitcast.3), calls=%async_computation | async-start | bytes 1048576 | tf_op jit(solution)/shard_map/all_to_all | solution.py:322
  27.3 4.7 %collective-permute-start.5 = (f32[4,64,128]{2,1,0:T(8,128)S(1)}, f32[4,64,128]{2,1,0:T(8,128)S(1)}, u32[]{:S(2)}, u32[]{:S(2)}) collective-permute-start(f32[4,64,128]{2,1,0:T(8,128)S(1)} %add_bitcast_fusion.1), channel_id=1, source_target_pairs={{0,8},{8,0},{16,24},{24,16},{32,40},{40,32},{48,56},{56,48},{1,9},... | collective-permute-start | bytes 393224 | tf_op jit(solution)/shard_map/ppermute | solution.py:28
  27.8 17.7 %collective-permute-start.2 = (f32[16,64,128]{2,1,0:T(8,128)}, f32[16,64,128]{2,1,0:T(8,128)S(1)}, u32[]{:S(2)}, u32[]{:S(2)}) collective-permute-start(f32[16,64,128]{2,1,0:T(8,128)} %add.44), channel_id=1, source_target_pairs={{0,2},{2,0},{4,6},{6,4},{1,3},{3,1},{5,7},{7,5},{8,10},{10,8},{12,... | collective-permute-start | bytes 1572872 | tf_op jit(solution)/shard_map/ppermute | solution.py:28
  32.0 8.7 %collective-permute-start.6 = (f32[4,64,128]{2,1,0:T(8,128)S(1)}, f32[4,64,128]{2,1,0:T(8,128)S(1)}, u32[]{:S(2)}, u32[]{:S(2)}) collective-permute-start(f32[4,64,128]{2,1,0:T(8,128)S(1)} %fusion), channel_id=1, source_target_pairs={{0,16},{8,24},{16,0},{24,8},{32,48},{40,56},{48,32},{56,40},{1,17}... | collective-permute-start | bytes 393224 | tf_op jit(solution)/shard_map/ppermute | solution.py:28
  41.8 30.1 %all-to-all-start.1 = ((f32[4,2,4,64,128]{4,3,2,1,0:T(8,128)}), f32[4,2,4,64,128]{4,3,2,1,0:T(8,128)S(1)}, u32[]{:S(2)}, u32[]{:S(2)}) async-start(f32[4,2,4,64,128]{4,3,2,1,0:T(8,128)} %broadcast_in_dim.2), calls=%async_computation.1 | async-start | bytes 2097152 | tf_op jit(solution)/shard_map/all_to_all | solution.py:322
  45.5 32.6 %copy-start.3 = (bf16[512,18,32]{0,2,1:T(8,128)(2,1)S(1)}, bf16[512,18,32]{0,2,1:T(8,128)(2,1)}, u32[]{:S(2)}) copy-start(bf16[512,18,32]{0,2,1:T(8,128)(2,1)} %param.8) | copy-start | bytes 1769476
  45.5 32.6 %copy-start.5 = (s32[3]{0:T(128)S(1)}, s32[3]{0:T(128)}, u32[]{:S(2)}) copy-start(s32[3]{0:T(128)} %copy-done.4) | copy-start | bytes 40
  46.7 23.4 %collective-permute-start.4 = (f32[16,64,128]{2,1,0:T(8,128)S(1)}, f32[16,64,128]{2,1,0:T(8,128)S(1)}, u32[]{:S(2)}, u32[]{:S(2)}) collective-permute-start(f32[16,64,128]{2,1,0:T(8,128)S(1)} %add.45), channel_id=1, source_target_pairs={{0,6},{2,4},{4,2},{6,0},{1,7},{3,5},{5,3},{7,1},{8,14},{10,12},{12... | collective-permute-start | bytes 1572872 | tf_op jit(solution)/shard_map/ppermute | solution.py:28
  49.5 20.7 %collective-permute-start.3 = (f32[4,1,4,64,128]{4,3,2,1,0:T(8,128)S(1)}, f32[4,1,4,64,128]{4,3,2,1,0:T(8,128)S(1)}, u32[]{:S(2)}, u32[]{:S(2)}) collective-permute-start(f32[4,1,4,64,128]{4,3,2,1,0:T(8,128)S(1)} %bitcast.29), channel_id=1, source_target_pairs={{0,1},{1,0},{2,3},{3,2},{4,5},{5,4},{6,7},{7,6},{8,9},{9,8},{10,11... | collective-permute-start | bytes 1572872 | tf_op jit(solution)/shard_map/ppermute | solution.py:28
  51.5 9.1 %collective-permute-start.7 = (f32[4,64,128]{2,1,0:T(8,128)S(1)}, f32[4,64,128]{2,1,0:T(8,128)S(1)}, u32[]{:S(2)}, u32[]{:S(2)}) collective-permute-start(f32[4,64,128]{2,1,0:T(8,128)S(1)} %add.51), channel_id=1, source_target_pairs={{0,32},{8,40},{16,48},{24,56},{32,0},{40,8},{48,16},{56,24},{1,33}... | collective-permute-start | bytes 393224 | tf_op jit(solution)/shard_map/ppermute | solution.py:28
  60.7 7.2 %collective-permute-start.10 = (f32[4,64,128]{2,1,0:T(8,128)S(1)}, f32[4,64,128]{2,1,0:T(8,128)S(1)}, u32[]{:S(2)}, u32[]{:S(2)}) collective-permute-start(f32[4,64,128]{2,1,0:T(8,128)S(1)} %add.52), channel_id=1, source_target_pairs={{0,192},{64,128},{128,64},{192,0},{1,193},{65,129},{129,65},{193,1... | collective-permute-start | bytes 393224 | tf_op jit(solution)/shard_map/ppermute | solution.py:28
  63.6 5.4 %collective-permute-start.9 = (f32[4,64,128]{2,1,0:T(8,128)S(1)}, f32[4,64,128]{2,1,0:T(8,128)S(1)}, u32[]{:S(2)}, u32[]{:S(2)}) collective-permute-start(f32[4,64,128]{2,1,0:T(8,128)S(1)} %add.52), channel_id=1, source_target_pairs={{0,128},{64,192},{128,0},{192,64},{1,129},{65,193},{129,1},{193,65... | collective-permute-start | bytes 393224 | tf_op jit(solution)/shard_map/ppermute | solution.py:28
  64.0 5.1 %collective-permute-start.8 = (f32[4,64,128]{2,1,0:T(8,128)S(1)}, f32[4,64,128]{2,1,0:T(8,128)S(1)}, u32[]{:S(2)}, u32[]{:S(2)}) collective-permute-start(f32[4,64,128]{2,1,0:T(8,128)S(1)} %add.52), channel_id=1, source_target_pairs={{0,64},{64,0},{128,192},{192,128},{1,65},{65,1},{129,193},{193,129... | collective-permute-start | bytes 393224 | tf_op jit(solution)/shard_map/ppermute | solution.py:28
  70.2 1.0 copy-start.6
  70.2 0.8 copy-start.8
  71.9 6.2 %collective-permute-start.12 = (f32[4,2,4,64,128]{4,3,2,1,0:T(8,128)S(1)}, f32[4,2,4,64,128]{4,3,2,1,0:T(8,128)S(1)}, u32[]{:S(2)}, u32[]{:S(2)}) collective-permute-start(f32[4,2,4,64,128]{4,3,2,1,0:T(8,128)S(1)} %all-to-all-done.1.refs_10_), channel_id=1, source_target_pairs={{0,1},{1,0},{2,3},{3,2},{4,5},{5,4},{6,7},{7,6},{8,9},{9,8},{10,11... | collective-permute-start | bytes 3145736 | tf_op jit(solution)/shard_map/ppermute | solution.py:28
  74.3 3.9 %collective-permute-start.11 = (f32[4,1,4,64,128]{4,3,2,1,0:T(8,128)}, f32[4,1,4,64,128]{4,3,2,1,0:T(8,128)S(1)}, u32[]{:S(2)}, u32[]{:S(2)}) collective-permute-start(f32[4,1,4,64,128]{4,3,2,1,0:T(8,128)} %bitcast.34), channel_id=1, source_target_pairs={{0,1},{1,0},{2,3},{3,2},{4,5},{5,4},{6,7},{7,6},{8,9},{9,8},{10,11... | collective-permute-start | bytes 1572872 | tf_op jit(solution)/shard_map/ppermute | solution.py:28
  74.3 15.7 %collective-permute-start.13 = (f32[3,4,64,128]{3,2,1,0:T(8,128)}, f32[3,4,64,128]{3,2,1,0:T(8,128)S(1)}, u32[]{:S(2)}, u32[]{:S(2)}) collective-permute-start(f32[3,4,64,128]{3,2,1,0:T(8,128)} %pad_maximum_fusion.1), channel_id=1, source_target_pairs={{0,2},{2,0},{4,6},{6,4},{1,3},{3,1},{5,7},{7,5},{8,10},{10,8},{12,... | collective-permute-start | bytes 1179656 | tf_op jit(solution)/shard_map/ppermute | solution.py:28
  74.3 18.6 %collective-permute-start.14 = (f32[3,4,64,128]{3,2,1,0:T(8,128)}, f32[3,4,64,128]{3,2,1,0:T(8,128)S(1)}, u32[]{:S(2)}, u32[]{:S(2)}) collective-permute-start(f32[3,4,64,128]{3,2,1,0:T(8,128)} %pad_maximum_fusion.1), channel_id=1, source_target_pairs={{0,4},{2,6},{4,0},{6,2},{1,5},{3,7},{5,1},{7,3},{8,12},{10,14},{12... | collective-permute-start | bytes 1179656 | tf_op jit(solution)/shard_map/ppermute | solution.py:28
  75.5 19.5 %collective-permute-start.15 = (f32[3,4,64,128]{3,2,1,0:T(8,128)}, f32[3,4,64,128]{3,2,1,0:T(8,128)S(1)}, u32[]{:S(2)}, u32[]{:S(2)}) collective-permute-start(f32[3,4,64,128]{3,2,1,0:T(8,128)} %pad_maximum_fusion.1), channel_id=1, source_target_pairs={{0,6},{2,4},{4,2},{6,0},{1,7},{3,5},{5,3},{7,1},{8,14},{10,12},{12... | collective-permute-start | bytes 1179656 | tf_op jit(solution)/shard_map/ppermute | solution.py:28
  78.2 2.2 %copy-start.1 = (bf16[512,4096]{1,0:T(8,128)(2,1)S(1)}, bf16[512,4096]{1,0:T(8,128)(2,1)}, u32[]{:S(2)}) copy-start(bf16[512,4096]{1,0:T(8,128)(2,1)} %refs_1_.5) | copy-start | bytes 12582916
  80.4 1.0 copy-start.7
  81.4 1.0 copy-start.9
  82.5 1.6 %copy-start.10 = (bf16[32,64,512]{2,1,0:T(8,128)(2,1)S(1)}, bf16[32,64,512]{2,1,0:T(8,128)(2,1)}, u32[]{:S(2)}) copy-start(bf16[32,64,512]{2,1,0:T(8,128)(2,1)} %local_attention.1.refs_2_) | copy-start | bytes 6291460
  84.1 10.9 %copy-start.11 = (f32[3,4,64,128]{3,2,1,0:T(8,128)S(1)}, f32[3,4,64,128]{3,2,1,0:T(8,128)}, u32[]{:S(2)}) copy-start(f32[3,4,64,128]{3,2,1,0:T(8,128)} %pad_maximum_fusion.1) | copy-start | bytes 1179652
  94.9 2.2 %copy-start.12 = (bf16[2048]{0:T(1024)(128)(2,1)S(1)}, bf16[2048]{0:T(1024)(128)(2,1)}, u32[]{:S(2)}) copy-start(bf16[2048]{0:T(1024)(128)(2,1)} %param.9) | copy-start | bytes 12292
  95.1 5.9 %collective-permute-start.16 = (f32[4,3,4,64,128]{4,3,2,1,0:T(8,128)S(1)}, f32[4,3,4,64,128]{4,3,2,1,0:T(8,128)S(1)}, u32[]{:S(2)}, u32[]{:S(2)}) collective-permute-start(f32[4,3,4,64,128]{4,3,2,1,0:T(8,128)S(1)} %pad_maximum_fusion.refs_5_), channel_id=1, source_target_pairs={{0,1},{1,0},{2,3},{3,2},{4,5},{5,4},{6,7},{7,6},{8,9},{9,8},{10,11... | collective-permute-start | bytes 4718600 | tf_op jit(solution)/shard_map/ppermute | solution.py:28
